TPU v7x, 32 devices: a whole 2x2x4 slice. The times are simulated.
32 devices in a mesh: dp: 32 (over z, y, x, core).
Axes of the slice: x: 2, y: 2, z: 4, core: 2. Of those that a mesh axis runs over, the one named last changes fastest.
Arguments:
- tokens: bfloat16 [32768, 768], P('dp'), may hold values from -6 to 6
- segment_ids: int32 [32768], P('dp'), may hold values from 0 to 10, as said below
- random_blocks: int32 [12, 6, 3], replicated, may hold values from 1 to 6, as said below
- clip_limit: int32 [1], replicated, may hold values from 6 to 12
- query_weight: bfloat16 [768, 768], P('dp'), may hold values from -1 to 1
- query_bias: bfloat16 [768], P('dp'), may hold values from -1 to 1
- key_weight: bfloat16 [768, 768], P('dp'), may hold values from -0.21875 to 0.21875
- value_weight: bfloat16 [768, 768], P('dp'), may hold values from -0.21875 to 0.21875
- value_bias: bfloat16 [768], P('dp'), may hold values from -1 to 1
- output_weight: bfloat16 [768, 768], P('dp'), may hold values from -1.25 to 1.25
- output_bias: bfloat16 [768], P('dp'), may hold values from -1 to 1
- attn_gain: bfloat16 [768], P('dp'), may hold values from 0.5 to 1.5
- attn_shift: bfloat16 [768], P('dp'), may hold values from -1 to 1
- inner_weight: bfloat16 [768, 3072], P('dp'), may hold values from -0.21875 to 0.21875
- inner_bias: bfloat16 [3072], P('dp'), may hold values from -1 to 1
- outer_weight: bfloat16 [3072, 768], P('dp'), may hold values from -0.15625 to 0.15625
- outer_bias: bfloat16 [768], P('dp'), may hold values from -1 to 1
- final_gain: bfloat16 [768], P('dp'), may hold values from 0.5 to 1.5
- final_shift: bfloat16 [768], P('dp'), may hold values from -1 to 1
- out_cotangent: bfloat16 [32768, 768], P('dp'), may hold values from -6 to 6
Outputs:
- layer_out: bfloat16 [32768, 768], P('dp')
- token_gradient: float32 [32768, 768], P('dp')
- query_weight_gradient: float32 [768, 768], P('dp')
- query_bias_gradient: float32 [768], P('dp')
- key_weight_gradient: float32 [768, 768], P('dp')
- value_weight_gradient: float32 [768, 768], P('dp')
- value_bias_gradient: float32 [768], P('dp')
- output_weight_gradient: float32 [768, 768], P('dp')
- output_bias_gradient: float32 [768], P('dp')
- attn_gain_gradient: float32 [768], P('dp')
- attn_shift_gradient: float32 [768], P('dp')
- inner_weight_gradient: float32 [768, 3072], P('dp')
- inner_bias_gradient: float32 [3072], P('dp')
- outer_weight_gradient: float32 [3072, 768], P('dp')
- outer_bias_gradient: float32 [768], P('dp')
- final_gain_gradient: float32 [768], P('dp')
- final_shift_gradient: float32 [768], P('dp')
- clipped_query: bfloat16 [768, 768], P('dp')
- clipped_key: bfloat16 [768, 768], P('dp')
- head_maxima: float32 [12], replicated
Inputs may be any that keep to these rules, and one draw needn't show every extreme that they name: `segment_ids`: within each sequence of 512 tokens the numbers never fall up to a final run of 1 to 128 tokens with number 0; every other number covers 60 to 480 consecutive tokens, except the last one before the final run, which may be shorter and always has the number 512 // 60 + 2; consecutive documents have consecutive numbers. `random_blocks`: row i - 1 of a head lists 3 different blocks for middle query block i, none of them 0, 7, i - 1, i or i + 1.
All inputs are finite; a program needn't handle non-finite values.
Results may differ from a plain program's by a relative error of at most 0.015.
The roundings to bfloat16 on the way count: a program that leaves them out, or rounds other values in their place, can miss the bound.
Values may be sent and summed in bfloat16 or wider, within the bound.
A program may use at most 384 MiB of HBM per device.

v0:
```python
from functools import partial
import math

import jax
import jax.numpy as jnp
from jax import lax
from jax.sharding import PartitionSpec as P

H = 12
HD = 64
BLOCK = 64
SEQ = 512
MICRO = 2


def add_pair(left_term, right_term):
    return left_term + right_term


def normalize_rows(summed_rows, gain_vec, shift_vec):
    row_mean = jnp.mean(summed_rows, axis=-1, keepdims=True)
    centered = summed_rows - row_mean
    row_var = jnp.mean(centered * centered, axis=-1, keepdims=True)
    inverse = lax.rsqrt(row_var + 1e-12)
    unit_rows = centered * inverse
    return (unit_rows * gain_vec + shift_vec, unit_rows, inverse)


def normalize_back(upstream, unit_rows, inverse, gain_vec):
    scaled = upstream * gain_vec
    spread = jnp.mean(scaled, axis=-1, keepdims=True)
    along = jnp.mean(scaled * unit_rows, axis=-1, keepdims=True)
    return inverse * (scaled - spread - unit_rows * along)


def block_tables(random_blocks, block_total):
    head_count = random_blocks.shape[0]
    middle = jnp.arange(1, block_total - 1, dtype=jnp.int32)
    zero_ids = jnp.zeros_like(middle)
    fixed_ids = jnp.stack(
        [middle - 1, middle, middle + 1, zero_ids, zero_ids + (block_total - 1)], axis=-1
    )
    block_index = jnp.concatenate(
        [jnp.broadcast_to(fixed_ids[None], (head_count, block_total - 2, 5)), random_blocks],
        axis=-1,
    )
    no_flags = jnp.zeros(middle.shape, dtype=bool)
    repeated = jnp.stack(
        [middle == 1, no_flags, middle == block_total - 2, no_flags, no_flags], axis=-1
    )
    extra_flags = jnp.zeros(random_blocks.shape, dtype=bool)
    keep_slots = jnp.logical_not(
        jnp.concatenate(
            [jnp.broadcast_to(repeated[None], (head_count, block_total - 2, 5)), extra_flags],
            axis=-1,
        )
    )
    onehot = (block_index[..., None] == jnp.arange(block_total, dtype=jnp.int32)).astype(
        jnp.float32
    )
    return (block_index, keep_slots, onehot)


def gather_blocks(array_rows, block_index, block_shape):
    by_head = jnp.transpose(array_rows.reshape(block_shape), (0, 3, 1, 2, 4))
    head_ids = jnp.arange(block_shape[3])[:, None, None]
    return by_head[:, head_ids, block_index]


def region_scores(queries, key_rows, seg_rows, block_index, keep_slots, block_shape):
    seq_count, block_total, block_len, head_count, head_width = block_shape
    logit_scale = 1.0 / math.sqrt(head_width)
    query_blocks = queries.reshape(block_shape)
    key_flat = key_rows.reshape(seq_count, block_total * block_len, head_count, head_width)
    key_gathered = gather_blocks(key_rows, block_index, block_shape)
    seg_blocks = seg_rows.reshape(seq_count, block_total, block_len)
    seg_flat = seg_rows.reshape(seq_count, block_total * block_len)
    seg_gathered = seg_blocks[:, block_index]
    query_mid = query_blocks[:, 1:-1]
    query_edge = jnp.concatenate([query_blocks[:, :1], query_blocks[:, -1:]], axis=1)
    seg_mid = seg_blocks[:, 1:-1]
    seg_edge = jnp.concatenate([seg_blocks[:, :1], seg_blocks[:, -1:]], axis=1)
    score_mid = (
        jnp.einsum(
            "sibhd,shijcd->shibjc", query_mid, key_gathered, preferred_element_type=jnp.float32
        )
        * logit_scale
    )
    allow_mid = (
        keep_slots[None, :, :, None, :, None]
        & (seg_mid[:, None, :, :, None, None] == seg_gathered[:, :, :, None, :, :])
        & (seg_gathered != 0)[:, :, :, None, :, :]
    )
    score_edge = (
        jnp.einsum("sgbhd,skhd->shgbk", query_edge, key_flat, preferred_element_type=jnp.float32)
        * logit_scale
    )
    allow_edge = (seg_edge[:, None, :, :, None] == seg_flat[:, None, None, None, :]) & (
        seg_flat != 0
    )[:, None, None, None, :]
    return (
        score_mid,
        allow_mid,
        score_edge,
        allow_edge,
        query_mid,
        query_edge,
        key_gathered,
        key_flat,
    )


def softmax_parts(scores, allowed, axes):
    masked = jnp.where(allowed, scores, -1e30)
    row_top = jnp.max(masked, axis=axes, keepdims=True)
    row_live = jnp.any(allowed, axis=axes, keepdims=True)
    row_base = jnp.where(row_live, row_top, 0.0)
    weights = jnp.exp(jnp.where(allowed, scores - row_base, -1e30))
    row_total = jnp.sum(weights, axis=axes, keepdims=True) + jnp.where(row_live, 0.0, 1.0)
    return (weights / row_total, row_base, row_total, jnp.where(row_live, row_top, -1e30))


def recompute_probs(scores, allowed, row_base, row_total):
    return jnp.exp(jnp.where(allowed, scores - row_base, -1e30)) / row_total


def attention_forward(queries, key_rows, values, seg_rows, tables, block_shape):
    block_index, keep_slots, onehot = tables
    seq_count, block_total, block_len, head_count, head_width = block_shape
    score_mid, allow_mid, score_edge, allow_edge, query_mid, query_edge, key_gathered, key_flat = (
        region_scores(queries, key_rows, seg_rows, block_index, keep_slots, block_shape)
    )
    probs_mid, base_mid, total_mid, top_mid = softmax_parts(score_mid, allow_mid, (4, 5))
    probs_edge, base_edge, total_edge, top_edge = softmax_parts(score_edge, allow_edge, (4,))
    value_gathered = gather_blocks(values, block_index, block_shape)
    value_flat = values.reshape(seq_count, block_total * block_len, head_count, head_width)
    context_mid = jnp.einsum(
        "shibjc,shijcd->sibhd",
        probs_mid.astype(jnp.bfloat16),
        value_gathered,
        preferred_element_type=jnp.float32,
    )
    context_edge = jnp.einsum(
        "shgbk,skhd->sgbhd",
        probs_edge.astype(jnp.bfloat16),
        value_flat,
        preferred_element_type=jnp.float32,
    )
    context = jnp.concatenate([context_edge[:, :1], context_mid, context_edge[:, 1:]], axis=1)
    context = context.reshape(seq_count * block_total * block_len, head_count * head_width).astype(
        jnp.bfloat16
    )
    head_top = jnp.maximum(
        jnp.max(top_mid, axis=(0, 2, 3, 4, 5)), jnp.max(top_edge, axis=(0, 2, 3, 4))
    )
    return (context, (base_mid, total_mid, base_edge, total_edge), head_top)


def attention_backward(
    queries, key_rows, values, seg_rows, tables, stats, delta_context, block_shape
):
    block_index, keep_slots, onehot = tables
    base_mid, total_mid, base_edge, total_edge = stats
    seq_count, block_total, block_len, head_count, head_width = block_shape
    logit_scale = 1.0 / math.sqrt(head_width)
    row_count = seq_count * block_total * block_len
    score_mid, allow_mid, score_edge, allow_edge, query_mid, query_edge, key_gathered, key_flat = (
        region_scores(queries, key_rows, seg_rows, block_index, keep_slots, block_shape)
    )
    probs_mid = recompute_probs(score_mid, allow_mid, base_mid, total_mid)
    probs_edge = recompute_probs(score_edge, allow_edge, base_edge, total_edge)
    value_gathered = gather_blocks(values, block_index, block_shape)
    value_flat = values.reshape(seq_count, block_total * block_len, head_count, head_width)
    delta_blocks = delta_context.reshape(block_shape)
    delta_mid = delta_blocks[:, 1:-1]
    delta_edge = jnp.concatenate([delta_blocks[:, :1], delta_blocks[:, -1:]], axis=1)
    slope_mid = jnp.einsum(
        "sibhd,shijcd->shibjc", delta_mid, value_gathered, preferred_element_type=jnp.float32
    )
    score_slope_mid = (
        probs_mid * (slope_mid - jnp.sum(probs_mid * slope_mid, axis=(4, 5), keepdims=True))
    ).astype(jnp.bfloat16)
    slope_edge = jnp.einsum(
        "sgbhd,skhd->shgbk", delta_edge, value_flat, preferred_element_type=jnp.float32
    )
    score_slope_edge = (
        probs_edge * (slope_edge - jnp.sum(probs_edge * slope_edge, axis=4, keepdims=True))
    ).astype(jnp.bfloat16)
    query_slope_mid = (
        jnp.einsum(
            "shibjc,shijcd->sibhd",
            score_slope_mid,
            key_gathered,
            preferred_element_type=jnp.float32,
        )
        * logit_scale
    )
    query_slope_edge = (
        jnp.einsum(
            "shgbk,skhd->sgbhd", score_slope_edge, key_flat, preferred_element_type=jnp.float32
        )
        * logit_scale
    )
    delta_queries = jnp.concatenate(
        [query_slope_edge[:, :1], query_slope_mid, query_slope_edge[:, 1:]], axis=1
    )
    delta_queries = delta_queries.reshape(row_count, head_count * head_width).astype(jnp.bfloat16)
    key_slope_gathered = (
        jnp.einsum(
            "shibjc,sibhd->shijcd", score_slope_mid, query_mid, preferred_element_type=jnp.float32
        )
        * logit_scale
    )
    value_slope_gathered = jnp.einsum(
        "shibjc,sibhd->shijcd",
        probs_mid.astype(jnp.bfloat16),
        delta_mid,
        preferred_element_type=jnp.float32,
    )
    key_slope_blocks = jnp.einsum(
        "shijcd,hijn->snchd",
        key_slope_gathered,
        onehot,
        precision=lax.Precision.HIGHEST,
        preferred_element_type=jnp.float32,
    )
    value_slope_blocks = jnp.einsum(
        "shijcd,hijn->snchd",
        value_slope_gathered,
        onehot,
        precision=lax.Precision.HIGHEST,
        preferred_element_type=jnp.float32,
    )
    key_slope_edge = (
        jnp.einsum(
            "shgbk,sgbhd->skhd", score_slope_edge, query_edge, preferred_element_type=jnp.float32
        )
        * logit_scale
    )
    value_slope_edge = jnp.einsum(
        "shgbk,sgbhd->skhd",
        probs_edge.astype(jnp.bfloat16),
        delta_edge,
        preferred_element_type=jnp.float32,
    )
    full_width = head_count * head_width
    delta_keys = (
        key_slope_blocks.reshape(row_count, full_width)
        + key_slope_edge.reshape(row_count, full_width)
    ).astype(jnp.bfloat16)
    delta_values = (
        value_slope_blocks.reshape(row_count, full_width)
        + value_slope_edge.reshape(row_count, full_width)
    ).astype(jnp.bfloat16)
    return (delta_queries, delta_keys, delta_values)


def per_device(
    tokens,
    segment_ids,
    random_blocks,
    clip_limit,
    query_weight,
    query_bias,
    key_weight,
    value_weight,
    value_bias,
    output_weight,
    output_bias,
    attn_gain,
    attn_shift,
    inner_weight,
    inner_bias,
    outer_weight,
    outer_bias,
    final_gain,
    final_shift,
    out_cotangent,
):
    shards = (
        query_weight,
        query_bias,
        key_weight,
        value_weight,
        value_bias,
        output_weight,
        output_bias,
        attn_gain,
        attn_shift,
        inner_weight,
        inner_bias,
        outer_weight,
        outer_bias,
        final_gain,
        final_shift,
    )
    block_total = SEQ // BLOCK
    batch_len = tokens.shape[0] // MICRO
    block_shape = (batch_len // SEQ, block_total, BLOCK, H, HD)
    tables = block_tables(random_blocks, block_total)
    running_top = jnp.full((H,), -1e30, dtype=jnp.float32)
    outputs = []
    token_grads = []
    for batch_index in range(MICRO):
        whole_set = (
            lax.all_gather(shards[0], "dp", axis=0, tiled=True),
            lax.all_gather(shards[1], "dp", axis=0, tiled=True),
            lax.all_gather(shards[2], "dp", axis=0, tiled=True),
            lax.all_gather(shards[3], "dp", axis=0, tiled=True),
            lax.all_gather(shards[4], "dp", axis=0, tiled=True),
            lax.all_gather(shards[5], "dp", axis=0, tiled=True),
            lax.all_gather(shards[6], "dp", axis=0, tiled=True),
            lax.all_gather(shards[7], "dp", axis=0, tiled=True),
            lax.all_gather(shards[8], "dp", axis=0, tiled=True),
            lax.all_gather(shards[9], "dp", axis=0, tiled=True),
            lax.all_gather(shards[10], "dp", axis=0, tiled=True),
            lax.all_gather(shards[11], "dp", axis=0, tiled=True),
            lax.all_gather(shards[12], "dp", axis=0, tiled=True),
            lax.all_gather(shards[13], "dp", axis=0, tiled=True),
            lax.all_gather(shards[14], "dp", axis=0, tiled=True),
        )
        (
            query_full,
            query_lift,
            key_full,
            value_full,
            value_lift,
            output_full,
            output_lift,
            attn_scale,
            attn_offset,
            inner_full,
            inner_lift,
            outer_full,
            outer_lift,
            final_scale,
            final_offset,
        ) = whole_set
        batch_start = batch_index * batch_len
        batch_rows = tokens[batch_start : batch_start + batch_len]
        batch_segs = segment_ids[batch_start : batch_start + batch_len]
        queries = (
            jnp.dot(batch_rows, query_full, preferred_element_type=jnp.float32) + query_lift
        ).astype(jnp.bfloat16)
        key_rows = jnp.dot(batch_rows, key_full, preferred_element_type=jnp.float32).astype(
            jnp.bfloat16
        )
        values = (
            jnp.dot(batch_rows, value_full, preferred_element_type=jnp.float32) + value_lift
        ).astype(jnp.bfloat16)
        context, stats, batch_top = attention_forward(
            queries, key_rows, values, batch_segs, tables, block_shape
        )
        running_top = jnp.maximum(running_top, batch_top)
        branch = jnp.dot(context, output_full, preferred_element_type=jnp.float32) + output_lift
        first_norm, unit_first, inverse_first = normalize_rows(
            batch_rows.astype(jnp.float32) + branch, attn_scale, attn_offset
        )
        first_low = first_norm.astype(jnp.bfloat16)
        inner = jnp.dot(first_low, inner_full, preferred_element_type=jnp.float32) + inner_lift
        active = jax.nn.gelu(inner, approximate=True).astype(jnp.bfloat16)
        outer = jnp.dot(active, outer_full, preferred_element_type=jnp.float32) + outer_lift
        final_norm, unit_final, inverse_final = normalize_rows(
            first_norm + outer, final_scale, final_offset
        )
        outputs.append(final_norm.astype(jnp.bfloat16))
        again_set = (
            lax.all_gather(query_weight, "dp", axis=0, tiled=True),
            lax.all_gather(key_weight, "dp", axis=0, tiled=True),
            lax.all_gather(value_weight, "dp", axis=0, tiled=True),
            lax.all_gather(output_weight, "dp", axis=0, tiled=True),
            lax.all_gather(attn_gain, "dp", axis=0, tiled=True),
            lax.all_gather(inner_weight, "dp", axis=0, tiled=True),
            lax.all_gather(outer_weight, "dp", axis=0, tiled=True),
            lax.all_gather(final_gain, "dp", axis=0, tiled=True),
        )
        (
            query_again,
            key_again,
            value_again,
            output_again,
            attn_again,
            inner_again,
            outer_again,
            final_again,
        ) = again_set
        upstream = out_cotangent[batch_start : batch_start + batch_len].astype(jnp.float32)
        final_gain_part = jnp.sum(upstream * unit_final, axis=0)
        final_shift_part = jnp.sum(upstream, axis=0)
        delta_second = normalize_back(upstream, unit_final, inverse_final, final_again)
        delta_outer = delta_second.astype(jnp.bfloat16)
        outer_bias_part = jnp.sum(delta_outer, axis=0, dtype=jnp.float32)
        outer_weight_part = jnp.dot(active.T, delta_outer, preferred_element_type=jnp.float32)
        gelu_value, gelu_back = jax.vjp(partial(jax.nn.gelu, approximate=True), inner)
        delta_inner = gelu_back(
            jnp.dot(delta_outer, outer_again.T, preferred_element_type=jnp.float32)
        )[0].astype(jnp.bfloat16)
        inner_bias_part = jnp.sum(delta_inner, axis=0, dtype=jnp.float32)
        inner_weight_part = jnp.dot(first_low.T, delta_inner, preferred_element_type=jnp.float32)
        delta_first = delta_second + jnp.dot(
            delta_inner, inner_again.T, preferred_element_type=jnp.float32
        )
        attn_gain_part = jnp.sum(delta_first * unit_first, axis=0)
        attn_shift_part = jnp.sum(delta_first, axis=0)
        delta_sum = normalize_back(delta_first, unit_first, inverse_first, attn_again)
        delta_branch = delta_sum.astype(jnp.bfloat16)
        output_bias_part = jnp.sum(delta_branch, axis=0, dtype=jnp.float32)
        output_weight_part = jnp.dot(context.T, delta_branch, preferred_element_type=jnp.float32)
        delta_context = jnp.dot(
            delta_branch, output_again.T, preferred_element_type=jnp.float32
        ).astype(jnp.bfloat16)
        delta_queries, delta_keys, delta_values = attention_backward(
            queries, key_rows, values, batch_segs, tables, stats, delta_context, block_shape
        )
        query_bias_part = jnp.sum(delta_queries, axis=0, dtype=jnp.float32)
        query_weight_part = jnp.dot(batch_rows.T, delta_queries, preferred_element_type=jnp.float32)
        key_weight_part = jnp.dot(batch_rows.T, delta_keys, preferred_element_type=jnp.float32)
        value_weight_part = jnp.dot(batch_rows.T, delta_values, preferred_element_type=jnp.float32)
        value_bias_part = jnp.sum(delta_values, axis=0, dtype=jnp.float32)
        input_slope = delta_sum + jnp.dot(
            delta_queries, query_again.T, preferred_element_type=jnp.float32
        )
        input_slope = input_slope + jnp.dot(
            delta_keys, key_again.T, preferred_element_type=jnp.float32
        )
        input_slope = input_slope + jnp.dot(
            delta_values, value_again.T, preferred_element_type=jnp.float32
        )
        token_grads.append(input_slope)
        batch_grads = (
            query_weight_part,
            query_bias_part,
            key_weight_part,
            value_weight_part,
            value_bias_part,
            output_weight_part,
            output_bias_part,
            attn_gain_part,
            attn_shift_part,
            inner_weight_part,
            inner_bias_part,
            outer_weight_part,
            outer_bias_part,
            final_gain_part,
            final_shift_part,
        )
        totals = batch_grads if batch_index == 0 else jax.tree.map(add_pair, totals, batch_grads)
    summed = lax.psum_scatter(totals, "dp", scatter_dimension=0, tiled=True)
    head_maxima = lax.pmax(running_top, "dp")
    limit_value = clip_limit[0].astype(jnp.float32)
    factor = jnp.sqrt(jnp.minimum(1.0, limit_value / jnp.maximum(head_maxima, 1.0)))
    columns = jnp.repeat(factor, HD)[None, :]
    clipped_query = (query_weight.astype(jnp.float32) * columns).astype(jnp.bfloat16)
    clipped_key = (key_weight.astype(jnp.float32) * columns).astype(jnp.bfloat16)
    layer_out = jnp.concatenate(outputs, axis=0)
    token_gradient = jnp.concatenate(token_grads, axis=0)
    return (
        layer_out,
        token_gradient,
        summed[0],
        summed[1],
        summed[2],
        summed[3],
        summed[4],
        summed[5],
        summed[6],
        summed[7],
        summed[8],
        summed[9],
        summed[10],
        summed[11],
        summed[12],
        summed[13],
        summed[14],
        clipped_query,
        clipped_key,
        head_maxima,
    )


def solution(mesh):
    in_specs = (
        P("dp", None),
        P("dp"),
        P(),
        P(),
        P("dp", None),
        P("dp"),
        P("dp", None),
        P("dp", None),
        P("dp"),
        P("dp", None),
        P("dp"),
        P("dp"),
        P("dp"),
        P("dp", None),
        P("dp"),
        P("dp", None),
        P("dp"),
        P("dp"),
        P("dp"),
        P("dp", None),
    )
    out_specs = (
        P("dp", None),
        P("dp", None),
        P("dp", None),
        P("dp"),
        P("dp", None),
        P("dp", None),
        P("dp"),
        P("dp", None),
        P("dp"),
        P("dp"),
        P("dp"),
        P("dp", None),
        P("dp"),
        P("dp", None),
        P("dp"),
        P("dp"),
        P("dp"),
        P("dp", None),
        P("dp", None),
        P(),
    )
    return jax.shard_map(
        per_device, mesh=mesh, in_specs=in_specs, out_specs=out_specs, check_vma=False
    )
```

profile of v0, /device:TPU:0, one launch (start us, length us, event | category | flops | bytes accessed | tf_op | source)
XLA Modules:
  0.0 1408.6 jit_solution(16829393562000990184)
XLA Ops:
  21.8 42.3 %all-reduce.20 = (bf16[768]{0:T(1024)(128)(2,1)S(1)}, bf16[768]{0:T(1024)(128)(2,1)S(1)}, bf16[768]{0:T(1024)(128)(2,1)S(1)}, bf16[768]{0:T(1024)(128)(2,1)S(1)}...) all-reduce(bf16[768]{0:T(1024)(128)(2,1)S(1)} %dynamic-update-slice, ...), channel_id=1, replica_groups=mesh['dp'=32] {'dp'}, use_global_device_ids=true, to_apply=%add.1 | all-reduce | flops 9216 | bytes 36864
  74.7 167.3 %and_reduce_fusion.1 = (pred[12,6,64]{2,1,0:T(8,128)(4,1)}, pred[12,6,64]{2,1,0:T(8,128)(4,1)S(1)}) fusion(s32[12,6,8,64]{3,2,1,0:T(8,128)S(1)} %bitcast.410, s32[6,64]{1,0:T(8,128)S(1)} %slice_bitcast_fusion.9, pred[12,6,8,64]{3,2,1,0:T(8,128)(4,1)S(1)} %broadcast_compare_fusion.1, pred[12,6,8]{2,1,0:T(8,128)(4,1)S(1)} %pad_not_fusion, ...), kind=kLoop, calls=%fused_computation.24 | loop fusion | flops 18865152 | bytes 381504 | tf_op jit(solution)/shard_map/reduce_or | solution.py:116
  246.4 2.8 slice.175
  266.3 3.0 slice.180
  272.9 3.8 reshape.1016
  280.7 3.8 reshape.1015
  288.4 10.2 gather_fusion.2
  298.6 10.1 gather_fusion.5
  308.8 15.8 %select_reduce_fusion.1 = (f32[12,6,64]{2,1,0:T(8,128)S(1)}, f32[12,6,64,8,64]{2,4,3,1,0:T(8,128)S(1)}) fusion(s32[12,6,8,64]{3,2,1,0:T(8,128)S(1)} %bitcast.411, s32[6,64]{1,0:T(8,128)S(1)} %copy-done.124, pred[12,6,8,64]{3,2,1,0:T(8,128)(4,1)S(1)} %copy-done.78, pred[12,6,8]{2,1,0:T(8,128)(4,1)S(1)} %pad_not_fusion, ...), kind=kOutput, calls=%fused_computation.21 | convolution fusion | flops 316141056 | bytes 14950464 | tf_op jit(solution)/shard_map/sibhd,shijcd->shibjc/dot_general | solution.py:84
  325.5 29.9 %fusion.9 = (f32[12,6,64]{2,1,0:T(8,128)S(1)}, f32[12,6,64]{2,1,0:T(8,128)}, f32[12,6,64,8,64]{2,4,3,1,0:T(8,128)}) fusion(f32[12,6,64,8,64]{2,4,3,1,0:T(8,128)S(1)} %get-tuple-element.212, f32[12,6,64]{2,1,0:T(8,128)S(1)} %get-tuple-element.184, s32[12,6,8,64]{3,2,1,0:T(8,128)S(1)} %bitcast.412, s32[6,64]{1,0:T(8,128)S(1)} %copy-done.124, ...), kind=kOutput, calls=%fused_computation.27 | convolution fusion | flops 332651520 | bytes 24610368 | tf_op jit(solution)/shard_map/sibhd,shijcd->shibjc/dot_general | solution.py:84
  356.4 9.9 gather_fusion
  375.0 27.4 %fusion.184 = (bf16[12,6,64,8,64]{2,4,3,1,0:T(8,128)(2,1)}, f32[12,6,64]{2,1,0:T(8,128)}) fusion(f32[12,6,64]{2,1,0:T(8,128)S(1)} %copy-done.95, f32[12,6,64]{2,1,0:T(8,128)S(1)} %copy-done.94, f32[12,6,64,8,64]{2,4,3,1,0:T(8,128)} %copy-done, pred[12,6,8,64]{3,2,1,0:T(8,128)(4,1)S(1)} %copy-done.78, s32[12,6,8,64]{3,2,1,0:T(8,128)S(1)} %bitcast.413, ...), kind=kLoop, calls=%fused_computation.325 | loop fusion | flops 35384832 | bytes 24038976 | tf_op jit(solution)/shard_map/convert_element_type | solution.py:139
  402.4 9.7 fusion.90
  417.5 10.0 gather_fusion.3
  433.0 16.6 %fusion.183 = bf16[12,6,64,8,64]{2,4,3,1,0:T(8,128)(2,1)} fusion(f32[12,6,64]{2,1,0:T(8,128)S(1)} %select_add_fusion, f32[12,6,64]{2,1,0:T(8,128)S(1)} %copy-done.92, f32[12,6,64,8,64]{2,4,3,1,0:T(8,128)} %get-tuple-element.213, pred[12,6,8,64]{3,2,1,0:T(8,128)(4,1)S(1)} %broadcast_compare_fusion, s32[12,6,8,64]{3,2,1,0:T(8,128)S(1)} %bitcast.400, ...), kind=kLoop, calls=%fused_computation.324 | loop fusion | flops 18874368 | bytes 14379072 | tf_op jit(solution)/shard_map/convert_element_type | solution.py:139
  449.6 9.7 fusion.95
  467.0 8.3 fusion.177
  475.3 7.9 fusion.197
  486.4 4.2 fusion.195
  493.3 3.0 convert_reduce_fusion.8
  496.3 7.1 convert_reduce_fusion.1
  503.4 3.6 multiply_reduce_fusion.5
  507.0 8.8 convert_reduce_fusion
  515.9 5.1 convert_reduce_fusion.11
  528.3 2.8 slice.185
  539.1 10.5 fusion.110
  549.6 7.7 fusion.111
  569.1 5.8 fusion.108
  575.0 21.6 %convert_reduce_fusion.3 = (f32[12,64]{1,0:T(8,128)}, f32[1,8,64,12,64]{4,1,2,3,0:T(8,128)}) fusion(f32[1,8,64,12,64]{4,1,2,3,0:T(8,128)} %copy.279, f32[12,6,8,64,64]{4,3,2,1,0:T(8,128)S(1)} %fusion.108, s32[12,6,8]{2,1,0:T(8,128)S(1)} %copy-done.75), kind=kOutput, calls=%fused_computation.73 | convolution fusion | flops 228069120 | bytes 12588288 | tf_op jit(solution)/shard_map/shijcd,hijn->snchd/dot_general | solution.py:227
  596.5 3.7 copy.262
  600.3 3.9 reshape.893
  612.6 3.8 reshape.903
  616.3 3.7 copy.280
  620.0 26.1 %convert_reduce_fusion.2 = (f32[12,64]{1,0:T(8,128)}, f32[1,8,64,12,64]{4,1,2,3,0:T(8,128)}) fusion(f32[1,8,64,12,64]{4,1,2,3,0:T(8,128)} %copy.280, f32[12,6,8,64,64]{4,3,2,1,0:T(8,128)} %fusion.110, s32[12,6,8]{2,1,0:T(8,128)S(1)} %copy-done.75), kind=kOutput, calls=%fused_computation.71 | convolution fusion | flops 228069120 | bytes 12588288 | tf_op jit(solution)/shard_map/shijcd,hijn->snchd/dot_general | solution.py:227
  646.1 3.7 copy.277
  649.9 3.8 reshape.900
  653.7 3.2 fusion.86
  657.0 37.4 %multiply_reduce_fusion.1 = (f32[12,6,64]{2,1,0:T(8,128)}, f32[12,6,64]{2,1,0:T(8,128)}, f32[12,6,64,8,64]{2,4,3,1,0:T(8,128)}) fusion(f32[12,6,64]{2,1,0:T(8,128)} %select_add_fusion.1, f32[12,6,64]{2,1,0:T(8,128)} %copy-done.93, f32[12,6,64,8,64]{2,4,3,1,0:T(8,128)} %copy-done, pred[12,6,8,64]{3,2,1,0:T(8,128)(4,1)} %copy-done.77, ...), kind=kOutput, calls=%fused_computation.17 | convolution fusion | flops 344448000 | bytes 43540032 | tf_op jit(solution)/shard_map/sibhd,shijcd->shibjc/dot_general | solution.py:177
  695.7 29.6 %multiply_convert_fusion.1 = (bf16[12,6,64,8,64]{2,4,3,1,0:T(8,128)(2,1)}, bf16[12,6,64,8,64]{2,4,3,1,0:T(8,128)(2,1)}) fusion(f32[12,6,64,8,64]{2,4,3,1,0:T(8,128)} %get-tuple-element.226, f32[12,6,64]{2,1,0:T(8,128)} %get-tuple-element.124, f32[12,6,64]{2,1,0:T(8,128)} %select_add_fusion.1, f32[12,6,64]{2,1,0:T(8,128)} %copy-done.93, ...), kind=kLoop, calls=%fused_computation.16 | loop fusion | flops 47185920 | bytes 47668800 | tf_op jit(solution)/shard_map/convert_element_type | solution.py:182
  725.3 5.9 broadcast_multiply_fusion.1
  731.2 23.9 %fusion.50 = f32[1,8,64,12,64]{4,1,2,3,0:T(8,128)} fusion(f32[12,6,8,64,64]{4,3,2,1,0:T(8,128)S(1)} %broadcast_multiply_fusion.1, s32[12,6,8]{2,1,0:T(8,128)S(1)} %copy-done.75), kind=kOutput, calls=%fused_computation.110 | convolution fusion | flops 226497024 | bytes 11012352 | tf_op jit(solution)/shard_map/shijcd,hijn->snchd/dot_general | solution.py:220
  755.1 3.3 add_bitcast_fusion
  758.5 3.3 copy.333
  764.1 3.8 reshape.891
  768.0 5.4 broadcast_multiply_fusion
  773.3 22.0 %fusion.56 = f32[1,8,64,12,64]{4,1,2,3,0:T(8,128)S(1)} fusion(f32[12,6,8,64,64]{4,3,2,1,0:T(8,128)S(1)} %broadcast_multiply_fusion, s32[12,6,8]{2,1,0:T(8,128)S(1)} %copy-done.75), kind=kOutput, calls=%fused_computation.112 | convolution fusion | flops 226497024 | bytes 11012352 | tf_op jit(solution)/shard_map/shijcd,hijn->snchd/dot_general | solution.py:220
  797.8 4.3 reshape.898
  802.2 4.1 multiply_reduce_fusion.3
  821.4 3.1 copy.331
  824.4 9.7 fusion.43
  837.7 3.0 copy.256
  840.8 3.5 convert_element_type.302
  844.8 8.5 fusion.42
  862.6 3.1 copy.329
  865.8 6.6 fusion.166
  872.5 10.4 convolution_add_fusion
  883.6 5.4 fusion.175
  889.0 5.7 convolution_add_fusion.1
  895.9 40.5 %pmax.7 = f32[12]{0:T(128)S(1)} all-reduce(f32[12]{0:T(128)S(1)} %maximum_maximum_fusion), channel_id=1, replica_groups=mesh['dp'=32] {'dp'}, use_global_device_ids=true, to_apply=%region_69.70 | all-reduce | flops 12 | bytes 96 | tf_op jit(solution)/shard_map/pmax | solution.py:449
  937.6 40.7 %all-reduce.19 = (f32[768]{0:T(1024)S(1)}, f32[768]{0:T(1024)S(1)}, f32[768]{0:T(1024)S(1)}, f32[768]{0:T(1024)S(1)}, f32[768]{0:T(1024)S(1)}, /*index=5*/f32[30...) all-reduce(f32[768]{0:T(1024)S(1)} %add.464, ...), channel_id=3, replica_groups=mesh['dp'=32] {'dp'}, use_global_device_ids=true, to_apply=%region_35.36.clone | all-reduce | flops 9216 | bytes 73728
  992.9 20.7 %reduce-scatter.21.cloned.1.call-done = f32[24,768]{1,0:T(8,128)} async-done(((f32[768,768]{1,0:T(8,128)}), f32[24,768]{1,0:T(8,128)}) %reduce-scatter.21.cloned.1.call-update) | async-done | bytes 73744
  1013.6 104.4 %reduce-scatter.19.cloned.1.call-done = f32[24,768]{1,0:T(8,128)} async-done(((f32[768,768]{1,0:T(8,128)}), f32[24,768]{1,0:T(8,128)}) %reduce-scatter.19.cloned.1.call-update) | async-done | bytes 73744
  1118.0 141.8 %reduce-scatter.17.cloned.1.call-done = f32[96,768]{1,0:T(8,128)} async-done(((f32[3072,768]{1,0:T(8,128)}), f32[96,768]{1,0:T(8,128)}) %reduce-scatter.17.cloned.1.call-update) | async-done | bytes 294928 | tf_op jit(solution)/shard_map/reduce_scatter | solution.py:448
  1259.8 141.8 %reduce-scatter.15.cloned.1.call-done = f32[24,3072]{1,0:T(8,128)} async-done(((f32[768,3072]{1,0:T(8,128)}), f32[24,3072]{1,0:T(8,128)}) %reduce-scatter.15.cloned.1.call-update) | async-done | bytes 294928 | tf_op jit(solution)/shard_map/reduce_scatter | solution.py:448
  (651 shorter events, 177.8 us)
Async XLA Ops:
  7.2 234.9 %all-gather.9.cloned.1.call-start = ((), (), s32[]{:S(2)}) async-start(), calls=%async_computation.7 | async-start | bytes 1216512 | tf_op jit(solution)/shard_map/all_gather | solution.py:306
  7.9 243.2 %all-gather.11.cloned.1.call-start = ((), (), s32[]{:S(2)}) async-start(), calls=%async_computation.8 | async-start | bytes 1216512 | tf_op jit(solution)/shard_map/all_gather | solution.py:308
  8.7 247.9 %all-gather.7.cloned.1.call-start = ((), (), s32[]{:S(2)}) async-start(), calls=%async_computation.6 | async-start | bytes 1216512 | tf_op jit(solution)/shard_map/all_gather | solution.py:309
  9.4 453.3 %all-gather.13.cloned.1.call-start = ((), (), s32[]{:S(2)}) async-start(), calls=%async_computation.9 | async-start | bytes 1216512 | tf_op jit(solution)/shard_map/all_gather | solution.py:311
  10.0 457.0 %all-gather.15.cloned.1.call-start = ((), (), s32[]{:S(2)}) async-start(), calls=%async_computation.10 | async-start | bytes 4866048 | tf_op jit(solution)/shard_map/all_gather | solution.py:315
  10.6 464.7 %all-gather.17.cloned.1.call-start = ((), (), s32[]{:S(2)}) async-start(), calls=%async_computation.11 | async-start | bytes 4866048 | tf_op jit(solution)/shard_map/all_gather | solution.py:317
  11.1 981.8 %reduce-scatter.13.cloned.1.call-start = ((), (), s32[]{:S(2)}) async-start(), calls=%async_computation.12 | async-start | bytes 2433024 | tf_op jit(solution)/shard_map/reduce_scatter | solution.py:448
  12.3 62.5 %copy-start.123 = (s32[6,64]{1,0:T(8,128)}, s32[6,64]{1,0:T(8,128)S(1)}, u32[]{:S(2)}) copy-start(s32[6,64]{1,0:T(8,128)S(1)} %slice_bitcast_fusion.9) | copy-start | bytes 4612
  12.3 420.6 %copy-start.121 = (s32[6,64]{1,0:T(8,128)}, s32[6,64]{1,0:T(8,128)S(1)}, u32[]{:S(2)}) copy-start(s32[6,64]{1,0:T(8,128)S(1)} %slice_bitcast_fusion.8) | copy-start | bytes 4612
  14.2 55.7 %copy-start.167 = (pred[2,64]{1,0:T(4,128)(4,1)}, pred[2,64]{1,0:T(4,128)(4,1)S(1)}, u32[]{:S(2)}) copy-start(pred[2,64]{1,0:T(4,128)(4,1)S(1)} %get-tuple-element.240) | copy-start | bytes 388
  14.2 58.1 %copy-start.165 = (pred[2,64]{1,0:T(4,128)(4,1)}, pred[2,64]{1,0:T(4,128)(4,1)S(1)}, u32[]{:S(2)}) copy-start(pred[2,64]{1,0:T(4,128)(4,1)S(1)} %get-tuple-element.239) | copy-start | bytes 388
  66.1 176.0 %copy-start.12 = (bf16[1024,768]{1,0:T(8,128)(2,1)S(1)}, bf16[1024,768]{1,0:T(8,128)(2,1)}, u32[]{:S(2)}) copy-start(bf16[1024,768]{1,0:T(8,128)(2,1)} %param.20) | copy-start | bytes 4718596
  67.7 176.4 %copy-start.27 = (s32[576,64]{1,0:T(8,128)}, s32[576,64]{1,0:T(8,128)S(1)}, u32[]{:S(2)}) copy-start(s32[576,64]{1,0:T(8,128)S(1)} %gather_fusion.1) | copy-start | bytes 442372
  67.8 176.4 %copy-start.77 = (pred[12,6,8,64]{3,2,1,0:T(8,128)(4,1)}, pred[12,6,8,64]{3,2,1,0:T(8,128)(4,1)S(1)}, u32[]{:S(2)}) copy-start(pred[12,6,8,64]{3,2,1,0:T(8,128)(4,1)S(1)} %broadcast_compare_fusion.1) | copy-start | bytes 110596
  68.2 364.8 %copy-start.97 = (pred[12,6,8]{2,1,0:T(8,128)(4,1)}, pred[12,6,8]{2,1,0:T(8,128)(4,1)S(1)}, u32[]{:S(2)}) copy-start(pred[12,6,8]{2,1,0:T(8,128)(4,1)S(1)} %pad_not_fusion) | copy-start | bytes 1732
  69.8 363.2 %copy-start.20 = (s32[576,64]{1,0:T(8,128)}, s32[576,64]{1,0:T(8,128)S(1)}, u32[]{:S(2)}) copy-start(s32[576,64]{1,0:T(8,128)S(1)} %gather_fusion.4) | copy-start | bytes 442372
  69.9 363.1 %copy-start.59 = (pred[12,6,8,64]{3,2,1,0:T(8,128)(4,1)}, pred[12,6,8,64]{3,2,1,0:T(8,128)(4,1)S(1)}, u32[]{:S(2)}) copy-start(pred[12,6,8,64]{3,2,1,0:T(8,128)(4,1)S(1)} %broadcast_compare_fusion) | copy-start | bytes 110596
  71.1 460.0 %copy-start.107 = (f32[768]{0:T(1024)}, f32[768]{0:T(1024)S(1)}, u32[]{:S(2)}) copy-start(f32[768]{0:T(1024)S(1)} %convert_element_type.275) | copy-start | bytes 9220
  71.1 415.2 %copy-start.119 = (f32[768]{0:T(1024)}, f32[768]{0:T(1024)S(1)}, u32[]{:S(2)}) copy-start(f32[768]{0:T(1024)S(1)} %convert_element_type.276) | copy-start | bytes 9220
  242.1 132.2 %copy-start.116 = (pred[12,6,64]{2,1,0:T(8,128)(4,1)}, pred[12,6,64]{2,1,0:T(8,128)(4,1)S(1)}, u32[]{:S(2)}) copy-start(pred[12,6,64]{2,1,0:T(8,128)(4,1)S(1)} %get-tuple-element.129) | copy-start | bytes 13828
  324.6 30.7 %copy-start = (f32[12,6,64,8,64]{2,4,3,1,0:T(8,128)}, f32[12,6,64,8,64]{2,4,3,1,0:T(8,128)S(1)}, u32[]{:S(2)}) copy-start(f32[12,6,64,8,64]{2,4,3,1,0:T(8,128)S(1)} %get-tuple-element.212) | copy-start | bytes 28311556
  430.3 179.3 %copy-start.114 = (f32[12,2,64]{2,1,0:T(2,128)}, f32[12,2,64]{2,1,0:T(2,128)S(1)}, u32[]{:S(2)}) copy-start(f32[12,2,64]{2,1,0:T(2,128)S(1)} %get-tuple-element.190) | copy-start | bytes 18436
  465.3 50.5 %copy-start.152 = (f32[512]{0:T(512)}, f32[512]{0:T(512)S(1)}, u32[]{:S(2)}) copy-start(f32[512]{0:T(512)S(1)} %broadcast_multiply_fusion.13) | copy-start | bytes 6148
  466.6 64.6 %copy-start.8 = (f32[512,768]{1,0:T(8,128)}, f32[512,768]{1,0:T(8,128)S(1)}, u32[]{:S(2)}) copy-start(f32[512,768]{1,0:T(8,128)S(1)} %get-tuple-element.215) | copy-start | bytes 4718596
  466.6 64.6 %copy-start.126 = (f32[512]{0:T(512)}, f32[512]{0:T(512)S(1)}, u32[]{:S(2)}) copy-start(f32[512]{0:T(512)S(1)} %broadcast_multiply_fusion.11) | copy-start | bytes 6148
  466.9 48.9 %copy-start.169 = (f32[512]{0:T(512)}, f32[512]{0:T(512)S(1)}, u32[]{:S(2)}) copy-start(f32[512]{0:T(512)S(1)} %add_rsqrt_fusion.3) | copy-start | bytes 6148
  466.9 64.2 %copy-start.138 = (f32[512]{0:T(512)}, f32[512]{0:T(512)S(1)}, u32[]{:S(2)}) copy-start(f32[512]{0:T(512)S(1)} %add_rsqrt_fusion.1) | copy-start | bytes 6148
  559.6 433.3 %reduce-scatter.23.cloned.1.call-start = ((), (), s32[]{:S(2)}) async-start(), calls=%async_computation.17 | async-start | bytes 2433024
  653.7 40.8 %slice-start = ((s8[18874368]{0:T(1024)(128)(4,1)}), s8[4194304]{0:T(1024)(128)(4,1)S(1)}, s32[]{:S(2)}) async-start(s8[18874368]{0:T(1024)(128)(4,1)} %bitcast.384), calls=%async_computation.18 | async-start | bytes 8388608
  653.7 40.8 %slice-start.5 = ((s8[18874368]{0:T(1024)(128)(4,1)}), s8[4194304]{0:T(1024)(128)(4,1)S(1)}, s32[]{:S(2)}) async-start(s8[18874368]{0:T(1024)(128)(4,1)} %bitcast.386), calls=%async_computation.23 | async-start | bytes 8388608
  656.9 37.5 %slice-start.1 = ((s8[18874368]{0:T(1024)(128)(4,1)}), s8[4194304]{0:T(1024)(128)(4,1)S(1)}, s32[]{:S(2)}) async-start(s8[18874368]{0:T(1024)(128)(4,1)} %bitcast.384), calls=%async_computation.19 | async-start | bytes 8388608
  656.9 37.5 %slice-start.2 = ((s8[18874368]{0:T(1024)(128)(4,1)}), s8[4194304]{0:T(1024)(128)(4,1)S(1)}, s32[]{:S(2)}) async-start(s8[18874368]{0:T(1024)(128)(4,1)} %bitcast.384), calls=%async_computation.20 | async-start | bytes 8388608
  657.0 37.5 %slice-start.3 = ((s8[18874368]{0:T(1024)(128)(4,1)}), s8[4194304]{0:T(1024)(128)(4,1)S(1)}, s32[]{:S(2)}) async-start(s8[18874368]{0:T(1024)(128)(4,1)} %bitcast.384), calls=%async_computation.21 | async-start | bytes 8388608
  657.0 37.5 %slice-start.4 = ((s8[18874368]{0:T(1024)(128)(4,1)}), s8[2097152]{0:T(1024)(128)(4,1)S(1)}, s32[]{:S(2)}) async-start(s8[18874368]{0:T(1024)(128)(4,1)} %bitcast.384), calls=%async_computation.22 | async-start | bytes 4194304
  657.0 37.5 %slice-start.6 = ((s8[18874368]{0:T(1024)(128)(4,1)}), s8[4194304]{0:T(1024)(128)(4,1)S(1)}, s32[]{:S(2)}) async-start(s8[18874368]{0:T(1024)(128)(4,1)} %bitcast.386), calls=%async_computation.24 | async-start | bytes 8388608
  657.0 37.5 %slice-start.7 = ((s8[18874368]{0:T(1024)(128)(4,1)}), s8[4194304]{0:T(1024)(128)(4,1)S(1)}, s32[]{:S(2)}) async-start(s8[18874368]{0:T(1024)(128)(4,1)} %bitcast.386), calls=%async_computation.25 | async-start | bytes 8388608
  657.0 38.1 %slice-start.8 = ((s8[18874368]{0:T(1024)(128)(4,1)}), s8[4194304]{0:T(1024)(128)(4,1)S(1)}, s32[]{:S(2)}) async-start(s8[18874368]{0:T(1024)(128)(4,1)} %bitcast.386), calls=%async_computation.26 | async-start | bytes 8388608
  657.0 38.7 %slice-start.9 = ((s8[18874368]{0:T(1024)(128)(4,1)}), s8[2097152]{0:T(1024)(128)(4,1)S(1)}, s32[]{:S(2)}) async-start(s8[18874368]{0:T(1024)(128)(4,1)} %bitcast.386), calls=%async_computation.27 | async-start | bytes 4194304
  808.9 204.7 %reduce-scatter.21.cloned.1.call-start = ((), (), s32[]{:S(2)}) async-start(), calls=%async_computation.16 | async-start | bytes 2433024
  834.2 283.8 %reduce-scatter.19.cloned.1.call-start = ((), (), s32[]{:S(2)}) async-start(), calls=%async_computation.15 | async-start | bytes 2433024
  865.8 394.0 %reduce-scatter.17.cloned.1.call-start = ((), (), s32[]{:S(2)}) async-start(), calls=%async_computation.14 | async-start | bytes 9732096 | tf_op jit(solution)/shard_map/reduce_scatter | solution.py:448
  882.9 518.6 %reduce-scatter.15.cloned.1.call-start = ((), (), s32[]{:S(2)}) async-start(), calls=%async_computation.13 | async-start | bytes 9732096 | tf_op jit(solution)/shard_map/reduce_scatter | solution.py:448
  894.8 41.7 %copy-start.109 = (bf16[24,768]{1,0:T(8,128)(2,1)S(1)}, bf16[24,768]{1,0:T(8,128)(2,1)}, u32[]{:S(2)}) copy-start(bf16[24,768]{1,0:T(8,128)(2,1)} %param.24) | copy-start | bytes 110596
  894.8 41.7 %copy-start.110 = (bf16[24,768]{1,0:T(8,128)(2,1)S(1)}, bf16[24,768]{1,0:T(8,128)(2,1)}, u32[]{:S(2)}) copy-start(bf16[24,768]{1,0:T(8,128)(2,1)} %param.26) | copy-start | bytes 110596
  894.8 42.4 %copy-start.136 = (f32[12,64]{1,0:T(8,128)S(1)}, f32[12,64]{1,0:T(8,128)}, u32[]{:S(2)}) copy-start(f32[12,64]{1,0:T(8,128)} %get-tuple-element.231) | copy-start | bytes 9220
  894.8 42.4 %copy-start.137 = (f32[12,64]{1,0:T(8,128)S(1)}, f32[12,64]{1,0:T(8,128)}, u32[]{:S(2)}) copy-start(f32[12,64]{1,0:T(8,128)} %get-tuple-element.233) | copy-start | bytes 9220
  894.8 42.5 %copy-start.142 = (f32[768]{0:T(1024)S(1)}, f32[768]{0:T(1024)}, u32[]{:S(2)}) copy-start(f32[768]{0:T(1024)} %get-tuple-element.152) | copy-start | bytes 9220
  894.9 42.5 %copy-start.158 = (f32[768]{0:T(1024)S(1)}, f32[768]{0:T(1024)}, u32[]{:S(2)}) copy-start(f32[768]{0:T(1024)} %get-tuple-element.154) | copy-start | bytes 9220
  894.9 42.5 %copy-start.155 = (f32[768]{0:T(1024)S(1)}, f32[768]{0:T(1024)}, u32[]{:S(2)}) copy-start(f32[768]{0:T(1024)} %get-tuple-element.106) | copy-start | bytes 9220
  894.9 42.5 %copy-start.157 = (f32[768]{0:T(1024)S(1)}, f32[768]{0:T(1024)}, u32[]{:S(2)}) copy-start(f32[768]{0:T(1024)} %get-tuple-element.200) | copy-start | bytes 9220
  894.9 42.5 %copy-start.154 = (f32[768]{0:T(1024)S(1)}, f32[768]{0:T(1024)}, u32[]{:S(2)}) copy-start(f32[768]{0:T(1024)} %get-tuple-element.123) | copy-start | bytes 9220
  894.9 42.5 %copy-start.156 = (f32[768]{0:T(1024)S(1)}, f32[768]{0:T(1024)}, u32[]{:S(2)}) copy-start(f32[768]{0:T(1024)} %get-tuple-element.197) | copy-start | bytes 9220
  894.9 42.5 %copy-start.150 = (f32[3072]{0:T(1024)S(1)}, f32[3072]{0:T(1024)}, u32[]{:S(2)}) copy-start(f32[3072]{0:T(1024)} %get-tuple-element.235) | copy-start | bytes 36868
  894.9 42.5 %copy-start.151 = (f32[3072]{0:T(1024)S(1)}, f32[3072]{0:T(1024)}, u32[]{:S(2)}) copy-start(f32[3072]{0:T(1024)} %get-tuple-element.237) | copy-start | bytes 36868
  894.9 42.5 %copy-start.140 = (f32[768]{0:T(1024)S(1)}, f32[768]{0:T(1024)}, u32[]{:S(2)}) copy-start(f32[768]{0:T(1024)} %get-tuple-element.148) | copy-start | bytes 9220
  894.9 42.5 %copy-start.141 = (f32[768]{0:T(1024)S(1)}, f32[768]{0:T(1024)}, u32[]{:S(2)}) copy-start(f32[768]{0:T(1024)} %get-tuple-element.171) | copy-start | bytes 9220
  894.9 42.6 %copy-start.146 = (f32[768]{0:T(1024)S(1)}, f32[768]{0:T(1024)}, u32[]{:S(2)}) copy-start(f32[768]{0:T(1024)} %get-tuple-element.118) | copy-start | bytes 9220
  895.0 42.6 %copy-start.147 = (f32[768]{0:T(1024)S(1)}, f32[768]{0:T(1024)}, u32[]{:S(2)}) copy-start(f32[768]{0:T(1024)} %get-tuple-element.121) | copy-start | bytes 9220
  895.0 42.6 %copy-start.144 = (f32[768]{0:T(1024)S(1)}, f32[768]{0:T(1024)}, u32[]{:S(2)}) copy-start(f32[768]{0:T(1024)} %get-tuple-element.114) | copy-start | bytes 9220
  895.0 42.6 %copy-start.145 = (f32[768]{0:T(1024)S(1)}, f32[768]{0:T(1024)}, u32[]{:S(2)}) copy-start(f32[768]{0:T(1024)} %get-tuple-element.115) | copy-start | bytes 9220
  895.0 88.5 %copy-start.48 = (bf16[512,768]{1,0:T(8,128)(2,1)S(1)}, bf16[512,768]{1,0:T(8,128)(2,1)}, u32[]{:S(2)}) copy-start(bf16[512,768]{1,0:T(8,128)(2,1)} %get-tuple-element.169) | copy-start | bytes 2359300
  895.0 88.5 %copy-start.49 = (bf16[512,768]{1,0:T(8,128)(2,1)S(1)}, bf16[512,768]{1,0:T(8,128)(2,1)}, u32[]{:S(2)}) copy-start(bf16[512,768]{1,0:T(8,128)(2,1)} %get-tuple-element.170) | copy-start | bytes 2359300
  895.0 89.7 %copy-start.56 = (bf16[512,768]{0,1:T(8,128)(2,1)S(1)}, bf16[512,768]{0,1:T(8,128)(2,1)}, u32[]{:S(2)}) copy-start(bf16[512,768]{0,1:T(8,128)(2,1)} %convert_element_type.302) | copy-start | bytes 2359300
  936.4 49.2 %copy-start.180 = (f32[12]{0:T(128)}, f32[12]{0:T(128)S(1)}, u32[]{:S(2)}) copy-start(f32[12]{0:T(128)S(1)} %pmax.7) | copy-start | bytes 148
  (148 other events, 787.8 us)
Sparse Core Ops, SparseCore 0:
  10.9 56.7 all-gather.8
  70.6 52.8 all-gather.10
  126.4 52.8 all-gather.6
  182.1 52.8 all-gather.12
  237.7 62.5 all-gather.14
  303.0 61.9 all-gather.16
  559.7 99.8 reduce-scatter.12
  809.0 99.8 reduce-scatter.22
  914.8 98.8 reduce-scatter.20
  1019.3 98.6 reduce-scatter.18
  1124.5 135.2 reduce-scatter.16
  1266.1 135.4 reduce-scatter.14
where the time goes:
time: 1410 us
  waiting for transfers between devices  412 us (29%)
  matrix products  384 us (27%)
  other arithmetic  278 us (20%)
  local copies, waits for them, and re-layouts  192 us (14%)
  blocking collectives  123 us (9%)
  between operations  18 us (1%)
    reduce_scatter x3, waiting for transfers between devices, per_device(): summed = lax.psum_scatter(totals, 'dp', scatter_dimension=0, tiled=True)  284 us
    reduce_or x2, other arithmetic, softmax_parts(): row_live = jnp.any(allowed, axis=axes, keepdims=True)  168 us
    unnamed x15, waiting for transfers between devices  129 us
    unnamed x2, blocking collectives  83 us
    dot_general x2, matrix products, attention_backward(): jnp.einsum('shijcd,hijn->snchd', value_slope_gathered, onehot, precision=...  47.7 us
    dot_general x2, matrix products, attention_backward(): jnp.einsum('shijcd,hijn->snchd', key_slope_gathered, onehot, precision=la...  45.9 us
    dot_general x2, matrix products, region_scores(): jnp.einsum('sibhd,shijcd->shibjc', query_mid, key_gathered, preferred_ele...  45.7 us
    dot_general x2, matrix products, attention_backward(): jnp.einsum('sibhd,shijcd->shibjc', delta_mid, value_gathered, preferred_e...  45.2 us
  transfers between devices with their start and end apart: 12, of which 4 were waited for; matrix products, arithmetic and copies ran while one was open for 54% of the time, Pallas kernels for 0%

commit v1 on v0

v1 whole, which is shorter than its diff:
```python
from functools import partial
import math

import jax
import jax.numpy as jnp
from jax import lax
from jax.experimental import pallas as pl
from jax.experimental.pallas import tpu as pltpu
from jax.sharding import PartitionSpec as P

HD = 64
BLOCK = 64
SEQ = 512
BF = jnp.bfloat16
F32 = jnp.float32
LOW = -1e30
VMEM_MAX = 67043328


def dot(a, b):
    return jnp.dot(a, b, preferred_element_type=F32)


def dot_nt(a, b):
    return lax.dot_general(a, b, (((1,), (1,)), ((), ())), preferred_element_type=F32)


def dot_tn(a, b):
    return lax.dot_general(a, b, (((0,), (0,)), ((), ())), preferred_element_type=F32)


def attn_fwd_body(rb, x, segr, segc, wq, wk, wv, wo, qb, vb, ob,
                  q_o, k_o, v_o, p_o, c_o, z_o, hm_o, bias, s_s):
    g = pl.program_id(0)
    seqs = segr.shape[0]
    pairs = wq.shape[1] // 128

    @pl.when(g == 0)
    def _():
        for s in range(seqs):
            kseg = segr[s:s + 1, :]
            for c in range(SEQ // BLOCK):
                qseg = segc[s * SEQ + c * BLOCK:s * SEQ + (c + 1) * BLOCK, :]
                bias[s, c * BLOCK:(c + 1) * BLOCK, :] = jnp.where((qseg == kseg) & (kseg != 0), 0.0, LOW)
        hm_o[...] = jnp.full(hm_o.shape, LOW, F32)
        z_o[...] = x[...].astype(F32) + ob[...].astype(F32)

    xv = x[...]
    q_o[...] = (dot(xv, wq[...]) + qb[...].astype(F32)).astype(BF)
    k_o[...] = dot(xv, wk[...]).astype(BF)
    v_o[...] = (dot(xv, wv[...]) + vb[...].astype(F32)).astype(BF)

    lane_block = lax.broadcasted_iota(jnp.int32, (1, SEQ), 1) // BLOCK
    first_half = lax.broadcasted_iota(jnp.int32, (1, 128), 1) < HD
    last = SEQ // BLOCK - 2

    def one_pair(it, _):
        s = it // pairs
        pair = it % pairs
        rows = pl.ds(pl.multiple_of(s * SEQ, SEQ), SEQ)
        lanes = pl.ds(pl.multiple_of(pair * 128, 128), 128)
        qp = q_o[rows, lanes]
        kp = k_o[rows, lanes]
        vp = v_o[rows, lanes]
        outs = []
        for j in range(2):
            head = g * (2 * pairs) + pair * 2 + j
            mine = first_half if j == 0 else jnp.logical_not(first_half)
            s_s[j] = dot_nt(jnp.where(mine, qp * 0.125, 0).astype(BF), kp)
            at = head * (6 * 3)
            miss1 = 18 - (rb[at] + rb[at + 1] + rb[at + 2])
            miss6 = 10 - (rb[at + 15] + rb[at + 16] + rb[at + 17])
            skip1 = jnp.where(lane_block == miss1, LOW, 0.0)
            skip6 = jnp.where(lane_block == miss6, LOW, 0.0)
            tops = None
            for c in range(SEQ // BLOCK):
                cr = slice(c * BLOCK, (c + 1) * BLOCK)
                sv = s_s[j, cr, :] + bias[s, cr, :]
                if c == 1:
                    sv = sv + skip1
                if c == last:
                    sv = sv + skip6
                top = jnp.max(sv, axis=1, keepdims=True)
                live = top > -1e29
                e = jnp.exp(sv - jnp.where(live, top, 0.0))
                total = jnp.sum(e, axis=1, keepdims=True) + jnp.where(live, 0.0, 1.0)
                p_o[s * (2 * pairs) + pair * 2 + j, cr, :] = (e * (1.0 / total)).astype(BF)
                tops = top if tops is None else jnp.maximum(tops, top)
            hm = jnp.max(tops, axis=0, keepdims=True)
            hm_o[pl.ds(head, 1), :] = jnp.maximum(hm_o[pl.ds(head, 1), :], hm)
            outs.append(dot(p_o[s * (2 * pairs) + pair * 2 + j], vp))
        c_o[rows, lanes] = jnp.where(first_half, outs[0], outs[1]).astype(BF)
        return 0

    lax.fori_loop(0, seqs * pairs, one_pair, 0)
    z_o[...] += dot(c_o[...], wo[...])


def attn_fwd(rb, x, segr, segc, wq, wk, wv, wo, qb, vb, ob):
    rows, d = x.shape
    seqs = rows // SEQ
    gw = 256
    groups = d // gw
    maps = seqs * (gw // HD)
    full = lambda shape: pl.BlockSpec(shape, lambda g, *_: (0,) * len(shape))
    col = pl.BlockSpec((d, gw), lambda g, *_: (0, g))
    vec = pl.BlockSpec((1, gw), lambda g, *_: (0, g))
    act = pl.BlockSpec((rows, gw), lambda g, *_: (0, g))
    return pl.pallas_call(
        attn_fwd_body,
        grid_spec=pltpu.PrefetchScalarGridSpec(
            num_scalar_prefetch=1, grid=(groups,),
            in_specs=[full((rows, d)), full((seqs, SEQ)), full((rows, 1)), col, col, col,
                      pl.BlockSpec((gw, d), lambda g, *_: (g, 0)), vec, vec, full((1, d))],
            out_specs=[act, act, act, pl.BlockSpec((maps, SEQ, SEQ), lambda g, *_: (g, 0, 0)), act,
                       full((rows, d)), full((16, 128))],
            scratch_shapes=[pltpu.VMEM((seqs, SEQ, SEQ), F32), pltpu.VMEM((2, SEQ, SEQ), F32)]),
        out_shape=[jax.ShapeDtypeStruct((rows, d), BF)] * 3
        + [jax.ShapeDtypeStruct((groups * maps, SEQ, SEQ), BF), jax.ShapeDtypeStruct((rows, d), BF),
           jax.ShapeDtypeStruct((rows, d), F32), jax.ShapeDtypeStruct((16, 128), F32)],
        compiler_params=pltpu.CompilerParams(vmem_limit_bytes=VMEM_MAX),
        name="attn_fwd",
    )(rb, x, segr, segc, wq, wk, wv, wo, qb, vb, ob)


def unit_rows(z):
    mean = jnp.mean(z, axis=-1, keepdims=True)
    c = z - mean
    inv = lax.rsqrt(jnp.mean(c * c, axis=-1, keepdims=True) + 1e-12)
    return c * inv, inv


def norm_back(up, unit, inv, gain):
    e = up * gain
    spread = jnp.mean(e, axis=-1, keepdims=True)
    along = jnp.mean(e * unit, axis=-1, keepdims=True)
    return inv * (e - spread - unit * along)


def col_sum(v):
    return jnp.sum(v, axis=0, keepdims=True)


def ffn_body(z, cot, wi, wo, bi, bo, ag, ash, fg, fs,
             out, dsum, db, dwi, dwo, dbi, small, fl, act, gp, acc, do):
    rows, d = z.shape
    ff = wi.shape[1]
    rt, ct, et = 512, 512, 128
    k0, k1 = math.sqrt(2.0 / math.pi), 0.044715
    agv, ashv = ag[...].astype(F32), ash[...].astype(F32)
    fgv, fsv, bov = fg[...].astype(F32), fs[...].astype(F32), bo[...].astype(F32)

    def prep(i, _):
        r = pl.ds(pl.multiple_of(i * et, et), et)
        unit, _inv = unit_rows(z[r, :])
        first = unit * agv + ashv
        fl[r, :] = first.astype(BF)
        acc[r, :] = first + bov
        return 0

    lax.fori_loop(0, rows // et, prep, 0)

    def up(i, _):
        r = pl.ds(pl.multiple_of((i % (rows // rt)) * rt, rt), rt)
        c = pl.ds(pl.multiple_of((i // (rows // rt)) * ct, ct), ct)
        u = dot(fl[r, :], wi[:, c]) + bi[:, c].astype(F32)
        u2 = u * u
        t = jnp.tanh(u * (k0 + (k0 * k1) * u2))
        h = 0.5 + 0.5 * t
        a = (u * h).astype(BF)
        act[r, c] = a
        gp[r, c] = (h + (0.5 * u) * (1.0 - t * t) * (k0 + (3.0 * k0 * k1) * u2)).astype(gp.dtype)
        acc[r, :] += dot(a, wo[c, :])
        return 0

    lax.fori_loop(0, (ff // ct) * (rows // rt), up, 0)

    small[...] = jnp.zeros(small.shape, F32)

    def mid(i, _):
        r = pl.ds(pl.multiple_of(i * et, et), et)
        unit, inv = unit_rows(acc[r, :])
        out[r, :] = (unit * fgv + fsv).astype(BF)
        upv = cot[r, :].astype(F32)
        small[0:1, :] += col_sum(upv * unit)
        small[1:2, :] += col_sum(upv)
        ds = norm_back(upv, unit, inv, fgv)
        dsl = ds.astype(BF)
        do[r, :] = dsl
        acc[r, :] = ds
        small[2:3, :] += col_sum(dsl.astype(F32))
        return 0

    lax.fori_loop(0, rows // et, mid, 0)

    def down(j, _):
        c = pl.ds(pl.multiple_of(j * ct, ct), ct)
        dwo[c, :] = dot_tn(act[:, c], do[...]).astype(dwo.dtype)
        sums = None
        for i in range(rows // rt):
            r = slice(i * rt, (i + 1) * rt)
            di = dot_nt(do[r, :], wo[c, :]) * gp[r, c].astype(F32)
            dil = di.astype(BF)
            act[r, c] = dil
            s = col_sum(dil.astype(F32))
            sums = s if sums is None else sums + s
            acc[r, :] += dot_nt(dil, wi[:, c])
        dbi[:, c] = sums
        dwi[:, c] = dot_tn(fl[...], act[:, c]).astype(dwi.dtype)
        return 0

    lax.fori_loop(0, ff // ct, down, 0)

    def tail(i, _):
        r = pl.ds(pl.multiple_of(i * et, et), et)
        unit, inv = unit_rows(z[r, :])
        df = acc[r, :]
        small[3:4, :] += col_sum(df * unit)
        small[4:5, :] += col_sum(df)
        ds = norm_back(df, unit, inv, agv)
        dsum[r, :] = ds
        dsl = ds.astype(BF)
        db[r, :] = dsl
        small[5:6, :] += col_sum(dsl.astype(F32))
        return 0

    lax.fori_loop(0, rows // et, tail, 0)


def ffn(z, cot, wi, wo, bi, bo, ag, ash, fg, fs, gdt):
    rows, d = z.shape
    ff = wi.shape[1]
    sd = jax.ShapeDtypeStruct
    vm = pl.BlockSpec(memory_space=pltpu.VMEM)
    return pl.pallas_call(
        ffn_body,
        in_specs=[vm] * 10,
        out_specs=[vm] * 7,
        out_shape=[sd((rows, d), BF), sd((rows, d), F32), sd((rows, d), BF), sd((d, ff), gdt), sd((ff, d), gdt),
                   sd((1, ff), F32), sd((8, d), F32)],
        scratch_shapes=[pltpu.VMEM((rows, d), BF), pltpu.VMEM((rows, ff), BF), pltpu.VMEM((rows, ff), BF),
                        pltpu.VMEM((rows, d), F32), pltpu.VMEM((rows, d), BF)],
        compiler_params=pltpu.CompilerParams(vmem_limit_bytes=VMEM_MAX),
        name="ffn",
    )(z, cot, wi, wo, bi, bo, ag, ash, fg, fs)


def attn_bwd_body(x, db, wq, wk, wv, wo, q, k, v, p, ctx, dsum,
                  dwq, dwk, dwv, dwo, dqb, dvb, dx, dc, dq, dk, dv, dp_s, ds_s):
    g = pl.program_id(0)
    seqs = x.shape[0] // SEQ
    pairs = wq.shape[1] // 128

    @pl.when(g == 0)
    def _():
        dx[...] = dsum[...]

    dbv = db[...]
    dc[...] = dot_nt(dbv, wo[...]).astype(BF)
    dwo[...] = dot_tn(ctx[...], dbv).astype(dwo.dtype)
    first_half = lax.broadcasted_iota(jnp.int32, (1, 128), 1) < HD

    def one_pair(it, _):
        s = it // pairs
        pair = it % pairs
        rows = pl.ds(pl.multiple_of(s * SEQ, SEQ), SEQ)
        lanes = pl.ds(pl.multiple_of(pair * 128, 128), 128)
        qp, kp, vp, dcp = q[rows, lanes], k[rows, lanes], v[rows, lanes], dc[rows, lanes]
        dqs, dks, dvs = [], [], []
        for j in range(2):
            mine = first_half if j == 0 else jnp.logical_not(first_half)
            m = s * (2 * pairs) + pair * 2 + j
            dp_s[j] = dot_nt(jnp.where(mine, dcp, 0).astype(BF), vp)
            for c in range(SEQ // BLOCK):
                cr = slice(c * BLOCK, (c + 1) * BLOCK)
                pv = p[m, cr, :].astype(F32)
                sl = dp_s[j, cr, :]
                mean = jnp.sum(pv * sl, axis=1, keepdims=True)
                ds_s[j, cr, :] = (pv * (sl - mean)).astype(BF)
            dqs.append(dot(ds_s[j], kp))
            dks.append(dot_tn(ds_s[j], qp))
            dvs.append(dot_tn(p[m], dcp))
        dq[rows, lanes] = (jnp.where(first_half, dqs[0], dqs[1]) * 0.125).astype(BF)
        dk[rows, lanes] = (jnp.where(first_half, dks[0], dks[1]) * 0.125).astype(BF)
        dv[rows, lanes] = jnp.where(first_half, dvs[0], dvs[1]).astype(BF)
        return 0

    lax.fori_loop(0, seqs * pairs, one_pair, 0)
    dqb[...] = col_sum(dq[...].astype(F32))
    dvb[...] = col_sum(dv[...].astype(F32))
    xv = x[...]
    dwq[...] = dot_tn(xv, dq[...]).astype(dwq.dtype)
    dwk[...] = dot_tn(xv, dk[...]).astype(dwk.dtype)
    dwv[...] = dot_tn(xv, dv[...]).astype(dwv.dtype)
    dx[...] += dot_nt(dq[...], wq[...]) + dot_nt(dk[...], wk[...]) + dot_nt(dv[...], wv[...])


def attn_bwd(x, db, wq, wk, wv, wo, q, k, v, p, ctx, dsum, gdt):
    rows, d = x.shape
    seqs = rows // SEQ
    gw = 256
    groups = d // gw
    maps = seqs * (gw // HD)
    full = lambda shape: pl.BlockSpec(shape, lambda g: (0,) * len(shape), pipeline_mode=pl.Buffered(1))
    col = pl.BlockSpec((d, gw), lambda g: (0, g))
    row = pl.BlockSpec((gw, d), lambda g: (g, 0))
    vec = pl.BlockSpec((1, gw), lambda g: (0, g))
    act = pl.BlockSpec((rows, gw), lambda g: (0, g))
    sd = jax.ShapeDtypeStruct
    return pl.pallas_call(
        attn_bwd_body,
        grid=(groups,),
        in_specs=[full((rows, d)), full((rows, d)), col, col, col, row, act, act, act,
                  pl.BlockSpec((maps, SEQ, SEQ), lambda g: (g, 0, 0)), act, full((rows, d))],
        out_specs=[col, col, col, row, vec, vec, pl.BlockSpec((rows, d), lambda g: (0, 0))],
        out_shape=[sd((d, d), gdt)] * 4 + [sd((1, d), F32)] * 2 + [sd((rows, d), F32)],
        scratch_shapes=[pltpu.VMEM((rows, gw), BF)] * 4
        + [pltpu.VMEM((2, SEQ, SEQ), F32), pltpu.VMEM((2, SEQ, SEQ), BF)],
        compiler_params=pltpu.CompilerParams(vmem_limit_bytes=VMEM_MAX),
        name="attn_bwd",
    )(x, db, wq, wk, wv, wo, q, k, v, p, ctx, dsum)


def per_device(tokens, segment_ids, random_blocks, clip_limit, query_weight, query_bias, key_weight, value_weight,
               value_bias, output_weight, output_bias, attn_gain, attn_shift, inner_weight, inner_bias,
               outer_weight, outer_bias, final_gain, final_shift, out_cotangent):
    heads = random_blocks.shape[0]
    rows, d = tokens.shape
    gather = lambda a: lax.all_gather(a, "dp", axis=0, tiled=True)
    wq, wk, wv, wo = map(gather, (query_weight, key_weight, value_weight, output_weight))
    wi, wu = gather(inner_weight), gather(outer_weight)
    names = (query_bias, value_bias, output_bias, attn_gain, attn_shift, outer_bias, final_gain, final_shift)
    part = query_bias.shape[0]
    vecs = gather(jnp.concatenate(names + (inner_bias,))[None])
    n = vecs.shape[0]
    qb, vb, ob, ag, ash, bo, fg, fs = (vecs[:, i * part:(i + 1) * part].reshape(1, n * part) for i in range(8))
    bi = vecs[:, 8 * part:].reshape(1, -1)
    q, k, v, p, ctx, z, hm = attn_fwd(
        random_blocks.reshape(-1), tokens, segment_ids.reshape(-1, SEQ), segment_ids.reshape(-1, 1),
        wq, wk, wv, wo, qb, vb, ob)
    out, dsum, db, dwi, dwu, dbi, small = ffn(z, out_cotangent, wi, wu, bi, bo, ag, ash, fg, fs, F32)
    dwq, dwk, dwv, dwo, dqb, dvb, dx = attn_bwd(tokens, db, wq, wk, wv, wo, q, k, v, p, ctx, dsum, F32)
    scatter = lambda a: lax.psum_scatter(a, "dp", scatter_dimension=0, tiled=True)
    dwu, dwi, dwo, dwq, dwk, dwv = (scatter(a) for a in (dwu, dwi, dwo, dwq, dwk, dwv))
    vec = lambda a: a.reshape(n, -1)
    smalls = jnp.concatenate([vec(dqb), vec(dvb), vec(small[5]), vec(small[3]), vec(small[4]), vec(small[2]),
                              vec(small[0]), vec(small[1]), vec(dbi)], axis=1)
    smalls = scatter(smalls)[0]
    dqb, dvb, dob, dag, dash, dbo, dfg, dfs = (smalls[i * part:(i + 1) * part] for i in range(8))
    dbi = smalls[8 * part:]
    head_maxima = lax.pmax(hm[:heads, 0], "dp")
    limit = clip_limit[0].astype(F32)
    factor = jnp.sqrt(jnp.minimum(1.0, limit / jnp.maximum(head_maxima, 1.0)))
    columns = jnp.repeat(factor, HD)[None, :]
    cq = (query_weight.astype(F32) * columns).astype(BF)
    ck = (key_weight.astype(F32) * columns).astype(BF)
    return (out, dx, dwq, dqb, dwk, dwv, dvb, dwo, dob, dag, dash, dwi, dbi, dwu, dbo, dfg, dfs, cq, ck, head_maxima)


def solution(mesh):
    mat, vec, rep = P("dp", None), P("dp"), P()
    in_specs = (mat, vec, rep, rep, mat, vec, mat, mat, vec, mat, vec, vec, vec, mat, vec, mat, vec, vec, vec, mat)
    out_specs = (mat, mat, mat, vec, mat, mat, vec, mat, vec, vec, vec, mat, vec, mat, vec, vec, vec, mat, mat, rep)
    return jax.shard_map(per_device, mesh=mesh, in_specs=in_specs, out_specs=out_specs, check_vma=False)
```

time: 1410 us -> 1170 us (0.83)
  waiting for transfers between devices: 412 us -> 878 us
  matrix products: 384 us -> 0 us
  other arithmetic: 278 us -> 1.38 us
  local copies, waits for them, and re-layouts: 192 us -> 20.2 us
  Pallas kernels: 0 us -> 136 us
    dot_general x64 -> x0, matrix products: 384 us -> none  [the longest x2 47.7 us: attention_backward(): jnp.einsum('shijcd,hijn->snchd', value_slope_gathered, onehot, precision=...]
    reduce_scatter x3 -> x6, waiting for transfers between devices: 284 us -> 607 us  [per_device(): lax.psum_scatter(a, 'dp', scatter_dimension=0, tiled=True)]
    all_gather x6, waiting for transfers between devices: 0.03 us -> 264 us  [per_device(): gather = lambda a: lax.all_gather(a, 'dp', axis=0, tiled=True)]
    reduce_or x2 -> x0, other arithmetic: 168 us -> none  [softmax_parts(): row_live = jnp.any(allowed, axis=axes, keepdims=True)]
    pallas_call x0 -> x3, Pallas kernels: none -> 136 us  [the longest x1 63.2 us: ffn(): pl.pallas_call(ffn_body, in_specs=[vm] * 10, out_specs=[vm] * 7, out_shap...]
    unnamed x15 -> x12, waiting for transfers between devices: 129 us -> 6.69 us
    convert_element_type x19 -> x1, other arithmetic: 87.2 us -> 0.66 us  [per_device(): ck = (key_weight.astype(F32) * columns).astype(BF)]
    reshape x24 -> x15, local copies, waits for them, and re-layouts: 54.6 us -> 10.1 us  [the longest x8 5.43 us: per_device(): vecs[:, i * part:(i + 1) * part].reshape(1, n * part)]
  transfers between devices with their start and end apart: 12 -> 12, of which waited for: 4 -> 11; matrix products, arithmetic and copies ran while one was open for 54% -> 2% of each run, Pallas kernels for 0% -> 3%
where the time goes in v1:
time: 1170 us
  waiting for transfers between devices  878 us (75%)
  Pallas kernels  136 us (12%)
  blocking collectives  122 us (10%)
  local copies, waits for them, and re-layouts  20.2 us (2%)
  between operations  15.1 us (1%)
    reduce_scatter x6, waiting for transfers between devices, per_device(): lax.psum_scatter(a, 'dp', scatter_dimension=0, tiled=True)  607 us
    all_gather x6, waiting for transfers between devices, per_device(): gather = lambda a: lax.all_gather(a, 'dp', axis=0, tiled=True)  264 us
    unnamed x2, blocking collectives  83.1 us
    pallas_call x1, Pallas kernels, ffn(): pl.pallas_call(ffn_body, in_specs=[vm] * 10, out_specs=[vm] * 7, out_shap...  63.2 us
    pallas_call x1, Pallas kernels, attn_bwd(): pl.pallas_call(attn_bwd_body, grid=(groups,), in_specs=[full((rows, d)),...  42.5 us
    pmax x1, blocking collectives, per_device(): head_maxima = lax.pmax(hm[:heads, 0], 'dp')  39.1 us
    pallas_call x1, Pallas kernels, attn_fwd(): pl.pallas_call(attn_fwd_body, grid_spec=pltpu.PrefetchScalarGridSpec(num_...  29.9 us
  transfers between devices with their start and end apart: 12, of which 11 were waited for; matrix products, arithmetic and copies ran while one was open for 2% of the time, Pallas kernels for 3%

profile of v1, /device:TPU:0, one launch (start us, length us, event | category | flops | bytes accessed | tf_op | source)
XLA Modules:
  0.0 1172.7 jit_solution(8923767856368980204)
XLA Ops:
  7.2 0.7 all-gather.10.cloned.1.call-update
  8.0 0.7 all-gather.12.cloned.1.call-update
  8.7 0.7 all-gather.14.cloned.1.call-update
  9.5 0.5 all-gather.8.cloned.1.call-update
  10.0 0.5 all-gather.16.cloned.1.call-update
  10.6 0.5 all-gather.18.cloned.1.call-update
  11.2 6.1 concatenate.6
  17.3 0.2 dynamic-update-slice
  17.6 42.4 %all-reduce = bf16[9216]{0:T(1024)(128)(2,1)S(1)} all-reduce(bf16[9216]{0:T(1024)(128)(2,1)S(1)} %dynamic-update-slice), channel_id=2, replica_groups=mesh['dp'=32] {'dp'}, use_global_device_ids=true, to_apply=%add | all-reduce | flops 9216 | bytes 36864
  59.9 0.1 reshape.111
  60.0 0.1 slice.139
  60.1 0.1 fusion
  60.2 0.7 reshape.100.vb
  60.9 0.7 reshape.101.ob
  61.6 0.7 reshape.99.qb
  62.2 1.3 reshape.97.segr
  63.5 1.7 copy.43.segc
  65.2 0.8 copy.42
  66.1 0.7 reshape.96.rb
  66.8 0.7 reshape.103.bo
  67.5 0.7 reshape.104.ag
  68.1 0.7 reshape.105.ash
  68.8 0.7 reshape.106.fg
  69.5 0.7 reshape.107.fs
  70.2 0.7 reshape.102.bi
  70.9 52.8 %all-gather.12.cloned.1.call-done.wv = bf16[768,768]{1,0:T(8,128)(2,1)} async-done(((bf16[24,768]{1,0:T(8,128)(2,1)}), bf16[768,768]{1,0:T(8,128)(2,1)}) %all-gather.12.cloned.1.call-update) | async-done | bytes 1179664 | tf_op jit(solution)/shard_map/all_gather | solution.py:329
  123.6 55.8 %all-gather.14.cloned.1.call-done.wo = bf16[768,768]{1,0:T(8,128)(2,1)} async-done(((bf16[24,768]{1,0:T(8,128)(2,1)}), bf16[768,768]{1,0:T(8,128)(2,1)}) %all-gather.14.cloned.1.call-update) | async-done | bytes 1179664 | tf_op jit(solution)/shard_map/all_gather | solution.py:329
  179.4 55.6 %all-gather.8.cloned.1.call-done.wq = bf16[768,768]{1,0:T(8,128)(2,1)} async-done(((bf16[24,768]{1,0:T(8,128)(2,1)}), bf16[768,768]{1,0:T(8,128)(2,1)}) %all-gather.8.cloned.1.call-update) | async-done | bytes 1179664 | tf_op jit(solution)/shard_map/all_gather | solution.py:329
  235.0 29.9 %attn_fwd.1 = (bf16[1024,768]{1,0:T(8,128)(2,1)}, bf16[1024,768]{1,0:T(8,128)(2,1)}, bf16[1024,768]{1,0:T(8,128)(2,1)}, bf16[24,512,512]{2,1,0:T(8,128)(2,1)}, b...) custom-call(s32[216]{0:T(256)} %reshape.96.rb, bf16[1024,768]{1,0:T(8,128)(2,1)} %x.4, ...), custom_call_target="tpu_custom_call" | custom-call | tf_op jit(solution)/shard_map/attn_fwd/pallas_call | solution.py:109
  264.9 35.4 %all-gather.16.cloned.1.call-done.wi = bf16[768,3072]{1,0:T(8,128)(2,1)} async-done(((bf16[24,3072]{1,0:T(8,128)(2,1)}), bf16[768,3072]{1,0:T(8,128)(2,1)}) %all-gather.16.cloned.1.call-update) | async-done | bytes 4718608 | tf_op jit(solution)/shard_map/all_gather | solution.py:329
  300.3 64.7 %all-gather.18.cloned.1.call-done.wo = bf16[3072,768]{1,0:T(8,128)(2,1)} async-done(((bf16[96,768]{1,0:T(8,128)(2,1)}), bf16[3072,768]{1,0:T(8,128)(2,1)}) %all-gather.18.cloned.1.call-update) | async-done | bytes 4718608 | tf_op jit(solution)/shard_map/all_gather | solution.py:329
  365.0 63.2 %ffn.1 = (bf16[1024,768]{1,0:T(8,128)(2,1)}, f32[1024,768]{1,0:T(8,128)}, bf16[1024,768]{1,0:T(8,128)(2,1)}, f32[768,3072]{1,0:T(8,128)}, f32[3072,768]{1,0:T(8,...) custom-call(f32[1024,768]{1,0:T(8,128)} %get-tuple-element.41.z, bf16[1024,768]{1,0:T(8,128)(2,1)} %cot.1, ...), custom_call_target="tpu_custom_call" | custom-call | tf_op jit(solution)/shard_map/ffn/pallas_call | solution.py:235
  428.2 42.5 %attn_bwd.1 = (f32[768,768]{1,0:T(8,128)}, f32[768,768]{1,0:T(8,128)}, f32[768,768]{1,0:T(8,128)}, f32[768,768]{1,0:T(8,128)}, f32[1,768]{1,0:T(1,128)}, /*index=5*/f32[1,768]{1,0:T(1,128)}, f32[1024,768]{1,0:T(8,128)}) custom-call(bf16[1024,768]{1,0:T(8,128)(2,1)} %x.4, bf16[1024,768]{1,0:T(8,128)(2,1)} %get-tuple-element.43.db, ...), custom_call_target="tpu_custom_call" | custom-call | tf_op jit(solution)/shard_map/attn_bwd/pallas_call | solution.py:310
  470.7 0.7 reduce-scatter.13.cloned.1.call-update
  471.5 0.7 reduce-scatter.7.cloned.1.call-update
  472.2 0.5 reduce-scatter.9.cloned.1.call-update
  472.8 0.7 reduce-scatter.15.cloned.1.call-update
  473.6 0.4 reduce-scatter.17.cloned.1.call-update
  474.7 0.1 slice_reduce_fusion
  474.8 39.1 %pmax.7 = f32[12]{0:T(128)S(1)} all-reduce(f32[12]{0:T(128)S(1)} %slice_reduce_fusion), channel_id=1, replica_groups=mesh['dp'=32] {'dp'}, use_global_device_ids=true, to_apply=%region_7.0 | all-reduce | flops 12 | bytes 96 | tf_op jit(solution)/shard_map/pmax | solution.py:351
  514.0 0.1 broadcast_in_dim.7
  514.0 0.1 mul.16
  514.1 0.7 multiply_convert_fusion
  514.8 0.1 reshape.108
  514.9 0.1 reshape.109
  515.1 0.1 reshape_squeeze.18
  515.2 0.1 reshape_squeeze.19
  515.3 0.1 reshape_squeeze.20
  515.3 0.1 reshape_squeeze.21
  515.4 0.1 reshape_squeeze.22
  515.5 0.1 reshape_squeeze.23
  515.6 0.5 broadcast.18
  516.1 0.7 reduce.19
  516.8 0.1 reshape.110
  516.9 0.1 concatenate.7
  517.0 40.7 %all-reduce.1 = f32[32,288]{1,0:T(8,128)S(1)} all-reduce(f32[32,288]{1,0:T(8,128)S(1)} %concatenate.7), channel_id=4, replica_groups=mesh['dp'=32] {'dp'}, use_global_device_ids=true, to_apply=%region_1.0.clone | all-reduce | flops 9216 | bytes 73728
  557.7 0.6 dynamic-slice_bitcast_fusion.3
  558.3 0.6 dynamic-slice_bitcast_fusion
  558.9 10.3 reduce-scatter.11.cloned.1.call-done
  569.2 104.6 %reduce-scatter.13.cloned.1.call-done = f32[24,768]{1,0:T(8,128)} async-done(((f32[768,768]{1,0:T(8,128)}), f32[24,768]{1,0:T(8,128)}) %reduce-scatter.13.cloned.1.call-update) | async-done | bytes 73744 | tf_op jit(solution)/shard_map/reduce_scatter | solution.py:343
  673.8 104.5 %reduce-scatter.7.cloned.1.call-done = f32[24,768]{1,0:T(8,128)} async-done(((f32[768,768]{1,0:T(8,128)}), f32[24,768]{1,0:T(8,128)}) %reduce-scatter.7.cloned.1.call-update) | async-done | bytes 73744 | tf_op jit(solution)/shard_map/reduce_scatter | solution.py:343
  778.3 104.4 %reduce-scatter.9.cloned.1.call-done = f32[24,768]{1,0:T(8,128)} async-done(((f32[768,768]{1,0:T(8,128)}), f32[24,768]{1,0:T(8,128)}) %reduce-scatter.9.cloned.1.call-update) | async-done | bytes 73744 | tf_op jit(solution)/shard_map/reduce_scatter | solution.py:343
  882.6 141.7 %reduce-scatter.15.cloned.1.call-done = f32[24,3072]{1,0:T(8,128)} async-done(((f32[768,3072]{1,0:T(8,128)}), f32[24,3072]{1,0:T(8,128)}) %reduce-scatter.15.cloned.1.call-update) | async-done | bytes 294928 | tf_op jit(solution)/shard_map/reduce_scatter | solution.py:343
  1024.3 141.5 %reduce-scatter.17.cloned.1.call-done = f32[96,768]{1,0:T(8,128)} async-done(((f32[3072,768]{1,0:T(8,128)}), f32[96,768]{1,0:T(8,128)}) %reduce-scatter.17.cloned.1.call-update) | async-done | bytes 294928 | tf_op jit(solution)/shard_map/reduce_scatter | solution.py:343
  (35 shorter events, 0.6 us)
Async XLA Ops:
  7.2 63.7 %all-gather.10.cloned.1.call-start = ((), (), s32[]{:S(2)}) async-start(), calls=%async_computation.7 | async-start | bytes 1216512 | tf_op jit(solution)/shard_map/all_gather | solution.py:329
  7.9 115.7 %all-gather.12.cloned.1.call-start = ((), (), s32[]{:S(2)}) async-start(), calls=%async_computation.8 | async-start | bytes 1216512 | tf_op jit(solution)/shard_map/all_gather | solution.py:329
  8.7 170.7 %all-gather.14.cloned.1.call-start = ((), (), s32[]{:S(2)}) async-start(), calls=%async_computation.9 | async-start | bytes 1216512 | tf_op jit(solution)/shard_map/all_gather | solution.py:329
  9.4 225.6 %all-gather.8.cloned.1.call-start = ((), (), s32[]{:S(2)}) async-start(), calls=%async_computation.6 | async-start | bytes 1216512 | tf_op jit(solution)/shard_map/all_gather | solution.py:329
  10.0 290.3 %all-gather.16.cloned.1.call-start = ((), (), s32[]{:S(2)}) async-start(), calls=%async_computation.10 | async-start | bytes 4866048 | tf_op jit(solution)/shard_map/all_gather | solution.py:329
  10.6 354.4 %all-gather.18.cloned.1.call-start = ((), (), s32[]{:S(2)}) async-start(), calls=%async_computation.11 | async-start | bytes 4866048 | tf_op jit(solution)/shard_map/all_gather | solution.py:329
  11.2 558.1 %reduce-scatter.11.cloned.1.call-start = ((), (), s32[]{:S(2)}) async-start(), calls=%async_computation.14 | async-start | bytes 2433024 | tf_op jit(solution)/shard_map/reduce_scatter | solution.py:343
  470.7 203.1 %reduce-scatter.13.cloned.1.call-start = ((), (), s32[]{:S(2)}) async-start(), calls=%async_computation.15 | async-start | bytes 2433024 | tf_op jit(solution)/shard_map/reduce_scatter | solution.py:343
  471.4 306.8 %reduce-scatter.7.cloned.1.call-start = ((), (), s32[]{:S(2)}) async-start(), calls=%async_computation.12 | async-start | bytes 2433024 | tf_op jit(solution)/shard_map/reduce_scatter | solution.py:343
  472.2 410.5 %reduce-scatter.9.cloned.1.call-start = ((), (), s32[]{:S(2)}) async-start(), calls=%async_computation.13 | async-start | bytes 2433024 | tf_op jit(solution)/shard_map/reduce_scatter | solution.py:343
  472.8 551.6 %reduce-scatter.15.cloned.1.call-start = ((), (), s32[]{:S(2)}) async-start(), calls=%async_computation.16 | async-start | bytes 9732096 | tf_op jit(solution)/shard_map/reduce_scatter | solution.py:343
  473.5 692.3 %reduce-scatter.17.cloned.1.call-start = ((), (), s32[]{:S(2)}) async-start(), calls=%async_computation.17 | async-start | bytes 9732096 | tf_op jit(solution)/shard_map/reduce_scatter | solution.py:343
  473.5 1.2 copy-start.4
  473.6 40.6 %copy-start = (bf16[24,768]{1,0:T(8,128)(2,1)S(1)}, bf16[24,768]{1,0:T(8,128)(2,1)}, u32[]{:S(2)}) copy-start(bf16[24,768]{1,0:T(8,128)(2,1)} %param.26) | copy-start | bytes 110596
  473.6 40.6 %copy-start.1 = (bf16[24,768]{1,0:T(8,128)(2,1)S(1)}, bf16[24,768]{1,0:T(8,128)(2,1)}, u32[]{:S(2)}) copy-start(bf16[24,768]{1,0:T(8,128)(2,1)} %param.24) | copy-start | bytes 110596
  473.6 41.2 %copy-start.6 = (f32[1,768]{1,0:T(1,128)S(1)}, f32[1,768]{1,0:T(1,128)}, u32[]{:S(2)}) copy-start(f32[1,768]{1,0:T(1,128)} %get-tuple-element.52) | copy-start | bytes 9220
  473.6 41.3 %copy-start.5 = (f32[1,768]{1,0:T(1,128)S(1)}, f32[1,768]{1,0:T(1,128)}, u32[]{:S(2)}) copy-start(f32[1,768]{1,0:T(1,128)} %get-tuple-element.53) | copy-start | bytes 9220
  473.6 41.4 %copy-start.2 = (f32[8,768]{1,0:T(8,128)S(1)}, f32[8,768]{1,0:T(8,128)}, u32[]{:S(2)}) copy-start(f32[8,768]{1,0:T(8,128)} %get-tuple-element.54) | copy-start | bytes 73732
  473.6 42.5 %copy-start.3 = (f32[1,3072]{1,0:T(1,128)S(1)}, f32[1,3072]{1,0:T(1,128)}, u32[]{:S(2)}) copy-start(f32[1,3072]{1,0:T(1,128)} %get-tuple-element.55) | copy-start | bytes 36868
  514.0 651.9 %copy-start.7 = (f32[12]{0:T(128)}, f32[12]{0:T(128)S(1)}, u32[]{:S(2)}) copy-start(f32[12]{0:T(128)S(1)} %pmax.7) | copy-start | bytes 148
Sparse Core Ops, SparseCore 0:
  10.9 56.9 all-gather.9
  70.8 52.8 all-gather.11
  126.5 52.8 all-gather.13
  182.1 52.8 all-gather.7
  237.7 62.4 all-gather.15
  303.0 61.9 all-gather.17
  470.8 98.3 reduce-scatter.10
  575.1 98.6 reduce-scatter.12
  679.6 98.5 reduce-scatter.6
  784.0 98.6 reduce-scatter.8
  889.1 135.1 reduce-scatter.14
  1030.6 135.1 reduce-scatter.16

commit v2 on v1

--- a/solution.py
+++ b/solution.py
@@ -96,22 +96,22 @@
     z_o[...] += dot(c_o[...], wo[...])
 
 
-def attn_fwd(rb, x, segr, segc, wq, wk, wv, wo, qb, vb, ob):
+def attn_fwd(rb, x, segr, segc, wall, qb, vb, ob):
     rows, d = x.shape
     seqs = rows // SEQ
     gw = 256
     groups = d // gw
     maps = seqs * (gw // HD)
     full = lambda shape: pl.BlockSpec(shape, lambda g, *_: (0,) * len(shape))
-    col = pl.BlockSpec((d, gw), lambda g, *_: (0, g))
+    col = lambda i: pl.BlockSpec((None, d, gw), lambda g, *_: (i, 0, g))
     vec = pl.BlockSpec((1, gw), lambda g, *_: (0, g))
     act = pl.BlockSpec((rows, gw), lambda g, *_: (0, g))
     return pl.pallas_call(
         attn_fwd_body,
         grid_spec=pltpu.PrefetchScalarGridSpec(
             num_scalar_prefetch=1, grid=(groups,),
-            in_specs=[full((rows, d)), full((seqs, SEQ)), full((rows, 1)), col, col, col,
-                      pl.BlockSpec((gw, d), lambda g, *_: (g, 0)), vec, vec, full((1, d))],
+            in_specs=[full((rows, d)), full((seqs, SEQ)), full((rows, 1)), col(0), col(1), col(2),
+                      pl.BlockSpec((None, gw, d), lambda g, *_: (3, g, 0)), vec, vec, full((1, d))],
             out_specs=[act, act, act, pl.BlockSpec((maps, SEQ, SEQ), lambda g, *_: (g, 0, 0)), act,
                        full((rows, d)), full((16, 128))],
             scratch_shapes=[pltpu.VMEM((seqs, SEQ, SEQ), F32), pltpu.VMEM((2, SEQ, SEQ), F32)]),
@@ -120,7 +120,7 @@
            jax.ShapeDtypeStruct((rows, d), F32), jax.ShapeDtypeStruct((16, 128), F32)],
         compiler_params=pltpu.CompilerParams(vmem_limit_bytes=VMEM_MAX),
         name="attn_fwd",
-    )(rb, x, segr, segc, wq, wk, wv, wo, qb, vb, ob)
+    )(rb, x, segr, segc, wall, wall, wall, wall, qb, vb, ob)
 
 
 def unit_rows(z):
@@ -246,7 +246,7 @@
 
 
 def attn_bwd_body(x, db, wq, wk, wv, wo, q, k, v, p, ctx, dsum,
-                  dwq, dwk, dwv, dwo, dqb, dvb, dx, dc, dq, dk, dv, dp_s, ds_s):
+                  dw, dqb, dvb, dx, dc, dq, dk, dv, dp_s, ds_s):
     g = pl.program_id(0)
     seqs = x.shape[0] // SEQ
     pairs = wq.shape[1] // 128
@@ -257,7 +257,8 @@
 
     dbv = db[...]
     dc[...] = dot_nt(dbv, wo[...]).astype(BF)
-    dwo[...] = dot_tn(ctx[...], dbv).astype(dwo.dtype)
+    part = pl.ds(pl.multiple_of(g * 256, 256), 256)
+    dw[3, part, :] = dot_tn(ctx[...], dbv).astype(dw.dtype)
     first_half = lax.broadcasted_iota(jnp.int32, (1, 128), 1) < HD
 
     def one_pair(it, _):
@@ -289,76 +290,370 @@
     dqb[...] = col_sum(dq[...].astype(F32))
     dvb[...] = col_sum(dv[...].astype(F32))
     xv = x[...]
-    dwq[...] = dot_tn(xv, dq[...]).astype(dwq.dtype)
-    dwk[...] = dot_tn(xv, dk[...]).astype(dwk.dtype)
-    dwv[...] = dot_tn(xv, dv[...]).astype(dwv.dtype)
+    dw[0, :, part] = dot_tn(xv, dq[...]).astype(dw.dtype)
+    dw[1, :, part] = dot_tn(xv, dk[...]).astype(dw.dtype)
+    dw[2, :, part] = dot_tn(xv, dv[...]).astype(dw.dtype)
     dx[...] += dot_nt(dq[...], wq[...]) + dot_nt(dk[...], wk[...]) + dot_nt(dv[...], wv[...])
 
 
-def attn_bwd(x, db, wq, wk, wv, wo, q, k, v, p, ctx, dsum, gdt):
+def attn_bwd(x, db, wall, q, k, v, p, ctx, dsum, gdt):
     rows, d = x.shape
     seqs = rows // SEQ
     gw = 256
     groups = d // gw
     maps = seqs * (gw // HD)
     full = lambda shape: pl.BlockSpec(shape, lambda g: (0,) * len(shape), pipeline_mode=pl.Buffered(1))
-    col = pl.BlockSpec((d, gw), lambda g: (0, g))
-    row = pl.BlockSpec((gw, d), lambda g: (g, 0))
+    col = lambda i: pl.BlockSpec((None, d, gw), lambda g: (i, 0, g))
+    row = pl.BlockSpec((None, gw, d), lambda g: (3, g, 0))
     vec = pl.BlockSpec((1, gw), lambda g: (0, g))
     act = pl.BlockSpec((rows, gw), lambda g: (0, g))
     sd = jax.ShapeDtypeStruct
     return pl.pallas_call(
         attn_bwd_body,
         grid=(groups,),
-        in_specs=[full((rows, d)), full((rows, d)), col, col, col, row, act, act, act,
+        in_specs=[full((rows, d)), full((rows, d)), col(0), col(1), col(2), row, act, act, act,
                   pl.BlockSpec((maps, SEQ, SEQ), lambda g: (g, 0, 0)), act, full((rows, d))],
-        out_specs=[col, col, col, row, vec, vec, pl.BlockSpec((rows, d), lambda g: (0, 0))],
-        out_shape=[sd((d, d), gdt)] * 4 + [sd((1, d), F32)] * 2 + [sd((rows, d), F32)],
+        out_specs=[full((4, d, d)), vec, vec, pl.BlockSpec((rows, d), lambda g: (0, 0))],
+        out_shape=[sd((4, d, d), gdt)] + [sd((1, d), F32)] * 2 + [sd((rows, d), F32)],
         scratch_shapes=[pltpu.VMEM((rows, gw), BF)] * 4
         + [pltpu.VMEM((2, SEQ, SEQ), F32), pltpu.VMEM((2, SEQ, SEQ), BF)],
         compiler_params=pltpu.CompilerParams(vmem_limit_bytes=VMEM_MAX),
         name="attn_bwd",
-    )(x, db, wq, wk, wv, wo, q, k, v, p, ctx, dsum)
-
-
-def per_device(tokens, segment_ids, random_blocks, clip_limit, query_weight, query_bias, key_weight, value_weight,
+    )(x, db, wall, wall, wall, wall, q, k, v, p, ctx, dsum)
+MESH_ID = pl.DeviceIdType.MESH
+
+
+def place():
+    me = lax.axis_index("dp")
+    c, x, y, z = me % 2, (me // 2) % 2, (me // 4) % 2, me // 8
+    fc, fx, fy = 1 - 2 * c, 2 * (1 - 2 * x), 4 * (1 - 2 * y)
+    d1 = fx * (1 - c) + fy * c
+    d2 = fy * (1 - c) + fx * c
+    zs = (0, 8 * (1 - 2 * (z % 2)), 16 * (1 - 2 * (z // 2)), 8 * (3 - 2 * z))
+    return me, fc, d1, d2, zs
+
+
+def meet(me, fc, d1, d2, zs):
+    barrier = pltpu.get_barrier_semaphore()
+    for off in (fc, d1, d2) + zs[1:]:
+        pl.semaphore_signal(barrier, inc=1, device_id=(me + off,), device_id_type=MESH_ID)
+    pl.semaphore_wait(barrier, 6)
+
+
+def unit_of(ref, lead, unit):
+    return ref.at[:, unit] if lead else ref.at[unit]
+
+
+class Gather:
+    def __init__(self, where, own, out, send, recv):
+        self.where, self.own, self.out, self.send, self.recv = where, own, out, send, recv
+        self.lead = len(out.shape) == 4
+
+    def copy(self, slot, unit, dest, own=False):
+        return pltpu.make_async_remote_copy(
+            src_ref=self.own if own else unit_of(self.out, self.lead, unit), dst_ref=unit_of(self.out, self.lead, unit),
+            send_sem=self.send.at[slot], recv_sem=self.recv.at[slot], device_id=(dest,), device_id_type=MESH_ID)
+
+    def begin(self):
+        me, fc, d1, d2, zs = self.where
+        for k in (1, 2, 3):
+            self.copy(k, me, me + zs[k], True).start()
+        self.copy(4, me, me + d1, True).start()
+        self.copy(8, me, me + d2, True).start()
+        self.copy(16, me, me + fc, True).start()
+
+    def landed(self, slot):
+        me, fc, d1, d2, zs = self.where
+        k = slot % 4
+        group = slot // 4
+        off = (0, d1, d2, d1 + d2, fc, fc + d2, fc + d1, fc + d1 + d2)[group]
+        unit = me + zs[k] + off
+        self.copy(slot, unit, me).wait_recv()
+        return unit
+
+    def step(self, slot):
+        me, fc, d1, d2, zs = self.where
+        k, group = slot % 4, slot // 4
+        unit = self.landed(slot)
+        if group == 0:
+            self.copy(4 + k, unit, me + d1).start()
+            self.copy(8 + k, unit, me + d2).start()
+        if group == 1:
+            self.copy(12 + k, unit, me + d2).start()
+        if group < 4:
+            self.copy(16 + slot, unit, me + fc).start()
+
+    ORDER = (1, 4, 2, 5, 8, 3, 6, 9, 7, 12, 10, 13, 11, 14, 15)
+
+    def finish(self):
+        me = self.where[0]
+        for slot in range(16, 32):
+            self.landed(slot)
+        for slot in range(1, 32):
+            self.copy(slot, me, me, slot in (1, 2, 3, 4, 8, 16)).wait_send()
+
+
+def gather_body(*refs):
+    n = (len(refs) - 3) // 2
+    own, out = refs[:n], refs[n:2 * n]
+    send, recv, local = refs[2 * n:]
+    where = place()
+    me = where[0]
+    mine = [pltpu.make_async_copy(own[a], unit_of(out[a], len(out[a].shape) == 4, me), local.at[a]) for a in range(n)]
+    for m in mine:
+        m.start()
+    meet(*where)
+    flows = [Gather(where, own[a], out[a], send.at[a], recv.at[a]) for a in range(n)]
+    for f in flows:
+        f.begin()
+    for slot in Gather.ORDER:
+        for f in flows:
+            f.step(slot)
+    for f in flows:
+        f.finish()
+    for m in mine:
+        m.wait()
+
+
+def gather_all(parts, n, cid):
+    na = len(parts)
+    return pl.pallas_call(
+        gather_body,
+        in_specs=[pl.BlockSpec(memory_space=pltpu.VMEM)] * na,
+        out_specs=[pl.BlockSpec(memory_space=pl.ANY)] * na,
+        out_shape=[jax.ShapeDtypeStruct(p.shape[:-2] + (n,) + p.shape[-2:], p.dtype) for p in parts],
+        scratch_shapes=[pltpu.SemaphoreType.DMA((na, 32)), pltpu.SemaphoreType.DMA((na, 32)),
+                        pltpu.SemaphoreType.DMA((na,))],
+        compiler_params=pltpu.CompilerParams(collective_id=cid, has_side_effects=True, vmem_limit_bytes=16 << 20),
+        name="gather_all",
+    )(*parts)
+
+
+class Scatter:
+    def __init__(self, where, grad, own, rp, r1, r2, rz, sems, lsem):
+        self.where, self.grad, self.own = where, grad, own
+        self.rp, self.r1, self.r2, self.rz, self.sems, self.lsem = rp, r1, r2, rz, sems, lsem
+
+    def remote(self, src, dst, slot, off):
+        return pltpu.make_async_remote_copy(
+            src_ref=src, dst_ref=dst, send_sem=self.sems.at[0, slot], recv_sem=self.sems.at[1, slot],
+            device_id=(self.where[0] + off,), device_id_type=MESH_ID)
+
+    def begin(self):
+        me, fc, d1, d2, zs = self.where
+        lead = len(self.grad.shape) == 4
+        for a in (1, 0):
+            for b in (1, 0):
+                for k in range(4):
+                    self.remote(unit_of(self.grad, lead, me + fc + a * d2 + b * d1 + zs[k]), self.rp.at[a, b, k],
+                                a, fc).start()
+            for b in (1, 0):
+                for k in range(4):
+                    pltpu.make_async_copy(unit_of(self.grad, lead, me + a * d1 + b * d2 + zs[k]),
+                                          self.own.at[a, b, k], self.lsem.at[a]).start()
+
+    def pair(self, a):
+        me, fc, d1, d2, zs = self.where
+        self.remote(self.own.at[a], self.rp.at[a], a, fc).wait_recv()
+        pltpu.make_async_copy(self.own.at[a], self.rp.at[a], self.lsem.at[a]).wait()
+        for b in (1, 0):
+            self.own[a, b] = (self.own[a, b].astype(F32) + self.rp[a, b].astype(F32)).astype(BF)
+            if a == 1:
+                self.remote(self.own.at[1, b], self.r1.at[b], 2 + b, d1).start()
+
+    def first(self, b):
+        me, fc, d1, d2, zs = self.where
+        self.remote(self.own.at[1, b], self.r1.at[b], 2 + b, d1).wait_recv()
+        self.own[0, b] = (self.own[0, b].astype(F32) + self.r1[b].astype(F32)).astype(BF)
+        if b == 1:
+            self.remote(self.own.at[0, 1], self.r2, 4, d2).start()
+
+    def second(self):
+        me, fc, d1, d2, zs = self.where
+        self.remote(self.own.at[0, 1], self.r2, 4, d2).wait_recv()
+        for k in (1, 2, 3):
+            self.own[0, 0, k] = (self.own[0, 0, k].astype(F32) + self.r2[k].astype(F32)).astype(BF)
+            self.remote(self.own.at[0, 0, k], self.rz.at[k - 1], 4 + k, zs[k]).start()
+
+    def last(self):
+        me, fc, d1, d2, zs = self.where
+        total = self.own[0, 0, 0].astype(F32) + self.r2[0].astype(F32)
+        for k in (1, 2, 3):
+            self.remote(self.own.at[0, 0, k], self.rz.at[k - 1], 4 + k, zs[k]).wait_recv()
+            total = total + self.rz[k - 1].astype(F32)
+        return total
+
+    def drain(self):
+        me, fc, d1, d2, zs = self.where
+        for a in (1, 0):
+            self.remote(self.own.at[a], self.rp.at[a], a, fc).wait_send()
+        for b in (1, 0):
+            self.remote(self.own.at[1, b], self.r1.at[b], 2 + b, d1).wait_send()
+        self.remote(self.own.at[0, 1], self.r2, 4, d2).wait_send()
+        for k in (1, 2, 3):
+            self.remote(self.own.at[0, 0, k], self.rz.at[k - 1], 4 + k, zs[k]).wait_send()
+
+
+class Vectors:
+    def __init__(self, where, held, got, sems):
+        self.where, self.held, self.got, self.sems = where, held, got, sems
+
+    def remote(self, src, slot, off):
+        return pltpu.make_async_remote_copy(
+            src_ref=self.held.at[src], dst_ref=self.got.at[slot], send_sem=self.sems.at[0, slot],
+            recv_sem=self.sems.at[1, slot], device_id=(self.where[0] + off,), device_id_type=MESH_ID)
+
+    def merge(self, a, b):
+        row = lax.broadcasted_iota(jnp.int32, a.shape, 0)
+        return jnp.where(row == 12, jnp.maximum(a, b), a + b)
+
+    def step(self, i):
+        me, fc, d1, d2, zs = self.where
+        offs = (fc, d1, d2)
+        if i > 0:
+            self.remote(i - 1, i - 1, offs[i - 1]).wait_recv()
+            self.held[i] = self.merge(self.held[i - 1], self.got[i - 1])
+        if i < 3:
+            self.remote(i, i, offs[i]).start()
+        else:
+            for k in (1, 2, 3):
+                self.remote(3, 2 + k, zs[k]).start()
+
+    def last(self):
+        me, fc, d1, d2, zs = self.where
+        total = self.held[3]
+        for k in (1, 2, 3):
+            self.remote(3, 2 + k, zs[k]).wait_recv()
+            total = self.merge(total, self.got[2 + k])
+        for i, off in enumerate((fc, d1, d2)):
+            self.remote(i, i, off).wait_send()
+        for k in (1, 2, 3):
+            self.remote(3, 2 + k, zs[k]).wait_send()
+        return total
+
+
+def scatter_body(na, *refs):
+    grads, vec = refs[:na], refs[na]
+    outs, vout = refs[na + 1:2 * na + 1], refs[2 * na + 1]
+    rest = refs[2 * na + 2:]
+    bufs, (held, got, sems, lsems, vsems) = rest[:5 * na], rest[5 * na:]
+    where = place()
+    flows = [Scatter(where, grads[a], *bufs[5 * a:5 * a + 5], sems.at[a], lsems.at[a]) for a in range(na)]
+    small = Vectors(where, held, got, vsems)
+    held[0] = vec[...]
+    meet(*where)
+    small.step(0)
+    for f in flows:
+        f.begin()
+    small.step(1)
+    for f in flows:
+        f.pair(1)
+    small.step(2)
+    for f in flows:
+        f.pair(0)
+    small.step(3)
+    for f in flows:
+        f.first(1)
+    for i, f in enumerate(flows):
+        f.first(0)
+        if i > 0:
+            flows[i - 1].second()
+    flows[-1].second()
+    vout[...] = small.last()
+    for f, o in zip(flows, outs):
+        o[...] = f.last()
+    for f in flows:
+        f.drain()
+
+
+def scatter_all(grads, vec, cid):
+    na = len(grads)
+    shapes = [g.shape[:-3] + g.shape[-2:] for g in grads]
+    bufs = []
+    for s in shapes:
+        bufs += [pltpu.VMEM((2, 2, 4) + s, BF)] * 2 + [pltpu.VMEM((2, 4) + s, BF), pltpu.VMEM((4,) + s, BF),
+                                                         pltpu.VMEM((3,) + s, BF)]
+    vm = pl.BlockSpec(memory_space=pltpu.VMEM)
+    return pl.pallas_call(
+        partial(scatter_body, na),
+        in_specs=[pl.BlockSpec(memory_space=pl.ANY)] * na + [vm],
+        out_specs=[vm] * (na + 1),
+        out_shape=[jax.ShapeDtypeStruct(s, F32) for s in shapes] + [jax.ShapeDtypeStruct(vec.shape, F32)],
+        scratch_shapes=bufs + [pltpu.VMEM((4,) + vec.shape, F32), pltpu.VMEM((6,) + vec.shape, F32),
+                               pltpu.SemaphoreType.DMA((na, 2, 8)), pltpu.SemaphoreType.DMA((na, 2)),
+                               pltpu.SemaphoreType.DMA((2, 6))],
+        compiler_params=pltpu.CompilerParams(collective_id=cid, has_side_effects=True, vmem_limit_bytes=VMEM_MAX),
+        name="scatter_all",
+    )(*grads, vec)
+
+
+def vectors_part(me, n, vecs, inner_bias):
+    part = vecs[0].shape[0]
+    d = part * n
+    rows = jnp.tile(jnp.stack(vecs), (1, n))
+    rows = jnp.where(lax.broadcasted_iota(jnp.int32, rows.shape, 1) // part == me, rows, 0)
+    flat = jnp.tile(inner_bias, n)
+    flat = jnp.where(lax.broadcasted_iota(jnp.int32, flat.shape, 0) // inner_bias.shape[0] == me, flat, 0)
+    flat = flat.reshape(-1, d)
+    rest = jnp.zeros((16 - rows.shape[0] - flat.shape[0], d), BF)
+    return jnp.concatenate([rows, flat, rest], axis=0)
+
+
+def per_device(n, tokens, segment_ids, random_blocks, clip_limit, query_weight, query_bias, key_weight, value_weight,
                value_bias, output_weight, output_bias, attn_gain, attn_shift, inner_weight, inner_bias,
                outer_weight, outer_bias, final_gain, final_shift, out_cotangent):
     heads = random_blocks.shape[0]
     rows, d = tokens.shape
-    gather = lambda a: lax.all_gather(a, "dp", axis=0, tiled=True)
-    wq, wk, wv, wo = map(gather, (query_weight, key_weight, value_weight, output_weight))
-    wi, wu = gather(inner_weight), gather(outer_weight)
+    ff = inner_weight.shape[1]
+    near = n == 32 and query_weight.shape[0] % 8 == 0
+    me = lax.axis_index("dp")
+    stack = jnp.stack([query_weight, key_weight, value_weight, output_weight])
     names = (query_bias, value_bias, output_bias, attn_gain, attn_shift, outer_bias, final_gain, final_shift)
     part = query_bias.shape[0]
-    vecs = gather(jnp.concatenate(names + (inner_bias,))[None])
-    n = vecs.shape[0]
-    qb, vb, ob, ag, ash, bo, fg, fs = (vecs[:, i * part:(i + 1) * part].reshape(1, n * part) for i in range(8))
-    bi = vecs[:, 8 * part:].reshape(1, -1)
+    vec_part = vectors_part(me, n, names, inner_bias)
+    if near:
+        wall, vecs, wi, wu = gather_all((stack, vec_part, inner_weight, outer_weight), n, 0)
+        wall, wi, wu = wall.reshape(4, d, d), wi.reshape(d, ff), wu.reshape(ff, d)
+        vecs = jnp.sum(vecs.astype(F32), axis=0)
+    else:
+        wall = lax.all_gather(stack, "dp", axis=1, tiled=True)
+        wi, wu = (lax.all_gather(a, "dp", axis=0, tiled=True) for a in (inner_weight, outer_weight))
+        vecs = lax.psum(vec_part.astype(F32), "dp")
+    qb, vb, ob, ag, ash, bo, fg, fs = (vecs[i:i + 1] for i in range(8))
+    bi = vecs[8:8 + ff // d].reshape(1, ff)
+    gdt = BF if near else F32
     q, k, v, p, ctx, z, hm = attn_fwd(
-        random_blocks.reshape(-1), tokens, segment_ids.reshape(-1, SEQ), segment_ids.reshape(-1, 1),
-        wq, wk, wv, wo, qb, vb, ob)
-    out, dsum, db, dwi, dwu, dbi, small = ffn(z, out_cotangent, wi, wu, bi, bo, ag, ash, fg, fs, F32)
-    dwq, dwk, dwv, dwo, dqb, dvb, dx = attn_bwd(tokens, db, wq, wk, wv, wo, q, k, v, p, ctx, dsum, F32)
-    scatter = lambda a: lax.psum_scatter(a, "dp", scatter_dimension=0, tiled=True)
-    dwu, dwi, dwo, dwq, dwk, dwv = (scatter(a) for a in (dwu, dwi, dwo, dwq, dwk, dwv))
-    vec = lambda a: a.reshape(n, -1)
-    smalls = jnp.concatenate([vec(dqb), vec(dvb), vec(small[5]), vec(small[3]), vec(small[4]), vec(small[2]),
-                              vec(small[0]), vec(small[1]), vec(dbi)], axis=1)
-    smalls = scatter(smalls)[0]
-    dqb, dvb, dob, dag, dash, dbo, dfg, dfs = (smalls[i * part:(i + 1) * part] for i in range(8))
-    dbi = smalls[8 * part:]
-    head_maxima = lax.pmax(hm[:heads, 0], "dp")
+        random_blocks.reshape(-1), tokens, segment_ids.reshape(-1, SEQ), segment_ids.reshape(-1, 1), wall, qb, vb, ob)
+    out, dsum, db, dwi, dwu, dbi, small = ffn(z, out_cotangent, wi, wu, bi, bo, ag, ash, fg, fs, gdt)
+    dwall, dqb, dvb, dx = attn_bwd(tokens, db, wall, q, k, v, p, ctx, dsum, gdt)
+    hm_row = jnp.pad(hm[:heads, 0], (0, d - heads))[None]
+    mine = jnp.concatenate([dqb, dvb, small[5:6], small[3:4], small[4:5], small[2:3], small[0:2],
+                            dbi.reshape(-1, d), hm_row, jnp.zeros((16 - 9 - ff // d, d), F32)], axis=0)
+    if near:
+        dwu, dwi, dwall, total = scatter_all(
+            (dwu.reshape(n, -1, d), dwi.reshape(n, -1, ff), dwall.reshape(4, n, -1, d)), mine, 1)
+    else:
+        scatter = lambda a, at: lax.psum_scatter(a, "dp", scatter_dimension=at, tiled=True)
+        dwu, dwi, dwall = scatter(dwu, 0), scatter(dwi, 0), scatter(dwall, 1)
+        total = jnp.where(lax.broadcasted_iota(jnp.int32, mine.shape, 0) == 12, lax.pmax(mine, "dp"),
+                          lax.psum(mine, "dp"))
+    vec8 = lax.dynamic_slice(total, (0, me * part), (8, part))
+    dqb, dvb, dob, dag, dash, dbo, dfg, dfs = (vec8[i] for i in range(8))
+    wide = inner_bias.shape[0]
+    dbi = lax.dynamic_slice(total[8:8 + ff // d].reshape(-1), (me * wide,), (wide,))
+    head_maxima = total[12, :heads]
     limit = clip_limit[0].astype(F32)
     factor = jnp.sqrt(jnp.minimum(1.0, limit / jnp.maximum(head_maxima, 1.0)))
     columns = jnp.repeat(factor, HD)[None, :]
     cq = (query_weight.astype(F32) * columns).astype(BF)
     ck = (key_weight.astype(F32) * columns).astype(BF)
-    return (out, dx, dwq, dqb, dwk, dwv, dvb, dwo, dob, dag, dash, dwi, dbi, dwu, dbo, dfg, dfs, cq, ck, head_maxima)
+    return (out, dx, dwall[0], dqb, dwall[1], dwall[2], dvb, dwall[3], dob, dag, dash, dwi, dbi, dwu, dbo, dfg, dfs,
+            cq, ck, head_maxima)
 
 
 def solution(mesh):
     mat, vec, rep = P("dp", None), P("dp"), P()
     in_specs = (mat, vec, rep, rep, mat, vec, mat, mat, vec, mat, vec, vec, vec, mat, vec, mat, vec, vec, vec, mat)
     out_specs = (mat, mat, mat, vec, mat, mat, vec, mat, vec, vec, vec, mat, vec, mat, vec, vec, vec, mat, mat, rep)
-    return jax.shard_map(per_device, mesh=mesh, in_specs=in_specs, out_specs=out_specs, check_vma=False)
+    return jax.shard_map(partial(per_device, mesh.shape["dp"]), mesh=mesh, in_specs=in_specs, out_specs=out_specs,
+                         check_vma=False)

time: 1170 us -> 341 us (0.29)
  waiting for transfers between devices: 878 us -> 0 us
  Pallas kernels: 136 us -> 304 us
  blocking collectives: 122 us -> 0 us
  between operations: 15.1 us -> 1.44 us
    reduce_scatter x6 -> x0, waiting for transfers between devices: 607 us -> none  [per_device(): lax.psum_scatter(a, 'dp', scatter_dimension=0, tiled=True)]
    all_gather x6 -> x0, waiting for transfers between devices: 264 us -> none  [per_device(): gather = lambda a: lax.all_gather(a, 'dp', axis=0, tiled=True)]
    pallas_call x0 -> x2, Pallas kernels: none -> 171 us  [the longest x1 94.6 us: scatter_all(): pl.pallas_call(partial(scatter_body, na), in_specs=[pl.BlockSpec(memory_s...]
    unnamed x2 -> x0, blocking collectives: 83.1 us -> none
    pmax x1 -> x0, blocking collectives: 39.1 us -> none  [per_device(): head_maxima = lax.pmax(hm[:heads, 0], 'dp')]
    unnamed x19 -> x17, local copies, waits for them, and re-layouts: 1.12 us -> 14.4 us
  transfers between devices with their start and end apart: 12 -> 0, of which waited for: 11 -> 0; matrix products, arithmetic and copies ran while one was open for 2% -> 0% of each run, Pallas kernels for 3% -> 0%
where the time goes in v2:
time: 341 us; the launch traced here: 340 us
  Pallas kernels  304 us (89%)
  local copies, waits for them, and re-layouts  29.8 us (9%)
  other arithmetic  5.04 us (1%)
    pallas_call x1, Pallas kernels, scatter_all(): pl.pallas_call(partial(scatter_body, na), in_specs=[pl.BlockSpec(memory_s...  94.6 us
    pallas_call x1, Pallas kernels, gather_all(): pl.pallas_call(gather_body, in_specs=[pl.BlockSpec(memory_space=pltpu.VME...  76.3 us
    pallas_call x1, Pallas kernels, ffn(): pl.pallas_call(ffn_body, in_specs=[vm] * 10, out_specs=[vm] * 7, out_shap...  60.1 us
    pallas_call x1, Pallas kernels, attn_bwd(): pl.pallas_call(attn_bwd_body, grid=(groups,), in_specs=[full((rows, d)),...  43 us
    pallas_call x1, Pallas kernels, attn_fwd(): pl.pallas_call(attn_fwd_body, grid_spec=pltpu.PrefetchScalarGridSpec(num_...  29.9 us
    unnamed x17, local copies, waits for them, and re-layouts  14.4 us

profile of v2, /device:TPU:0, one launch (start us, length us, event | category | flops | bytes accessed | tf_op | source)
XLA Modules:
  0.0 340.3 jit_solution(17328205075032856561)
XLA Ops:
  0.7 0.8 stack.55
  1.5 0.1 tile.21
  1.7 0.7 tile.22
  2.3 0.1 tile.23
  2.5 0.8 pad_maximum_fusion.refs_0_
  3.3 0.0 copy-start.3
  3.3 0.9 copy-done.3
  4.2 0.0 copy-start.4
  4.2 0.9 copy-done.4
  5.1 76.3 %gather_all.1 = (bf16[4,32,24,768]{3,2,1,0:T(8,128)(2,1)S(1)}, bf16[32,16,768]{2,1,0:T(8,128)(2,1)S(1)}, bf16[32,24,3072]{2,1,0:T(8,128)(2,1)S(1)}, bf16[32,96,768]{2,1,0:T(8,128)(2,1)S(1)}) custom-call(bf16[4,24,768]{2,1,0:T(8,128)(2,1)S(1)} %pad_maximum_fusion.refs_0_, bf16[16,768]{1,0:T(8,128)(2,1)S(1)} %pad_maximum_fusion.1.refs_1_, ...), custom_call_target="tpu_custom_call" | custom-call | tf_op jit(solution)/shard_map/gather_all/pallas_call | solution.py:420
  81.5 0.0 copy-start
  81.5 2.1 copy-done
  83.5 0.0 copy-start.1
  83.5 2.1 copy-done.1
  85.7 0.0 copy-start.2
  85.7 2.2 copy-done.2
  87.8 0.1 convert_reduce_fusion
  88.0 0.0 copy-start.5
  88.0 0.6 copy-done.5
  88.6 0.6 fusion.7
  89.2 1.7 copy.41.segc
  90.9 0.8 copy.40
  91.7 0.7 reshape.89.rb
  92.4 1.3 reshape.90.segr
  93.7 29.9 %attn_fwd.1 = (bf16[1024,768]{1,0:T(8,128)(2,1)}, bf16[1024,768]{1,0:T(8,128)(2,1)}, bf16[1024,768]{1,0:T(8,128)(2,1)}, bf16[24,512,512]{2,1,0:T(8,128)(2,1)}, b...) custom-call(s32[216]{0:T(256)} %reshape.89.rb, bf16[1024,768]{1,0:T(8,128)(2,1)} %x.5, ...), custom_call_target="tpu_custom_call" | custom-call | tf_op jit(solution)/shard_map/attn_fwd/pallas_call | solution.py:109
  123.6 0.7 slice_bitcast_fusion.4
  124.4 0.6 copy.42
  125.0 60.1 %ffn.1 = (bf16[1024,768]{1,0:T(8,128)(2,1)}, f32[1024,768]{1,0:T(8,128)}, bf16[1024,768]{1,0:T(8,128)(2,1)}, bf16[768,3072]{1,0:T(8,128)(2,1)}, bf16[3072,768]{1...) custom-call(f32[1024,768]{1,0:T(8,128)} %get-tuple-element.48.z, bf16[1024,768]{1,0:T(8,128)(2,1)} %cot.1, ...), custom_call_target="tpu_custom_call" | custom-call | tf_op jit(solution)/shard_map/ffn/pallas_call | solution.py:235
  185.1 43.0 %attn_bwd.1 = (bf16[4,768,768]{2,1,0:T(8,128)(2,1)}, f32[1,768]{1,0:T(1,128)}, f32[1,768]{1,0:T(1,128)}, f32[1024,768]{1,0:T(8,128)}) custom-call(bf16[1024,768]{1,0:T(8,128)(2,1)} %x.5, bf16[1024,768]{1,0:T(8,128)(2,1)} %get-tuple-element.52.db, bf16[4,768,768]{2,1,0:T(8,128)(2,1)} %bitcast.55, bf16[4,768,768]{2,1,0:T(8,128)(2,1)} %bitcast.56, ...), custom_call_target="tpu_custom_call" | custom-call | tf_op jit(solution)/shard_map/attn_bwd/pallas_call | solution.py:311
  228.1 0.5 broadcast.45
  228.6 1.4 reduce.5
  230.0 0.8 fusion.8
  230.8 0.8 fusion.9
  231.6 0.8 slice_reduce_fusion
  232.5 2.0 concatenate.7.refs_3_
  234.4 94.6 %scatter_all.1 = (f32[96,768]{1,0:T(8,128)}, f32[24,3072]{1,0:T(8,128)}, f32[4,24,768]{2,1,0:T(8,128)}, f32[16,768]{1,0:T(8,128)}) custom-call(bf16[32,96,768]{2,1,0:T(8,128)(2,1)} %bitcast.62, bf16[32,24,3072]{2,1,0:T(8,128)(2,1)} %bitcast.61, bf16[4,32,24,768]{3,2,1,0:T(8,128)(2,1)} %bitcast.63, f32[16,768]{1,0:T(8,128)} %concatenate.7.refs_3_), custom_call_target="tpu_custom_call" | custom-call | tf_op jit(solution)/shard_map/scatter_all/pallas_call | solution.py:577
  329.1 1.7 slice_bitcast_fusion
  331.5 1.2 minimum_sqrt_fusion
  332.6 0.1 broadcast_in_dim.22
  332.7 0.1 mul.24
  332.8 1.4 multiply_convert_fusion
  334.2 0.7 slice.109
  335.0 0.6 dynamic_slice.7
  335.6 0.8 constant_dynamic-slice_fusion
  336.3 0.5 slice_bitcast_fusion.6
  336.9 1.7 copy.46
  338.6 1.7 copy.47
  (12 shorter events, 0.1 us)
Async XLA Ops:
  3.3 0.9 copy-start.3
  4.2 0.9 copy-start.4
  81.5 2.1 copy-start
  83.5 2.1 copy-start.1
  85.7 2.2 copy-start.2
  88.0 0.6 copy-start.5

commit v3 on v1

v3 whole, which is shorter than its diff:
```python
from functools import partial
import math

import jax
import jax.numpy as jnp
from jax import lax
from jax.experimental import pallas as pl
from jax.experimental.pallas import tpu as pltpu
from jax.sharding import PartitionSpec as P

HD = 64
BLOCK = 64
SEQ = 512
GW = 256
BF = jnp.bfloat16
F32 = jnp.float32
LOW = -1e30
VMEM_MAX = 67043328
MESH_ID = pl.DeviceIdType.MESH
QB, VB, OB, AG, ASH, BO, FG, FS, BI, TOP = 0, 1, 2, 3, 4, 5, 6, 7, 8, 12


def dot(a, b):
    return jnp.dot(a, b, preferred_element_type=F32)


def dot_nt(a, b):
    return lax.dot_general(a, b, (((1,), (1,)), ((), ())), preferred_element_type=F32)


def dot_tn(a, b):
    return lax.dot_general(a, b, (((0,), (0,)), ((), ())), preferred_element_type=F32)


def col_sum(v):
    return jnp.sum(v, axis=0, keepdims=True)


def first_half():
    return lax.broadcasted_iota(jnp.int32, (1, 128), 1) < HD


def same_document(segr, segc, bias):
    for s in range(segr.shape[0]):
        kseg = segr[s:s + 1, :]
        for c in range(SEQ // BLOCK):
            qseg = segc[s * SEQ + c * BLOCK:s * SEQ + (c + 1) * BLOCK, :]
            bias[s, c * BLOCK:(c + 1) * BLOCK, :] = jnp.where((qseg == kseg) & (kseg != 0), 0.0, LOW)


def pair_forward(g, it, rb, q, k, v, p, ctx, hm, bias, s_s):
    pairs = GW // 128
    s, pair = it // pairs, it % pairs
    rows = pl.ds(pl.multiple_of(s * SEQ, SEQ), SEQ)
    lanes = pl.ds(pl.multiple_of(pair * 128, 128), 128)
    lane_block = lax.broadcasted_iota(jnp.int32, (1, SEQ), 1) // BLOCK
    half = first_half()
    last = SEQ // BLOCK - 2
    qp, kp, vp = q[rows, lanes], k[rows, lanes], v[rows, lanes]
    outs = []
    for j in range(2):
        head = g * (2 * pairs) + pair * 2 + j
        m = s * (2 * pairs) + pair * 2 + j
        mine = half if j == 0 else jnp.logical_not(half)
        s_s[j] = dot_nt(jnp.where(mine, qp * 0.125, 0).astype(BF), kp)
        at = head * (6 * 3)
        miss1 = 18 - (rb[at] + rb[at + 1] + rb[at + 2])
        miss6 = 10 - (rb[at + 15] + rb[at + 16] + rb[at + 17])
        skip1 = jnp.where(lane_block == miss1, LOW, 0.0)
        skip6 = jnp.where(lane_block == miss6, LOW, 0.0)
        tops = None
        for c in range(SEQ // BLOCK):
            cr = slice(c * BLOCK, (c + 1) * BLOCK)
            sv = s_s[j, cr, :] + bias[s, cr, :]
            if c == 1:
                sv = sv + skip1
            if c == last:
                sv = sv + skip6
            top = jnp.max(sv, axis=1, keepdims=True)
            live = top > -1e29
            e = jnp.exp(sv - jnp.where(live, top, 0.0))
            total = jnp.sum(e, axis=1, keepdims=True) + jnp.where(live, 0.0, 1.0)
            p[m, cr, :] = (e * (1.0 / total)).astype(BF)
            tops = top if tops is None else jnp.maximum(tops, top)
        top = jnp.max(tops, axis=0, keepdims=True)
        hm[pl.ds(head, 1), :] = jnp.maximum(hm[pl.ds(head, 1), :], top)
        outs.append(dot(p[m], vp))
    ctx[rows, lanes] = jnp.where(half, outs[0], outs[1]).astype(BF)


def pair_backward(it, q, k, v, p, dc, dq, dk, dv, dp_s, ds_s):
    pairs = GW // 128
    s, pair = it // pairs, it % pairs
    rows = pl.ds(pl.multiple_of(s * SEQ, SEQ), SEQ)
    lanes = pl.ds(pl.multiple_of(pair * 128, 128), 128)
    half = first_half()
    qp, kp, vp, dcp = q[rows, lanes], k[rows, lanes], v[rows, lanes], dc[rows, lanes]
    dqs, dks, dvs = [], [], []
    for j in range(2):
        mine = half if j == 0 else jnp.logical_not(half)
        m = s * (2 * pairs) + pair * 2 + j
        dp_s[j] = dot_nt(jnp.where(mine, dcp, 0).astype(BF), vp)
        for c in range(SEQ // BLOCK):
            cr = slice(c * BLOCK, (c + 1) * BLOCK)
            pv = p[m, cr, :].astype(F32)
            sl = dp_s[j, cr, :]
            mean = jnp.sum(pv * sl, axis=1, keepdims=True)
            ds_s[j, cr, :] = (pv * (sl - mean)).astype(BF)
        dqs.append(dot(ds_s[j], kp))
        dks.append(dot_tn(ds_s[j], qp))
        dvs.append(dot_tn(p[m], dcp))
    dq[rows, lanes] = (jnp.where(half, dqs[0], dqs[1]) * 0.125).astype(BF)
    dk[rows, lanes] = (jnp.where(half, dks[0], dks[1]) * 0.125).astype(BF)
    dv[rows, lanes] = jnp.where(half, dvs[0], dvs[1]).astype(BF)


def unit_rows(z):
    mean = jnp.mean(z, axis=-1, keepdims=True)
    c = z - mean
    inv = lax.rsqrt(jnp.mean(c * c, axis=-1, keepdims=True) + 1e-12)
    return c * inv, inv


def norm_back(up, unit, inv, gain):
    e = up * gain
    spread = jnp.mean(e, axis=-1, keepdims=True)
    along = jnp.mean(e * unit, axis=-1, keepdims=True)
    return inv * (e - spread - unit * along)


def ffn_body(z, cot, wi, wo, vecs, out, dsum, db, dwi, dwo, small, fl, act, gp, acc, do):
    rows, d = z.shape
    ff = wi.shape[1]
    rt, et = 512, 128
    k0, k1 = math.sqrt(2.0 / math.pi), 0.044715
    row = lambda i: vecs[i:i + 1, :]
    small[...] = jnp.zeros(small.shape, F32)

    def prep(i, _):
        r = pl.ds(pl.multiple_of(i * et, et), et)
        unit, _inv = unit_rows(z[r, :])
        first = unit * row(AG) + row(ASH)
        fl[r, :] = first.astype(BF)
        acc[r, :] = first + row(BO)
        return 0

    lax.fori_loop(0, rows // et, prep, 0)

    def up(i, _):
        j = i // (rows // rt)
        r = pl.ds(pl.multiple_of((i % (rows // rt)) * rt, rt), rt)
        c = pl.ds(pl.multiple_of(j * d, d), d)
        u = dot(fl[r, :], wi[:, c]) + vecs[pl.ds(BI + j, 1), :]
        u2 = u * u
        t = jnp.tanh(u * (k0 + (k0 * k1) * u2))
        h = 0.5 + 0.5 * t
        a = (u * h).astype(BF)
        act[r, c] = a
        gp[r, c] = (h + (0.5 * u) * (1.0 - t * t) * (k0 + (3.0 * k0 * k1) * u2)).astype(gp.dtype)
        acc[r, :] += dot(a, wo[c, :])
        return 0

    lax.fori_loop(0, (ff // d) * (rows // rt), up, 0)

    def mid(i, _):
        r = pl.ds(pl.multiple_of(i * et, et), et)
        unit, inv = unit_rows(acc[r, :])
        out[r, :] = (unit * row(FG) + row(FS)).astype(BF)
        upv = cot[r, :].astype(F32)
        small[FG:FG + 1, :] += col_sum(upv * unit)
        small[FS:FS + 1, :] += col_sum(upv)
        ds = norm_back(upv, unit, inv, row(FG))
        dsl = ds.astype(BF)
        do[r, :] = dsl
        acc[r, :] = ds
        small[BO:BO + 1, :] += col_sum(dsl.astype(F32))
        return 0

    lax.fori_loop(0, rows // et, mid, 0)

    def down(j, _):
        c = pl.ds(pl.multiple_of(j * d, d), d)
        dwo[c, :] = dot_tn(act[:, c], do[...]).astype(dwo.dtype)
        sums = None
        for i in range(rows // rt):
            r = slice(i * rt, (i + 1) * rt)
            di = dot_nt(do[r, :], wo[c, :]) * gp[r, c].astype(F32)
            dil = di.astype(BF)
            act[r, c] = dil
            s = col_sum(dil.astype(F32))
            sums = s if sums is None else sums + s
            acc[r, :] += dot_nt(dil, wi[:, c])
        small[pl.ds(BI + j, 1), :] = sums
        dwi[:, c] = dot_tn(fl[...], act[:, c]).astype(dwi.dtype)
        return 0

    lax.fori_loop(0, ff // d, down, 0)

    def tail(i, _):
        r = pl.ds(pl.multiple_of(i * et, et), et)
        unit, inv = unit_rows(z[r, :])
        df = acc[r, :]
        small[AG:AG + 1, :] += col_sum(df * unit)
        small[ASH:ASH + 1, :] += col_sum(df)
        ds = norm_back(df, unit, inv, row(AG))
        dsum[r, :] = ds
        dsl = ds.astype(BF)
        db[r, :] = dsl
        small[OB:OB + 1, :] += col_sum(dsl.astype(F32))
        return 0

    lax.fori_loop(0, rows // et, tail, 0)


def ffn(z, cot, wi, wo, vecs, gdt):
    rows, d = z.shape
    ff = wi.shape[1]
    sd = jax.ShapeDtypeStruct
    vm = pl.BlockSpec(memory_space=pltpu.VMEM)
    return pl.pallas_call(
        ffn_body,
        in_specs=[vm] * 5,
        out_specs=[vm] * 6,
        out_shape=[sd((rows, d), BF), sd((rows, d), F32), sd((rows, d), BF), sd((d, ff), gdt), sd((ff, d), gdt),
                   sd((16, d), F32)],
        scratch_shapes=[pltpu.VMEM((rows, d), BF), pltpu.VMEM((rows, ff), BF), pltpu.VMEM((rows, ff), BF),
                        pltpu.VMEM((rows, d), F32), pltpu.VMEM((rows, d), BF)],
        compiler_params=pltpu.CompilerParams(vmem_limit_bytes=VMEM_MAX),
        name="ffn",
    )(z, cot, wi, wo, vecs)


def place():
    me = lax.axis_index("dp")
    c, x, y, z = me % 2, (me // 2) % 2, (me // 4) % 2, me // 8
    fc, fx, fy = 1 - 2 * c, 2 * (1 - 2 * x), 4 * (1 - 2 * y)
    d1 = fx * (1 - c) + fy * c
    d2 = fy * (1 - c) + fx * c
    zs = (0, 8 * (1 - 2 * (z % 2)), 16 * (1 - 2 * (z // 2)), 8 * (3 - 2 * z))
    return me, fc, d1, d2, zs


def meet(me, fc, d1, d2, zs):
    barrier = pltpu.get_barrier_semaphore()
    for off in (fc, d1, d2) + zs[1:]:
        pl.semaphore_signal(barrier, inc=1, device_id=(me + off,), device_id_type=MESH_ID)
    pl.semaphore_wait(barrier, 6)


def unit_of(ref, unit):
    return ref.at[:, unit] if len(ref.shape) == 4 else ref.at[unit]


class Gather:
    ORDER = (1, 4, 2, 5, 8, 3, 6, 9, 7, 12, 10, 13, 11, 14, 15)

    def __init__(self, where, own, out, send, recv):
        self.where, self.own, self.out, self.send, self.recv = where, own, out, send, recv

    def copy(self, slot, unit, dest, own=False):
        return pltpu.make_async_remote_copy(
            src_ref=self.own if own else unit_of(self.out, unit), dst_ref=unit_of(self.out, unit),
            send_sem=self.send.at[slot], recv_sem=self.recv.at[slot], device_id=(dest,), device_id_type=MESH_ID)

    def begin_z(self):
        me, fc, d1, d2, zs = self.where
        for k in (1, 2, 3):
            self.copy(k, me, me + zs[k], True).start()

    def begin_xy(self):
        me, fc, d1, d2, zs = self.where
        self.copy(4, me, me + d1, True).start()
        self.copy(8, me, me + d2, True).start()
        self.copy(16, me, me + fc, True).start()

    def landed(self, slot):
        me, fc, d1, d2, zs = self.where
        unit = me + zs[slot % 4] + (0, d1, d2, d1 + d2, fc, fc + d2, fc + d1, fc + d1 + d2)[slot // 4]
        self.copy(slot, unit, me).wait_recv()
        return unit

    def step(self, slot):
        me, fc, d1, d2, zs = self.where
        k, group = slot % 4, slot // 4
        unit = self.landed(slot)
        if group == 0:
            self.copy(4 + k, unit, me + d1).start()
            self.copy(8 + k, unit, me + d2).start()
        if group == 1:
            self.copy(12 + k, unit, me + d2).start()
        self.copy(16 + slot, unit, me + fc).start()

    def finish(self):
        for slot in range(16, 32):
            self.landed(slot)

    def drain(self):
        me = self.where[0]
        for slot in range(1, 32):
            self.copy(slot, me, me, slot in (1, 2, 3, 4, 8, 16)).wait_send()


LATE = ((1, 0), (4, 1), (2, 2), (5, 3), (8, 4), (3, 5), (6, 6), (9, 7), (7, 8), (12, 9), (10, 10), (13, 11))


def front_body(rb, x, segr, segc, stack, vpart, wis, wus,
               wall_o, wi_o, wu_o, vec_o, q_o, k_o, v_o, p_o, c_o, z_o, hm_o,
               wall, vg, bias, s_s, q_s, k_s, v_s, p_s, c_s, send, recv, local, outs):
    where = place()
    me = where[0]
    rows, d = x.shape
    groups = d // GW
    steps = (rows // SEQ) * (GW // 128)
    owns, targets = (stack, vpart, wis, wus), (wall, vg, wi_o, wu_o)
    mine = [pltpu.make_async_copy(o, unit_of(t, me), local.at[i]) for i, (o, t) in enumerate(zip(owns, targets))]
    for m in mine:
        m.start()
    meet(*where)
    flows = [Gather(where, o, t, send.at[i], recv.at[i]) for i, (o, t) in enumerate(zip(owns, targets))]
    early, late = flows[:2], flows[2:]
    for f in early:
        f.begin_z()
    for f in early:
        f.begin_xy()
    same_document(segr, segc, bias)
    for slot in Gather.ORDER:
        for f in early:
            f.step(slot)
        if slot == 3:
            for f in late:
                f.begin_z()
    for f in late:
        f.begin_xy()
    for f in early:
        f.finish()
    mine[0].wait()
    mine[1].wait()
    keep = pltpu.make_async_copy(wall, wall_o, outs.at[5])
    keep.start()
    vec = jnp.sum(vg[...].astype(F32), axis=0)
    vec_o[...] = vec
    hm_o[...] = jnp.full(hm_o.shape, LOW, F32)
    z_o[...] = x[...].astype(F32) + vec_o[OB:OB + 1, :]

    def put(g, i):
        src = (q_s, k_s, v_s, c_s)[i].at[g] if i < 4 else p_s.at[g]
        return pltpu.make_async_copy(src, (q_o, k_o, v_o, c_o, p_o)[i].at[g], outs.at[i])

    def group(g, _):
        cols = pl.ds(pl.multiple_of(g * GW, GW), GW)
        weight = lambda i: wall[i, :, :, cols].reshape(d, GW)
        xv = x[...]
        q_s[g] = (dot(xv, weight(0)) + vec_o[QB:QB + 1, cols]).astype(BF)
        k_s[g] = dot(xv, weight(1)).astype(BF)
        v_s[g] = (dot(xv, weight(2)) + vec_o[VB:VB + 1, cols]).astype(BF)

        def one_pair(it, _):
            pair_forward(g, it, rb, q_s.at[g], k_s.at[g], v_s.at[g], p_s.at[g], c_s.at[g], hm_o, bias, s_s)
            for slot, when in LATE:
                @pl.when(g * steps + it == when)
                def _():
                    for f in late:
                        f.step(slot)
            return 0

        lax.fori_loop(0, steps, one_pair, 0)
        for i in range(5):
            put(g, i).start()
        return 0

    lax.fori_loop(0, groups, group, 0)
    wo = wall[3].reshape(d, d)
    for g in range(groups):
        z_o[...] += dot(c_s[g], wo[g * GW:(g + 1) * GW, :])
    done = [slot for slot, _ in LATE]
    for slot in Gather.ORDER:
        if slot not in done:
            for f in late:
                f.step(slot)
    for f in late:
        f.finish()
    mine[2].wait()
    mine[3].wait()
    for f in flows:
        f.drain()
    keep.wait()
    for g in range(groups):
        for i in range(5):
            put(g, i).wait()


def front(rb, x, segr, segc, stack, vpart, wis, wus, n):
    rows, d = x.shape
    groups = d // GW
    maps = (rows // SEQ) * (GW // HD)
    sd = jax.ShapeDtypeStruct
    vm, hbm = pl.BlockSpec(memory_space=pltpu.VMEM), pl.BlockSpec(memory_space=pl.ANY)
    whole = lambda a: a.shape[:-2] + (n,) + a.shape[-2:]
    act = (groups, rows, GW)
    return pl.pallas_call(
        front_body,
        in_specs=[pl.BlockSpec(memory_space=pltpu.SMEM)] + [vm] * 7,
        out_specs=[hbm] * 3 + [vm] + [hbm] * 5 + [vm] * 2,
        out_shape=[sd(whole(stack), BF), sd(whole(wis), BF), sd(whole(wus), BF), sd((16, d), F32),
                   sd(act, BF), sd(act, BF), sd(act, BF), sd((groups, maps, SEQ, SEQ), BF), sd(act, BF),
                   sd((rows, d), F32), sd((16, 128), F32)],
        scratch_shapes=[pltpu.VMEM(whole(stack), BF), pltpu.VMEM(whole(vpart), BF),
                        pltpu.VMEM((rows // SEQ, SEQ, SEQ), F32), pltpu.VMEM((2, SEQ, SEQ), F32),
                        pltpu.VMEM(act, BF), pltpu.VMEM(act, BF), pltpu.VMEM(act, BF),
                        pltpu.VMEM((groups, maps, SEQ, SEQ), BF), pltpu.VMEM(act, BF),
                        pltpu.SemaphoreType.DMA((4, 32)), pltpu.SemaphoreType.DMA((4, 32)),
                        pltpu.SemaphoreType.DMA((4,)), pltpu.SemaphoreType.DMA((6,))],
        compiler_params=pltpu.CompilerParams(collective_id=0, has_side_effects=True, vmem_limit_bytes=VMEM_MAX),
        name="front",
    )(rb, x, segr, segc, stack, vpart, wis, wus)


class Scatter:
    def __init__(self, where, grad, own, rp, r1, r2, rz, sems, lsem):
        self.where, self.grad, self.own = where, grad, own
        self.rp, self.r1, self.r2, self.rz, self.sems, self.lsem = rp, r1, r2, rz, sems, lsem

    def remote(self, src, dst, slot, off):
        return pltpu.make_async_remote_copy(
            src_ref=src, dst_ref=dst, send_sem=self.sems.at[0, slot], recv_sem=self.sems.at[1, slot],
            device_id=(self.where[0] + off,), device_id_type=MESH_ID)

    def begin(self):
        me, fc, d1, d2, zs = self.where
        for a in (1, 0):
            for b in (1, 0):
                for k in range(4):
                    self.remote(unit_of(self.grad, me + fc + a * d2 + b * d1 + zs[k]), self.rp.at[a, b, k], a, fc).start()
            if self.own is not None:
                for b in (1, 0):
                    for k in range(4):
                        pltpu.make_async_copy(unit_of(self.grad, me + a * d1 + b * d2 + zs[k]), self.own.at[a, b, k],
                                              self.lsem.at[a]).start()

    def pair(self, a):
        me, fc, d1, d2, zs = self.where
        self.remote(self.rp.at[a], self.rp.at[a], a, fc).wait_recv()
        if self.own is not None:
            pltpu.make_async_copy(self.own.at[a], self.own.at[a], self.lsem.at[a]).wait()
        for b in (1, 0):
            for k in range(4):
                held = self.own[a, b, k] if self.own is not None else (
                    unit_of(self.grad, me + a * d1 + b * d2 + zs[k])[...])
                self.rp[a, b, k] = (held.astype(F32) + self.rp[a, b, k].astype(F32)).astype(BF)
            if a == 1:
                self.remote(self.rp.at[1, b], self.r1.at[b], 2 + b, d1).start()

    def first(self, b):
        me, fc, d1, d2, zs = self.where
        self.remote(self.rp.at[1, b], self.r1.at[b], 2 + b, d1).wait_recv()
        self.rp[0, b] = (self.rp[0, b].astype(F32) + self.r1[b].astype(F32)).astype(BF)
        if b == 1:
            self.remote(self.rp.at[0, 1], self.r2, 4, d2).start()

    def second(self):
        me, fc, d1, d2, zs = self.where
        self.remote(self.rp.at[0, 1], self.r2, 4, d2).wait_recv()
        for k in (1, 2, 3):
            self.rp[0, 0, k] = (self.rp[0, 0, k].astype(F32) + self.r2[k].astype(F32)).astype(BF)
            self.remote(self.rp.at[0, 0, k], self.rz.at[k - 1], 4 + k, zs[k]).start()

    def last(self):
        me, fc, d1, d2, zs = self.where
        total = self.rp[0, 0, 0].astype(F32) + self.r2[0].astype(F32)
        for k in (1, 2, 3):
            self.remote(self.rp.at[0, 0, k], self.rz.at[k - 1], 4 + k, zs[k]).wait_recv()
            total = total + self.rz[k - 1].astype(F32)
        return total

    def drain(self):
        me, fc, d1, d2, zs = self.where
        for a in (1, 0):
            self.remote(self.rp.at[a], self.rp.at[a], a, fc).wait_send()
        for b in (1, 0):
            self.remote(self.rp.at[1, b], self.r1.at[b], 2 + b, d1).wait_send()
        self.remote(self.rp.at[0, 1], self.r2, 4, d2).wait_send()
        for k in (1, 2, 3):
            self.remote(self.rp.at[0, 0, k], self.rz.at[k - 1], 4 + k, zs[k]).wait_send()


def scatter_buffers(shape, own):
    bufs = [pltpu.VMEM((2, 2, 4) + shape, BF)] if own else []
    return bufs + [pltpu.VMEM((2, 2, 4) + shape, BF), pltpu.VMEM((2, 4) + shape, BF), pltpu.VMEM((4,) + shape, BF),
                   pltpu.VMEM((3,) + shape, BF)]


class Vectors:
    def __init__(self, where, held, got, sems):
        self.where, self.held, self.got, self.sems = where, held, got, sems

    def remote(self, src, slot, off):
        return pltpu.make_async_remote_copy(
            src_ref=self.held.at[src], dst_ref=self.got.at[slot], send_sem=self.sems.at[0, slot],
            recv_sem=self.sems.at[1, slot], device_id=(self.where[0] + off,), device_id_type=MESH_ID)

    def merge(self, a, b):
        row = lax.broadcasted_iota(jnp.int32, a.shape, 0)
        return jnp.where(row == TOP, jnp.maximum(a, b), a + b)

    def step(self, i):
        me, fc, d1, d2, zs = self.where
        offs = (fc, d1, d2)
        if i > 0:
            self.remote(i - 1, i - 1, offs[i - 1]).wait_recv()
            self.held[i] = self.merge(self.held[i - 1], self.got[i - 1])
        if i < 3:
            self.remote(i, i, offs[i]).start()
        else:
            for k in (1, 2, 3):
                self.remote(3, 2 + k, zs[k]).start()

    def last(self):
        me, fc, d1, d2, zs = self.where
        total = self.held[3]
        for k in (1, 2, 3):
            self.remote(3, 2 + k, zs[k]).wait_recv()
            total = self.merge(total, self.got[2 + k])
        for i, off in enumerate((fc, d1, d2)):
            self.remote(i, i, off).wait_send()
        for k in (1, 2, 3):
            self.remote(3, 2 + k, zs[k]).wait_send()
        return total


def back_body(x_h, db_h, dsum_h, wall_h, q_h, k_h, v_h, c_h, p_h, small, hm, gu, gi,
              dx, o_q, o_k, o_v, o_o, o_i, o_u, vout, *rest):
    (x, db, wall, q, k, v, c, p, dc, dq, dk, dv, dp_s, ds_s, go, gg, held, got, sems, lsems, vsems, isem) = rest[:22]
    bufs = rest[22:]
    where = place()
    rows, d = x.shape
    groups = d // GW
    n = go.shape[0]
    steps = (rows // SEQ) * (GW // 128)
    small_flow = Vectors(where, held, got, vsems)
    up_flow = Scatter(where, gu, *bufs[0:5], sems.at[0], lsems.at[0])
    in_flow = Scatter(where, gi, *bufs[5:10], sems.at[1], lsems.at[1])
    out_flow = Scatter(where, go, None, *bufs[10:14], sems.at[2], None)
    group_flow = [Scatter(where, gg.at[g], None, *bufs[14 + 4 * g:18 + 4 * g], sems.at[3 + g], None)
                  for g in range(groups)]

    def fetch(i):
        pairs = ((db_h, db), (wall_h.at[3], wall.at[3]), (c_h, c), (dsum_h, dx), (x_h, x),
                 (wall_h.at[pl.ds(0, 3)], wall.at[pl.ds(0, 3)]))
        return pltpu.make_async_copy(*pairs[i], isem.at[i])

    def fetch_group(g, i):
        src = (v_h, q_h, k_h, p_h)[i].at[g]
        dst = ((v, q, k)[i].at[g] if i < 3 else p.at[lax.rem(g, 2)])
        return pltpu.make_async_copy(src, dst, isem.at[6 + 4 * lax.rem(g, 2) + i])

    for i in range(3):
        fetch(i).start()
    for i in range(4):
        fetch_group(0, i).start()
    for i in range(3, 6):
        fetch(i).start()
    meet(*where)
    up_flow.begin()
    in_flow.begin()
    for i in range(3):
        fetch(i).wait()

    dbv = db[...]
    go[...] = jnp.concatenate([dot_tn(c[g], dbv) for g in range(groups)], axis=0).astype(BF).reshape(go.shape)
    out_flow.begin()

    events = {
        0: [(up_flow.pair, 1)], 1: [(in_flow.pair, 1)], 2: [(up_flow.pair, 0)], 3: [(in_flow.pair, 0)],
        4: [(out_flow.pair, 1)], 5: [(up_flow.first, 1), (out_flow.pair, 0)], 6: [(in_flow.first, 1)],
        7: [(up_flow.first, 0)], 8: [(in_flow.first, 0), (group_flow[0].pair, 1)],
        9: [(out_flow.first, 1), (up_flow.second,)], 10: [(out_flow.first, 0), (group_flow[0].pair, 0)],
        11: [(in_flow.second,)],
    }

    def group(g, _):
        cols = pl.ds(pl.multiple_of(g * GW, GW), GW)
        weight = lambda i: wall[i, :, cols]
        for i in range(4):
            fetch_group(g, i).wait()

        @pl.when(g + 1 < groups)
        def _():
            for i in range(4):
                fetch_group(g + 1, i).start()

        dc[...] = dot_nt(db[...], wall[3, cols, :]).astype(BF)

        def one_pair(it, _):
            pair_backward(it, q.at[g], k.at[g], v.at[g], p.at[lax.rem(g, 2)], dc, dq, dk, dv, dp_s, ds_s)
            for when, todo in events.items():
                @pl.when(g * steps + it == when)
                def _():
                    for fn, *a in todo:
                        fn(*a)
            return 0

        lax.fori_loop(0, steps, one_pair, 0)
        held[0, QB:QB + 1, cols] = col_sum(dq[...].astype(F32))
        held[0, VB:VB + 1, cols] = col_sum(dv[...].astype(F32))

        @pl.when(g == 0)
        def _():
            for i in range(3, 6):
                fetch(i).wait()

        xv = x[...]
        for i, part in enumerate((dq, dk, dv)):
            gg[g, i] = dot_tn(xv, part[...]).astype(BF).reshape(n, d // n, GW)
        for i in range(groups):
            @pl.when(g == i)
            def _():
                group_flow[i].begin()
        dx[...] += dot_nt(dq[...], weight(0)) + dot_nt(dk[...], weight(1)) + dot_nt(dv[...], weight(2))
        return 0

    held[0] = small[...]
    lax.fori_loop(0, groups, group, 0)
    diag = lax.broadcasted_iota(jnp.int32, hm.shape, 0) == lax.broadcasted_iota(jnp.int32, hm.shape, 1)
    held[0, TOP:TOP + 1, 0:128] = jnp.sum(jnp.where(diag, hm[...], 0.0), axis=0, keepdims=True)
    small_flow.step(0)
    g1, g2 = group_flow[1:]
    g1.pair(1)
    g2.pair(1)
    small_flow.step(1)
    out_flow.second()
    group_flow[0].first(1)
    g1.pair(0)
    g2.pair(0)
    small_flow.step(2)
    g1.first(1)
    g2.first(1)
    small_flow.step(3)
    group_flow[0].first(0)
    g1.first(0)
    g2.first(0)
    for f in group_flow:
        f.second()
    o_u[...] = up_flow.last()
    o_i[...] = in_flow.last()
    o_o[...] = out_flow.last()
    for g, f in enumerate(group_flow):
        t = f.last()
        for i, o in enumerate((o_q, o_k, o_v)):
            o[:, g * GW:(g + 1) * GW] = t[i]
    vout[...] = small_flow.last()
    for f in [up_flow, in_flow, out_flow] + group_flow:
        f.drain()


def back(x, db, dsum, wall, q, k, v, c, p, small, hm, gu, gi):
    rows, d = x.shape
    groups, n = d // GW, gu.shape[0]
    maps = (rows // SEQ) * (GW // HD)
    r, ru, ff = d // n, gu.shape[1], gi.shape[2]
    sd = jax.ShapeDtypeStruct
    vm, hbm = pl.BlockSpec(memory_space=pltpu.VMEM), pl.BlockSpec(memory_space=pl.ANY)
    act = pltpu.VMEM((groups, rows, GW), BF)
    one = pltpu.VMEM((rows, GW), BF)
    bufs = scatter_buffers((ru, d), True) + scatter_buffers((r, ff), True) + scatter_buffers((r, d), False)
    for _ in range(groups):
        bufs += scatter_buffers((3, r, GW), False)
    return pl.pallas_call(
        back_body,
        in_specs=[hbm] * 9 + [vm] * 2 + [hbm] * 2,
        out_specs=[vm] * 8,
        out_shape=[sd((rows, d), F32)] + [sd((r, d), F32)] * 4 + [sd((r, ff), F32), sd((ru, d), F32), sd((16, d), F32)],
        scratch_shapes=[pltpu.VMEM((rows, d), BF), pltpu.VMEM((rows, d), BF), pltpu.VMEM((4, d, d), BF),
                        act, act, act, act, pltpu.VMEM((2, maps, SEQ, SEQ), BF), one, one, one, one,
                        pltpu.VMEM((2, SEQ, SEQ), F32), pltpu.VMEM((2, SEQ, SEQ), BF),
                        pltpu.VMEM((n, r, d), BF), pltpu.VMEM((groups, 3, n, r, GW), BF),
                        pltpu.VMEM((4, 16, d), F32), pltpu.VMEM((6, 16, d), F32),
                        pltpu.SemaphoreType.DMA((3 + groups, 2, 8)), pltpu.SemaphoreType.DMA((2, 2)),
                        pltpu.SemaphoreType.DMA((2, 6)), pltpu.SemaphoreType.DMA((14,))] + bufs,
        compiler_params=pltpu.CompilerParams(collective_id=1, has_side_effects=True, vmem_limit_bytes=VMEM_MAX),
        name="back",
    )(x, db, dsum, wall, q, k, v, c, p, small, hm, gu, gi)


def attn_fwd_body(rb, x, segr, segc, wq, wk, wv, wo, vecs, q, k, v, p, c, z, hm, bias, s_s):
    g = pl.program_id(0)

    @pl.when(g == 0)
    def _():
        same_document(segr, segc, bias)
        hm[...] = jnp.full(hm.shape, LOW, F32)
        z[...] = x[...].astype(F32) + vecs[OB:OB + 1, :]

    cols = pl.ds(pl.multiple_of(g * GW, GW), GW)
    xv = x[...]
    q[...] = (dot(xv, wq[...]) + vecs[QB:QB + 1, cols]).astype(BF)
    k[...] = dot(xv, wk[...]).astype(BF)
    v[...] = (dot(xv, wv[...]) + vecs[VB:VB + 1, cols]).astype(BF)

    def one_pair(it, _):
        pair_forward(g, it, rb, q, k, v, p, c, hm, bias, s_s)
        return 0

    lax.fori_loop(0, x.shape[0] // SEQ * (GW // 128), one_pair, 0)
    z[...] += dot(c[...], wo[...])


def attn_fwd(rb, x, segr, segc, wall, vecs):
    rows, d = x.shape
    groups, seqs = d // GW, rows // SEQ
    maps = seqs * (GW // HD)
    full = lambda shape: pl.BlockSpec(shape, lambda g, *_: (0,) * len(shape))
    col = lambda i: pl.BlockSpec((None, d, GW), lambda g, *_: (i, 0, g))
    act = pl.BlockSpec((None, rows, GW), lambda g, *_: (g, 0, 0))
    sd = jax.ShapeDtypeStruct
    return pl.pallas_call(
        attn_fwd_body,
        grid_spec=pltpu.PrefetchScalarGridSpec(
            num_scalar_prefetch=1, grid=(groups,),
            in_specs=[full((rows, d)), full((seqs, SEQ)), full((rows, 1)), col(0), col(1), col(2),
                      pl.BlockSpec((None, GW, d), lambda g, *_: (3, g, 0)), full((16, d))],
            out_specs=[act, act, act, pl.BlockSpec((None, maps, SEQ, SEQ), lambda g, *_: (g, 0, 0, 0)), act,
                       full((rows, d)), full((16, 128))],
            scratch_shapes=[pltpu.VMEM((seqs, SEQ, SEQ), F32), pltpu.VMEM((2, SEQ, SEQ), F32)]),
        out_shape=[sd((groups, rows, GW), BF)] * 3
        + [sd((groups, maps, SEQ, SEQ), BF), sd((groups, rows, GW), BF), sd((rows, d), F32), sd((16, 128), F32)],
        compiler_params=pltpu.CompilerParams(vmem_limit_bytes=VMEM_MAX),
        name="attn_fwd",
    )(rb, x, segr, segc, wall, wall, wall, wall, vecs)


def attn_bwd_body(x, db, wq, wk, wv, wo, q, k, v, p, c, dsum, dw, dqb, dvb, dx, dc, dq, dk, dv, dp_s, ds_s):
    g = pl.program_id(0)

    @pl.when(g == 0)
    def _():
        dx[...] = dsum[...]

    dbv = db[...]
    cols = pl.ds(pl.multiple_of(g * GW, GW), GW)
    dc[...] = dot_nt(dbv, wo[...]).astype(BF)
    dw[3, cols, :] = dot_tn(c[...], dbv).astype(dw.dtype)

    def one_pair(it, _):
        pair_backward(it, q, k, v, p, dc, dq, dk, dv, dp_s, ds_s)
        return 0

    lax.fori_loop(0, x.shape[0] // SEQ * (GW // 128), one_pair, 0)
    dqb[...] = col_sum(dq[...].astype(F32))
    dvb[...] = col_sum(dv[...].astype(F32))
    xv = x[...]
    for i, part in enumerate((dq, dk, dv)):
        dw[i, :, cols] = dot_tn(xv, part[...]).astype(dw.dtype)
    dx[...] += dot_nt(dq[...], wq[...]) + dot_nt(dk[...], wk[...]) + dot_nt(dv[...], wv[...])


def attn_bwd(x, db, wall, q, k, v, p, c, dsum, gdt):
    rows, d = x.shape
    groups = d // GW
    maps = (rows // SEQ) * (GW // HD)
    full = lambda shape: pl.BlockSpec(shape, lambda g: (0,) * len(shape), pipeline_mode=pl.Buffered(1))
    col = lambda i: pl.BlockSpec((None, d, GW), lambda g: (i, 0, g))
    vec = pl.BlockSpec((1, GW), lambda g: (0, g))
    act = pl.BlockSpec((None, rows, GW), lambda g: (g, 0, 0))
    sd = jax.ShapeDtypeStruct
    return pl.pallas_call(
        attn_bwd_body,
        grid=(groups,),
        in_specs=[full((rows, d)), full((rows, d)), col(0), col(1), col(2),
                  pl.BlockSpec((None, GW, d), lambda g: (3, g, 0)), act, act, act,
                  pl.BlockSpec((None, maps, SEQ, SEQ), lambda g: (g, 0, 0, 0)), act, full((rows, d))],
        out_specs=[full((4, d, d)), vec, vec, full((rows, d))],
        out_shape=[sd((4, d, d), gdt)] + [sd((1, d), F32)] * 2 + [sd((rows, d), F32)],
        scratch_shapes=[pltpu.VMEM((rows, GW), BF)] * 4
        + [pltpu.VMEM((2, SEQ, SEQ), F32), pltpu.VMEM((2, SEQ, SEQ), BF)],
        compiler_params=pltpu.CompilerParams(vmem_limit_bytes=VMEM_MAX),
        name="attn_bwd",
    )(x, db, wall, wall, wall, wall, q, k, v, p, c, dsum)


def far_layer(n, rb, tokens, segr, segc, cot, stack, vec_part, inner_weight, outer_weight):
    d, ff = tokens.shape[1], inner_weight.shape[1]
    wall = lax.all_gather(stack, "dp", axis=1, tiled=True)
    wi, wu = (lax.all_gather(a, "dp", axis=0, tiled=True) for a in (inner_weight, outer_weight))
    vecs = lax.psum(vec_part.astype(F32), "dp")
    q, k, v, p, c, z, hm = attn_fwd(rb, tokens, segr, segc, wall, vecs)
    out, dsum, db, dwi, dwu, small = ffn(z, cot, wi, wu, vecs, F32)
    dwall, dqb, dvb, dx = attn_bwd(tokens, db, wall, q, k, v, p, c, dsum, F32)
    mine = small.at[QB:QB + 1].set(dqb).at[VB:VB + 1].set(dvb).at[TOP, :hm.shape[0]].set(hm[:, 0])
    scatter = lambda a, at: lax.psum_scatter(a, "dp", scatter_dimension=at, tiled=True)
    dwu, dwi, dwall = scatter(dwu, 0), scatter(dwi, 0), scatter(dwall, 1)
    row = lax.broadcasted_iota(jnp.int32, mine.shape, 0)
    total = jnp.where(row == TOP, lax.pmax(mine, "dp"), lax.psum(mine, "dp"))
    return out, dx, dwall[0], dwall[1], dwall[2], dwall[3], dwi, dwu, total


def near_layer(n, rb, tokens, segr, segc, cot, stack, vec_part, inner_weight, outer_weight):
    d, ff = tokens.shape[1], inner_weight.shape[1]
    wall, wi, wu, vecs, q, k, v, p, c, z, hm = front(rb, tokens, segr, segc, stack, vec_part, inner_weight,
                                                     outer_weight, n)
    out, dsum, db, dwi, dwu, small = ffn(z, cot, wi.reshape(d, ff), wu.reshape(ff, d), vecs, BF)
    dx, dwq, dwk, dwv, dwo, dwi, dwu, total = back(
        tokens, db, dsum, wall.reshape(4, d, d), q, k, v, c, p, small, hm, dwu.reshape(n, -1, d), dwi.reshape(n, -1, ff))
    return out, dx, dwq, dwk, dwv, dwo, dwi, dwu, total


def vectors_part(me, n, vecs, inner_bias):
    part = vecs[0].shape[0]
    d = part * n
    rows = jnp.tile(jnp.stack(vecs), (1, n))
    rows = jnp.where(lax.broadcasted_iota(jnp.int32, rows.shape, 1) // part == me, rows, 0)
    flat = jnp.tile(inner_bias, n)
    flat = jnp.where(lax.broadcasted_iota(jnp.int32, flat.shape, 0) // inner_bias.shape[0] == me, flat, 0)
    flat = flat.reshape(-1, d)
    rest = jnp.zeros((16 - rows.shape[0] - flat.shape[0], d), BF)
    return jnp.concatenate([rows, flat, rest], axis=0)


def per_device(n, tokens, segment_ids, random_blocks, clip_limit, query_weight, query_bias, key_weight, value_weight,
               value_bias, output_weight, output_bias, attn_gain, attn_shift, inner_weight, inner_bias,
               outer_weight, outer_bias, final_gain, final_shift, out_cotangent):
    heads = random_blocks.shape[0]
    d, ff = tokens.shape[1], inner_weight.shape[1]
    me = lax.axis_index("dp")
    stack = jnp.stack([query_weight, key_weight, value_weight, output_weight])
    names = (query_bias, value_bias, output_bias, attn_gain, attn_shift, outer_bias, final_gain, final_shift)
    part, wide = query_bias.shape[0], inner_bias.shape[0]
    layer = near_layer if n == 32 and query_weight.shape[0] % 8 == 0 else far_layer
    out, dx, dwq, dwk, dwv, dwo, dwi, dwu, total = layer(
        n, random_blocks.reshape(-1), tokens, segment_ids.reshape(-1, SEQ), segment_ids.reshape(-1, 1), out_cotangent,
        stack, vectors_part(me, n, names, inner_bias), inner_weight, outer_weight)
    vec8 = lax.dynamic_slice(total, (0, me * part), (8, part))
    dqb, dvb, dob, dag, dash, dbo, dfg, dfs = (vec8[i] for i in range(8))
    dbi = lax.dynamic_slice(total[BI:BI + ff // d].reshape(-1), (me * wide,), (wide,))
    head_maxima = total[TOP, :heads]
    limit = clip_limit[0].astype(F32)
    factor = jnp.sqrt(jnp.minimum(1.0, limit / jnp.maximum(head_maxima, 1.0)))
    columns = jnp.repeat(factor, HD)[None, :]
    cq = (query_weight.astype(F32) * columns).astype(BF)
    ck = (key_weight.astype(F32) * columns).astype(BF)
    return (out, dx, dwq, dqb, dwk, dwv, dvb, dwo, dob, dag, dash, dwi, dbi, dwu, dbo, dfg, dfs, cq, ck, head_maxima)


def solution(mesh):
    mat, vec, rep = P("dp", None), P("dp"), P()
    in_specs = (mat, vec, rep, rep, mat, vec, mat, mat, vec, mat, vec, vec, vec, mat, vec, mat, vec, vec, vec, mat)
    out_specs = (mat, mat, mat, vec, mat, mat, vec, mat, vec, vec, vec, mat, vec, mat, vec, vec, vec, mat, mat, rep)
    return jax.shard_map(partial(per_device, mesh.shape["dp"]), mesh=mesh, in_specs=in_specs, out_specs=out_specs,
                         check_vma=False)
```

time: 1170 us -> 257 us (0.22)
  waiting for transfers between devices: 878 us -> 0 us
  blocking collectives: 122 us -> 0 us
  Pallas kernels: 136 us -> 233 us
  between operations: 15.1 us -> 1.4 us
    reduce_scatter x6 -> x0, waiting for transfers between devices: 607 us -> none  [per_device(): lax.psum_scatter(a, 'dp', scatter_dimension=0, tiled=True)]
    all_gather x6 -> x0, waiting for transfers between devices: 264 us -> none  [per_device(): gather = lambda a: lax.all_gather(a, 'dp', axis=0, tiled=True)]
    pallas_call x3, Pallas kernels: 136 us -> 233 us  [the longest x1 95.3 us: back(): pl.pallas_call(back_body, in_specs=[hbm] * 9 + [vm] * 2 + [hbm] * 2, out_...]
    unnamed x2 -> x0, blocking collectives: 83.1 us -> none
    pmax x1 -> x0, blocking collectives: 39.1 us -> none  [per_device(): head_maxima = lax.pmax(hm[:heads, 0], 'dp')]
  transfers between devices with their start and end apart: 12 -> 0, of which waited for: 11 -> 0; matrix products, arithmetic and copies ran while one was open for 2% -> 0% of each run, Pallas kernels for 3% -> 0%
where the time goes in v3:
time: 257 us; the launch traced here: 256 us
  Pallas kernels  233 us (91%)
  local copies, waits for them, and re-layouts  16.8 us (7%)
  other arithmetic  4.8 us (2%)
    pallas_call x1, Pallas kernels, back(): pl.pallas_call(back_body, in_specs=[hbm] * 9 + [vm] * 2 + [hbm] * 2, out_...  95.3 us
    pallas_call x1, Pallas kernels, front(): pl.pallas_call(front_body, in_specs=[pl.BlockSpec(memory_space=pltpu.SMEM...  80.5 us
    pallas_call x1, Pallas kernels, ffn(): pl.pallas_call(ffn_body, in_specs=[vm] * 5, out_specs=[vm] * 6, out_shape...  57.4 us
    unnamed x20, local copies, waits for them, and re-layouts  8.64 us

profile of v3, /device:TPU:0, one launch (start us, length us, event | category | flops | bytes accessed | tf_op | source)
XLA Modules:
  0.0 256.2 jit_solution(9643412807522478601)
XLA Ops:
  0.7 0.8 stack.55
  1.5 0.1 tile.21
  1.7 0.7 tile.22
  2.3 0.1 tile.23
  2.5 0.6 pad_maximum_fusion.1.vpart
  3.1 1.7 copy.41.segc
  4.8 1.5 pad_maximum_fusion.stack
  6.3 0.8 copy.40
  7.1 0.7 reshape.80.rb
  7.8 1.3 reshape.81.segr
  9.1 80.5 %front.1 = (bf16[4,32,24,768]{3,2,1,0:T(8,128)(2,1)}, bf16[32,24,3072]{2,1,0:T(8,128)(2,1)}, bf16[32,96,768]{2,1,0:T(8,128)(2,1)}, f32[16,768]{1,0:T(8,128)}, bf...) custom-call(s32[216]{0:T(256)} %reshape.80.rb, ...), custom_call_target="tpu_custom_call" | custom-call | tf_op jit(solution)/shard_map/front/pallas_call | solution.py:400
  89.6 57.4 %ffn.1 = (bf16[1024,768]{1,0:T(8,128)(2,1)}, f32[1024,768]{1,0:T(8,128)}, bf16[1024,768]{1,0:T(8,128)(2,1)}, bf16[768,3072]{1,0:T(8,128)(2,1)}, bf16[3072,768]{1,0:T(8,128)(2,1)}, /*index=5*/f32[16,768]{1,0:T(8,128)}) custom-call(f32[1024,768]{1,0:T(8,128)} %get-tuple-element.45.z, bf16[1024,768]{1,0:T(8,128)(2,1)} %cot.1, bf16[768,3072]{1,0:T(8,128)(2,1)} %bitcast.41, ...), custom_call_target="tpu_custom_call" | custom-call | tf_op jit(solution)/shard_map/ffn/pallas_call | solution.py:220
  147.0 95.3 %back.1 = (f32[1024,768]{1,0:T(8,128)}, f32[24,768]{1,0:T(8,128)}, f32[24,768]{1,0:T(8,128)}, f32[24,768]{1,0:T(8,128)}, f32[24,768]{1,0:T(8,128)}, /*index=5*/f...) custom-call(bf16[1024,768]{1,0:T(8,128)(2,1)} %x_h.1, bf16[1024,768]{1,0:T(8,128)(2,1)} %get-tuple-element.50.db_h, ...), custom_call_target="tpu_custom_call" | custom-call | tf_op jit(solution)/shard_map/back/pallas_call | solution.py:667
  243.0 1.2 minimum_sqrt_fusion
  244.2 0.1 broadcast_in_dim.14
  244.2 0.1 mul.24
  244.3 1.4 multiply_convert_fusion
  245.7 0.7 slice.35
  246.5 0.6 dynamic_slice.7
  247.1 0.8 constant_dynamic-slice_fusion
  247.8 0.5 slice_bitcast_fusion.1
  248.4 0.0 copy-start.5
  248.4 0.0 copy-start.4
  248.4 0.0 copy-start.3
  248.4 0.0 copy-start.2
  248.4 0.0 copy-start.1
  248.4 0.0 copy-start
  248.4 3.8 %copy.50 = f32[1024,768]{1,0:T(8,128)} copy(f32[1024,768]{1,0:T(8,128)} %get-tuple-element.105) | data formatting | bytes 6291456
  252.3 0.0 copy-done.5
  252.3 0.6 copy.51
  252.9 0.0 copy-done.4
  252.9 0.6 copy.52
  253.5 0.0 copy-done.3
  253.5 0.6 copy.53
  254.2 0.0 copy-done.2
  254.2 0.6 copy.54
  254.8 0.0 copy-done.1
  254.8 0.7 copy.55
  255.5 0.0 copy-done
  255.5 0.7 copy.56
  (7 shorter events, 0.1 us)
Async XLA Ops:
  248.4 3.9 %copy-start.5 = (f32[24,768]{1,0:T(8,128)S(1)}, f32[24,768]{1,0:T(8,128)}, u32[]{:S(2)}) copy-start(f32[24,768]{1,0:T(8,128)} %get-tuple-element.106) | copy-start | bytes 221188
  248.4 4.5 %copy-start.4 = (f32[24,768]{1,0:T(8,128)S(1)}, f32[24,768]{1,0:T(8,128)}, u32[]{:S(2)}) copy-start(f32[24,768]{1,0:T(8,128)} %get-tuple-element.108) | copy-start | bytes 221188
  248.4 5.1 %copy-start.3 = (f32[24,768]{1,0:T(8,128)S(1)}, f32[24,768]{1,0:T(8,128)}, u32[]{:S(2)}) copy-start(f32[24,768]{1,0:T(8,128)} %get-tuple-element.109) | copy-start | bytes 221188
  248.4 5.8 %copy-start.2 = (f32[24,768]{1,0:T(8,128)S(1)}, f32[24,768]{1,0:T(8,128)}, u32[]{:S(2)}) copy-start(f32[24,768]{1,0:T(8,128)} %get-tuple-element.111) | copy-start | bytes 221188
  248.4 6.4 %copy-start.1 = (f32[24,3072]{1,0:T(8,128)S(1)}, f32[24,3072]{1,0:T(8,128)}, u32[]{:S(2)}) copy-start(f32[24,3072]{1,0:T(8,128)} %get-tuple-element.115) | copy-start | bytes 884740
  248.4 7.1 %copy-start = (f32[96,768]{1,0:T(8,128)S(1)}, f32[96,768]{1,0:T(8,128)}, u32[]{:S(2)}) copy-start(f32[96,768]{1,0:T(8,128)} %get-tuple-element.117) | copy-start | bytes 884740

commit v4 on v3

--- a/solution.py
+++ b/solution.py
@@ -60,7 +60,7 @@
     outs = []
     for j in range(2):
         head = g * (2 * pairs) + pair * 2 + j
-        m = s * (2 * pairs) + pair * 2 + j
+        keys = pl.ds(pl.multiple_of((pair * 2 + j) * SEQ, SEQ), SEQ)
         mine = half if j == 0 else jnp.logical_not(half)
         s_s[j] = dot_nt(jnp.where(mine, qp * 0.125, 0).astype(BF), kp)
         at = head * (6 * 3)
@@ -80,11 +80,11 @@
             live = top > -1e29
             e = jnp.exp(sv - jnp.where(live, top, 0.0))
             total = jnp.sum(e, axis=1, keepdims=True) + jnp.where(live, 0.0, 1.0)
-            p[m, cr, :] = (e * (1.0 / total)).astype(BF)
+            p[pl.ds(pl.multiple_of(s * SEQ + c * BLOCK, BLOCK), BLOCK), keys] = (e * (1.0 / total)).astype(BF)
             tops = top if tops is None else jnp.maximum(tops, top)
         top = jnp.max(tops, axis=0, keepdims=True)
         hm[pl.ds(head, 1), :] = jnp.maximum(hm[pl.ds(head, 1), :], top)
-        outs.append(dot(p[m], vp))
+        outs.append(dot(p[rows, keys], vp))
     ctx[rows, lanes] = jnp.where(half, outs[0], outs[1]).astype(BF)
 
 
@@ -98,17 +98,17 @@
     dqs, dks, dvs = [], [], []
     for j in range(2):
         mine = half if j == 0 else jnp.logical_not(half)
-        m = s * (2 * pairs) + pair * 2 + j
-        dp_s[j] = dot_nt(jnp.where(mine, dcp, 0).astype(BF), vp)
+        keys = pl.ds(pl.multiple_of((pair * 2 + j) * SEQ, SEQ), SEQ)
+        dp_s[j][...] = dot_nt(jnp.where(mine, dcp, 0).astype(BF), vp)
         for c in range(SEQ // BLOCK):
             cr = slice(c * BLOCK, (c + 1) * BLOCK)
-            pv = p[m, cr, :].astype(F32)
-            sl = dp_s[j, cr, :]
+            pv = p[pl.ds(pl.multiple_of(s * SEQ + c * BLOCK, BLOCK), BLOCK), keys].astype(F32)
+            sl = dp_s[j][cr, :]
             mean = jnp.sum(pv * sl, axis=1, keepdims=True)
-            ds_s[j, cr, :] = (pv * (sl - mean)).astype(BF)
-        dqs.append(dot(ds_s[j], kp))
-        dks.append(dot_tn(ds_s[j], qp))
-        dvs.append(dot_tn(p[m], dcp))
+            ds_s[j][cr, :] = (pv * (sl - mean)).astype(BF)
+        dqs.append(dot(ds_s[j][...], kp))
+        dks.append(dot_tn(ds_s[j][...], qp))
+        dvs.append(dot_tn(p[rows, keys], dcp))
     dq[rows, lanes] = (jnp.where(half, dqs[0], dqs[1]) * 0.125).astype(BF)
     dk[rows, lanes] = (jnp.where(half, dks[0], dks[1]) * 0.125).astype(BF)
     dv[rows, lanes] = jnp.where(half, dvs[0], dvs[1]).astype(BF)
@@ -240,11 +240,13 @@
     return me, fc, d1, d2, zs
 
 
-def meet(me, fc, d1, d2, zs):
-    barrier = pltpu.get_barrier_semaphore()
+def greet(me, fc, d1, d2, zs):
     for off in (fc, d1, d2) + zs[1:]:
-        pl.semaphore_signal(barrier, inc=1, device_id=(me + off,), device_id_type=MESH_ID)
-    pl.semaphore_wait(barrier, 6)
+        pl.semaphore_signal(pltpu.get_barrier_semaphore(), inc=1, device_id=(me + off,), device_id_type=MESH_ID)
+
+
+def meet():
+    pl.semaphore_wait(pltpu.get_barrier_semaphore(), 6)
 
 
 def unit_of(ref, unit):
@@ -315,7 +317,8 @@
     mine = [pltpu.make_async_copy(o, unit_of(t, me), local.at[i]) for i, (o, t) in enumerate(zip(owns, targets))]
     for m in mine:
         m.start()
-    meet(*where)
+    greet(*where)
+    meet()
     flows = [Gather(where, o, t, send.at[i], recv.at[i]) for i, (o, t) in enumerate(zip(owns, targets))]
     early, late = flows[:2], flows[2:]
     for f in early:
@@ -392,7 +395,7 @@
 def front(rb, x, segr, segc, stack, vpart, wis, wus, n):
     rows, d = x.shape
     groups = d // GW
-    maps = (rows // SEQ) * (GW // HD)
+    maps = (groups, rows, GW // HD * SEQ)
     sd = jax.ShapeDtypeStruct
     vm, hbm = pl.BlockSpec(memory_space=pltpu.VMEM), pl.BlockSpec(memory_space=pl.ANY)
     whole = lambda a: a.shape[:-2] + (n,) + a.shape[-2:]
@@ -402,12 +405,12 @@
         in_specs=[pl.BlockSpec(memory_space=pltpu.SMEM)] + [vm] * 7,
         out_specs=[hbm] * 3 + [vm] + [hbm] * 5 + [vm] * 2,
         out_shape=[sd(whole(stack), BF), sd(whole(wis), BF), sd(whole(wus), BF), sd((16, d), F32),
-                   sd(act, BF), sd(act, BF), sd(act, BF), sd((groups, maps, SEQ, SEQ), BF), sd(act, BF),
+                   sd(act, BF), sd(act, BF), sd(act, BF), sd(maps, BF), sd(act, BF),
                    sd((rows, d), F32), sd((16, 128), F32)],
         scratch_shapes=[pltpu.VMEM(whole(stack), BF), pltpu.VMEM(whole(vpart), BF),
                         pltpu.VMEM((rows // SEQ, SEQ, SEQ), F32), pltpu.VMEM((2, SEQ, SEQ), F32),
                         pltpu.VMEM(act, BF), pltpu.VMEM(act, BF), pltpu.VMEM(act, BF),
-                        pltpu.VMEM((groups, maps, SEQ, SEQ), BF), pltpu.VMEM(act, BF),
+                        pltpu.VMEM(maps, BF), pltpu.VMEM(act, BF),
                         pltpu.SemaphoreType.DMA((4, 32)), pltpu.SemaphoreType.DMA((4, 32)),
                         pltpu.SemaphoreType.DMA((4,)), pltpu.SemaphoreType.DMA((6,))],
         compiler_params=pltpu.CompilerParams(collective_id=0, has_side_effects=True, vmem_limit_bytes=VMEM_MAX),
@@ -416,9 +419,8 @@
 
 
 class Scatter:
-    def __init__(self, where, grad, own, rp, r1, r2, rz, sems, lsem):
-        self.where, self.grad, self.own = where, grad, own
-        self.rp, self.r1, self.r2, self.rz, self.sems, self.lsem = rp, r1, r2, rz, sems, lsem
+    def __init__(self, where, grad, rp, r1, r2, rz, sems):
+        self.where, self.grad, self.rp, self.r1, self.r2, self.rz, self.sems = where, grad, rp, r1, r2, rz, sems
 
     def remote(self, src, dst, slot, off):
         return pltpu.make_async_remote_copy(
@@ -431,21 +433,13 @@
             for b in (1, 0):
                 for k in range(4):
                     self.remote(unit_of(self.grad, me + fc + a * d2 + b * d1 + zs[k]), self.rp.at[a, b, k], a, fc).start()
-            if self.own is not None:
-                for b in (1, 0):
-                    for k in range(4):
-                        pltpu.make_async_copy(unit_of(self.grad, me + a * d1 + b * d2 + zs[k]), self.own.at[a, b, k],
-                                              self.lsem.at[a]).start()
 
     def pair(self, a):
         me, fc, d1, d2, zs = self.where
         self.remote(self.rp.at[a], self.rp.at[a], a, fc).wait_recv()
-        if self.own is not None:
-            pltpu.make_async_copy(self.own.at[a], self.own.at[a], self.lsem.at[a]).wait()
         for b in (1, 0):
             for k in range(4):
-                held = self.own[a, b, k] if self.own is not None else (
-                    unit_of(self.grad, me + a * d1 + b * d2 + zs[k])[...])
+                held = unit_of(self.grad, me + a * d1 + b * d2 + zs[k])[...]
                 self.rp[a, b, k] = (held.astype(F32) + self.rp[a, b, k].astype(F32)).astype(BF)
             if a == 1:
                 self.remote(self.rp.at[1, b], self.r1.at[b], 2 + b, d1).start()
@@ -464,18 +458,22 @@
             self.rp[0, 0, k] = (self.rp[0, 0, k].astype(F32) + self.r2[k].astype(F32)).astype(BF)
             self.remote(self.rp.at[0, 0, k], self.rz.at[k - 1], 4 + k, zs[k]).start()
 
+    def near(self):
+        return self.rp[0, 0, 0].astype(F32) + self.r2[0].astype(F32)
+
+    def far(self, k):
+        self.remote(self.rp.at[0, 0, k], self.rz.at[k - 1], 4 + k, self.where[4][k]).wait_recv()
+        return self.rz[k - 1].astype(F32)
+
     def last(self):
-        me, fc, d1, d2, zs = self.where
-        total = self.rp[0, 0, 0].astype(F32) + self.r2[0].astype(F32)
-        for k in (1, 2, 3):
-            self.remote(self.rp.at[0, 0, k], self.rz.at[k - 1], 4 + k, zs[k]).wait_recv()
-            total = total + self.rz[k - 1].astype(F32)
-        return total
+        return self.near() + self.far(1) + self.far(2) + self.far(3)
+
+    def core_sent(self):
+        for a in (1, 0):
+            self.remote(self.rp.at[a], self.rp.at[a], a, self.where[1]).wait_send()
 
     def drain(self):
         me, fc, d1, d2, zs = self.where
-        for a in (1, 0):
-            self.remote(self.rp.at[a], self.rp.at[a], a, fc).wait_send()
         for b in (1, 0):
             self.remote(self.rp.at[1, b], self.r1.at[b], 2 + b, d1).wait_send()
         self.remote(self.rp.at[0, 1], self.r2, 4, d2).wait_send()
@@ -483,10 +481,54 @@
             self.remote(self.rp.at[0, 0, k], self.rz.at[k - 1], 4 + k, zs[k]).wait_send()
 
 
-def scatter_buffers(shape, own):
-    bufs = [pltpu.VMEM((2, 2, 4) + shape, BF)] if own else []
-    return bufs + [pltpu.VMEM((2, 2, 4) + shape, BF), pltpu.VMEM((2, 4) + shape, BF), pltpu.VMEM((4,) + shape, BF),
-                   pltpu.VMEM((3,) + shape, BF)]
+class Plane(Scatter):
+    def __init__(self, k, *rest):
+        Scatter.__init__(self, *rest)
+        self.k = k
+
+    def begin(self):
+        me, fc, d1, d2, zs = self.where
+        for a in (1, 0):
+            for b in (1, 0):
+                self.remote(self.grad.at[lax.rem(me, 8) + fc + a * d2 + b * d1], self.rp.at[a, b], a, fc).start()
+
+    def pair(self, a):
+        me, fc, d1, d2, zs = self.where
+        self.remote(self.rp.at[a], self.rp.at[a], a, fc).wait_recv()
+        for b in (1, 0):
+            held = self.grad[lax.rem(me, 8) + a * d1 + b * d2]
+            self.rp[a, b] = (held.astype(F32) + self.rp[a, b].astype(F32)).astype(BF)
+            if a == 1:
+                self.remote(self.rp.at[1, b], self.r1.at[b], 2 + b, d1).start()
+
+    def along(self):
+        return self.remote(self.rp.at[0, 0], self.rz.at[self.k - 1], 4 + self.k, self.where[4][self.k])
+
+    def second(self):
+        self.remote(self.rp.at[0, 1], self.r2, 4, self.where[3]).wait_recv()
+        if self.k:
+            self.rp[0, 0] = (self.rp[0, 0].astype(F32) + self.r2[...].astype(F32)).astype(BF)
+            self.along().start()
+
+    def near(self):
+        return self.rp[0, 0].astype(F32) + self.r2[...].astype(F32)
+
+    def far(self):
+        self.along().wait_recv()
+        return self.rz[self.k - 1].astype(F32)
+
+    def drain(self):
+        me, fc, d1, d2, zs = self.where
+        for b in (1, 0):
+            self.remote(self.rp.at[1, b], self.r1.at[b], 2 + b, d1).wait_send()
+        self.remote(self.rp.at[0, 1], self.r2, 4, d2).wait_send()
+        if self.k:
+            self.along().wait_send()
+
+
+def scatter_buffers(lead, shape):
+    return [pltpu.VMEM(lead + (2, 2, 4) + shape, BF), pltpu.VMEM(lead + (2, 4) + shape, BF),
+            pltpu.VMEM(lead + (4,) + shape, BF), pltpu.VMEM(lead + (3,) + shape, BF)]
 
 
 class Vectors:
@@ -527,71 +569,231 @@
         return total
 
 
-def back_body(x_h, db_h, dsum_h, wall_h, q_h, k_h, v_h, c_h, p_h, small, hm, gu, gi,
-              dx, o_q, o_k, o_v, o_o, o_i, o_u, vout, *rest):
-    (x, db, wall, q, k, v, c, p, dc, dq, dk, dv, dp_s, ds_s, go, gg, held, got, sems, lsems, vsems, isem) = rest[:22]
-    bufs = rest[22:]
+def rear_body(z_h, cot_h, wi_h, wu_h, x_h, wall_h, q_h, k_h, v_h, c_h, p_h, vecs, hm,
+              out_h, dx, o_q, o_k, o_v, o_o, o_i, o_u, vout,
+              wi, wu, ag, z, fl, do, db, gu, gi, gg, held, got, usems, nsems, sems, vsems, isem, osem, *bufs):
     where = place()
-    rows, d = x.shape
-    groups = d // GW
-    n = go.shape[0]
+    zi = where[0] // 8
+    rows, d = z.shape
+    ff = wi.shape[1]
+    groups, n = gg.shape[0], gi.shape[1]
+    rt, et = 512, 128
+    k0, k1 = math.sqrt(2.0 / math.pi), 0.044715
+    act, gp, small = ag.at[0], ag.at[1], held.at[0]
+    row = lambda i: vecs[i:i + 1, :]
+    part = lambda j: pl.ds(pl.multiple_of(j * d, d), d)
+    beside = lambda k: (zi % 2 + k % 2 - 2 * (zi % 2) * (k % 2)) + 2 * (zi // 2 + k // 2 - 2 * (zi // 2) * (k // 2))
+
+    def up_flow(it):
+        k = (it + 1) % 4 if isinstance(it, int) else None
+        return Plane(k, where, gu.at[lax.rem(it, 2)], bufs[0].at[it], bufs[1].at[it], bufs[2].at[it], bufs[3], usems.at[it])
+
+    def in_flow(it):
+        return Scatter(where, gi.at[lax.rem(it, 2)], *(b.at[it] for b in bufs[4:8]), nsems.at[it])
+
+    small_flow = Vectors(where, held, got, vsems)
+    out_flow = Scatter(where, gi.at[0], *bufs[8:12], sems.at[0])
+    group_flow = [Scatter(where, gg.at[g], *bufs[12 + 4 * g:16 + 4 * g], sems.at[1 + g]) for g in range(groups)]
+
+    def get_up(j):
+        return pltpu.make_async_copy(wi_h.at[:, part(j)], wi.at[:, part(j)], isem.at[j])
+
+    def get_down(j):
+        return pltpu.make_async_copy(wu_h.at[part(j)], wu.at[part(j)], isem.at[4 + j])
+
+    def get_wall(i):
+        return pltpu.make_async_copy(wall_h.at[i], wi.at[:, pl.ds(i * d, d)], isem.at[i])
+
+    def get_ctx(g):
+        return pltpu.make_async_copy(c_h.at[g], fl.at[:, pl.ds(g * GW, GW)], isem.at[4 + g])
+
+    get_z = pltpu.make_async_copy(z_h, z, isem.at[8])
+    get_cot = pltpu.make_async_copy(cot_h, do, isem.at[9])
+    get_x = pltpu.make_async_copy(x_h, do, isem.at[9])
+    put_out = pltpu.make_async_copy(db, out_h, osem)
+    mid_cols = pl.ds(0, GW // HD * SEQ)
+
+    def get_group(g, i):
+        cols = pl.ds(pl.multiple_of(g * GW, GW), GW)
+        src = (v_h, q_h, k_h, p_h)[i].at[g]
+        dst = wu.at[pl.ds((2, 0, 1)[i] * rows, rows), cols] if i < 3 else ag.at[lax.rem(g, 2), :, mid_cols]
+        return pltpu.make_async_copy(src, dst, isem.at[10 + 4 * lax.rem(g, 2) + i])
+
+    get_z.start()
+    for j in range(ff // d):
+        get_up(j).start()
+        get_down(j).start()
+    get_cot.start()
+    greet(*where)
+    small[...] = jnp.zeros(small.shape, F32)
+    get_z.wait()
+
+    def prep(i, _):
+        r = pl.ds(pl.multiple_of(i * et, et), et)
+        unit, _inv = unit_rows(z[r, :])
+        first = unit * row(AG) + row(ASH)
+        fl[r, :] = first.astype(BF)
+        dx[r, :] = first + row(BO)
+        return 0
+
+    lax.fori_loop(0, rows // et, prep, 0)
+
+    def up(i, _):
+        j = i // (rows // rt)
+        r = pl.ds(pl.multiple_of((i % (rows // rt)) * rt, rt), rt)
+        c = part(j)
+
+        @pl.when(i % (rows // rt) == 0)
+        def _():
+            get_up(j).wait()
+            get_down(j).wait()
+
+        u = dot(fl[r, :], wi[:, c]) + vecs[pl.ds(BI + j, 1), :]
+        u2 = u * u
+        t = jnp.tanh(u * (k0 + (k0 * k1) * u2))
+        h = 0.5 + 0.5 * t
+        a = (u * h).astype(BF)
+        act[r, c] = a
+        gp[r, c] = (h + (0.5 * u) * (1.0 - t * t) * (k0 + (3.0 * k0 * k1) * u2)).astype(BF)
+        dx[r, :] += dot(a, wu[c, :])
+        return 0
+
+    lax.fori_loop(0, (ff // d) * (rows // rt), up, 0)
+    get_cot.wait()
+
+    def mid(i, _):
+        r = pl.ds(pl.multiple_of(i * et, et), et)
+        unit, inv = unit_rows(dx[r, :])
+        db[r, :] = (unit * row(FG) + row(FS)).astype(BF)
+        upv = do[r, :].astype(F32)
+        small[FG:FG + 1, :] += col_sum(upv * unit)
+        small[FS:FS + 1, :] += col_sum(upv)
+        ds = norm_back(upv, unit, inv, row(FG))
+        dsl = ds.astype(BF)
+        do[r, :] = dsl
+        dx[r, :] = ds
+        small[BO:BO + 1, :] += col_sum(dsl.astype(F32))
+        return 0
+
+    lax.fori_loop(0, rows // et, mid, 0)
+    put_out.start()
+    meet()
+
+    def down(it, _):
+        j = beside((it + 1) % 4)
+        c = part(j)
+        slot = lax.rem(it, 2)
+
+        @pl.when(it >= 2)
+        def _():
+            up_flow(it - 2).core_sent()
+
+        gu[slot] = dot_tn(act[:, c], do[...]).astype(BF).reshape(gu.shape[1:])
+        up_flow(it).begin()
+        sums = None
+        for i in range(rows // rt):
+            r = slice(i * rt, (i + 1) * rt)
+            di = dot_nt(do[r, :], wu[c, :]) * gp[r, c].astype(F32)
+            dil = di.astype(BF)
+            act[r, c] = dil
+            s = col_sum(dil.astype(F32))
+            sums = s if sums is None else sums + s
+            dx[r, :] += dot_nt(dil, wi[:, c])
+            if i == 0:
+                @pl.when(it >= 1)
+                def _():
+                    in_flow(it - 1).pair(1)
+                    in_flow(it - 1).pair(0)
+        small[pl.ds(BI + j, 1), :] = sums
+        up_flow(it).pair(1)
+        up_flow(it).pair(0)
+
+        @pl.when(it >= 2)
+        def _():
+            in_flow(it - 2).core_sent()
+
+        gi[slot] = dot_tn(fl[...], act[:, c]).reshape(gi.shape[1:]).astype(BF)
+        in_flow(it).begin()
+
+        @pl.when(it >= 2)
+        def _():
+            for f in (up_flow(it - 2), in_flow(it - 2)):
+                f.first(1)
+                f.first(0)
+
+        return 0
+
+    lax.fori_loop(0, ff // d, down, 0)
+    get_wall(3).start()
+    for i in range(4):
+        get_group(0, i).start()
+    for g in range(groups):
+        get_ctx(g).start()
+    get_x.start()
+    for i in range(3):
+        get_wall(i).start()
+    put_out.wait()
+
+    def tail(i, _):
+        r = pl.ds(pl.multiple_of(i * et, et), et)
+        unit, inv = unit_rows(z[r, :])
+        df = dx[r, :]
+        small[AG:AG + 1, :] += col_sum(df * unit)
+        small[ASH:ASH + 1, :] += col_sum(df)
+        ds = norm_back(df, unit, inv, row(AG))
+        dx[r, :] = ds
+        dsl = ds.astype(BF)
+        db[r, :] = dsl
+        small[OB:OB + 1, :] += col_sum(dsl.astype(F32))
+        return 0
+
+    lax.fori_loop(0, rows // et, tail, 0)
+    in_flow(3).pair(1)
+    in_flow(3).pair(0)
+    for g in range(groups):
+        get_ctx(g).wait()
+    in_flow(2).core_sent()
+    gi[0] = dot_tn(fl[...], db[...]).reshape(gi.shape[1:]).astype(BF)
+    out_flow.begin()
+    get_wall(3).wait()
+
     steps = (rows // SEQ) * (GW // 128)
-    small_flow = Vectors(where, held, got, vsems)
-    up_flow = Scatter(where, gu, *bufs[0:5], sems.at[0], lsems.at[0])
-    in_flow = Scatter(where, gi, *bufs[5:10], sems.at[1], lsems.at[1])
-    out_flow = Scatter(where, go, None, *bufs[10:14], sems.at[2], None)
-    group_flow = [Scatter(where, gg.at[g], None, *bufs[14 + 4 * g:18 + 4 * g], sems.at[3 + g], None)
-                  for g in range(groups)]
-
-    def fetch(i):
-        pairs = ((db_h, db), (wall_h.at[3], wall.at[3]), (c_h, c), (dsum_h, dx), (x_h, x),
-                 (wall_h.at[pl.ds(0, 3)], wall.at[pl.ds(0, 3)]))
-        return pltpu.make_async_copy(*pairs[i], isem.at[i])
-
-    def fetch_group(g, i):
-        src = (v_h, q_h, k_h, p_h)[i].at[g]
-        dst = ((v, q, k)[i].at[g] if i < 3 else p.at[lax.rem(g, 2)])
-        return pltpu.make_async_copy(src, dst, isem.at[6 + 4 * lax.rem(g, 2) + i])
-
-    for i in range(3):
-        fetch(i).start()
-    for i in range(4):
-        fetch_group(0, i).start()
-    for i in range(3, 6):
-        fetch(i).start()
-    meet(*where)
-    up_flow.begin()
-    in_flow.begin()
-    for i in range(3):
-        fetch(i).wait()
-
-    dbv = db[...]
-    go[...] = jnp.concatenate([dot_tn(c[g], dbv) for g in range(groups)], axis=0).astype(BF).reshape(go.shape)
-    out_flow.begin()
-
+    edge = GW // HD * SEQ
+    dc, dq, dk, dv = (act.at[:, pl.ds(edge + i * GW, GW)] for i in range(4))
+    dp_s = [z.at[pl.ds(j * SEQ, SEQ), pl.ds(0, SEQ)] for j in range(2)]
+    ds_s = [gp.at[pl.ds(j * SEQ, SEQ), pl.ds(edge, SEQ)] for j in range(2)]
+    both = lambda f: [(f.first, 1), (f.first, 0)]
+    g0, g1, g2 = group_flow
     events = {
-        0: [(up_flow.pair, 1)], 1: [(in_flow.pair, 1)], 2: [(up_flow.pair, 0)], 3: [(in_flow.pair, 0)],
-        4: [(out_flow.pair, 1)], 5: [(up_flow.first, 1), (out_flow.pair, 0)], 6: [(in_flow.first, 1)],
-        7: [(up_flow.first, 0)], 8: [(in_flow.first, 0), (group_flow[0].pair, 1)],
-        9: [(out_flow.first, 1), (up_flow.second,)], 10: [(out_flow.first, 0), (group_flow[0].pair, 0)],
-        11: [(in_flow.second,)],
+        0: [(up_flow(0).second,), (in_flow(0).second,), (out_flow.pair, 1)],
+        1: [(out_flow.pair, 0)] + both(up_flow(2)),
+        2: both(in_flow(2)) + [(up_flow(1).second,)],
+        3: [(in_flow(1).second,)],
+        4: both(up_flow(3)),
+        5: both(in_flow(3)) + [(g0.pair, 1)],
+        6: [(g0.pair, 0), (up_flow(2).second,), (out_flow.first, 1)],
+        7: [(out_flow.first, 0), (in_flow(2).second,)],
+        8: [(up_flow(3).second,), (in_flow(3).second,), (g0.first, 1)],
+        9: [(g0.first, 0), (g1.pair, 1)],
+        10: [(g1.pair, 0), (out_flow.second,)],
+        11: [(g0.second,), (g1.first, 1)],
     }
 
     def group(g, _):
         cols = pl.ds(pl.multiple_of(g * GW, GW), GW)
-        weight = lambda i: wall[i, :, cols]
         for i in range(4):
-            fetch_group(g, i).wait()
+            get_group(g, i).wait()
 
         @pl.when(g + 1 < groups)
         def _():
             for i in range(4):
-                fetch_group(g + 1, i).start()
-
-        dc[...] = dot_nt(db[...], wall[3, cols, :]).astype(BF)
+                get_group(g + 1, i).start()
+
+        dc[...] = dot_nt(db[...], wi[cols, 3 * d:4 * d]).astype(BF)
+        heads = [wu.at[pl.ds(i * rows, rows), cols] for i in range(3)]
 
         def one_pair(it, _):
-            pair_backward(it, q.at[g], k.at[g], v.at[g], p.at[lax.rem(g, 2)], dc, dq, dk, dv, dp_s, ds_s)
+            pair_backward(it, *heads, ag.at[lax.rem(g, 2)], dc, dq, dk, dv, dp_s, ds_s)
             for when, todo in events.items():
                 @pl.when(g * steps + it == when)
                 def _():
@@ -600,85 +802,91 @@
             return 0
 
         lax.fori_loop(0, steps, one_pair, 0)
-        held[0, QB:QB + 1, cols] = col_sum(dq[...].astype(F32))
-        held[0, VB:VB + 1, cols] = col_sum(dv[...].astype(F32))
+        small[QB:QB + 1, cols] = col_sum(dq[...].astype(F32))
+        small[VB:VB + 1, cols] = col_sum(dv[...].astype(F32))
 
         @pl.when(g == 0)
         def _():
-            for i in range(3, 6):
-                fetch(i).wait()
-
-        xv = x[...]
-        for i, part in enumerate((dq, dk, dv)):
-            gg[g, i] = dot_tn(xv, part[...]).astype(BF).reshape(n, d // n, GW)
+            get_x.wait()
+            for i in range(3):
+                get_wall(i).wait()
+
+        xv = do[...]
+        for i, grad in enumerate((dq, dk, dv)):
+            gg[g, i] = dot_tn(xv, grad[...]).reshape(n, d // n, GW).astype(BF)
         for i in range(groups):
             @pl.when(g == i)
             def _():
                 group_flow[i].begin()
+        weight = lambda i: wi[:, pl.ds(pl.multiple_of(i * d + g * GW, GW), GW)]
         dx[...] += dot_nt(dq[...], weight(0)) + dot_nt(dk[...], weight(1)) + dot_nt(dv[...], weight(2))
         return 0
 
-    held[0] = small[...]
     lax.fori_loop(0, groups, group, 0)
     diag = lax.broadcasted_iota(jnp.int32, hm.shape, 0) == lax.broadcasted_iota(jnp.int32, hm.shape, 1)
-    held[0, TOP:TOP + 1, 0:128] = jnp.sum(jnp.where(diag, hm[...], 0.0), axis=0, keepdims=True)
+    small[TOP:TOP + 1, 0:128] = jnp.sum(jnp.where(diag, hm[...], 0.0), axis=0, keepdims=True)
     small_flow.step(0)
-    g1, g2 = group_flow[1:]
-    g1.pair(1)
     g2.pair(1)
+    g2.pair(0)
     small_flow.step(1)
-    out_flow.second()
-    group_flow[0].first(1)
-    g1.pair(0)
-    g2.pair(0)
+    g1.first(0)
+    g2.first(1)
     small_flow.step(2)
-    g1.first(1)
-    g2.first(1)
+    g1.second()
+    g2.first(0)
     small_flow.step(3)
-    group_flow[0].first(0)
-    g1.first(0)
-    g2.first(0)
-    for f in group_flow:
-        f.second()
-    o_u[...] = up_flow.last()
-    o_i[...] = in_flow.last()
+    o_u[...] = up_flow(3).near() + up_flow(0).far() + up_flow(1).far() + up_flow(2).far()
+    for it in range(4):
+        k = (it + 1) % 4
+        total = in_flow(it).near()
+        for m in (1, 2, 3):
+            total = total + in_flow(((k ^ m) - 1) % 4).far(m)
+        o_i[:, part(beside(k))] = total
     o_o[...] = out_flow.last()
+    g2.second()
     for g, f in enumerate(group_flow):
         t = f.last()
         for i, o in enumerate((o_q, o_k, o_v)):
             o[:, g * GW:(g + 1) * GW] = t[i]
     vout[...] = small_flow.last()
-    for f in [up_flow, in_flow, out_flow] + group_flow:
+    up_flow(2).core_sent()
+    up_flow(3).core_sent()
+    in_flow(3).core_sent()
+    for f in [out_flow] + group_flow:
+        f.core_sent()
+    for f in [up_flow(i) for i in range(4)] + [in_flow(i) for i in range(4)] + [out_flow] + group_flow:
         f.drain()
 
 
-def back(x, db, dsum, wall, q, k, v, c, p, small, hm, gu, gi):
+def rear(n, z, cot, wi, wu, x, wall, q, k, v, c, p, vecs, hm):
     rows, d = x.shape
-    groups, n = d // GW, gu.shape[0]
-    maps = (rows // SEQ) * (GW // HD)
-    r, ru, ff = d // n, gu.shape[1], gi.shape[2]
+    ff = wi.shape[1]
+    groups = d // GW
+    r, ru = d // n, ff // n
     sd = jax.ShapeDtypeStruct
     vm, hbm = pl.BlockSpec(memory_space=pltpu.VMEM), pl.BlockSpec(memory_space=pl.ANY)
-    act = pltpu.VMEM((groups, rows, GW), BF)
-    one = pltpu.VMEM((rows, GW), BF)
-    bufs = scatter_buffers((ru, d), True) + scatter_buffers((r, ff), True) + scatter_buffers((r, d), False)
+    flat = pltpu.VMEM((rows, d), BF)
+    bufs = [pltpu.VMEM((4, 2, 2, ru, d), BF), pltpu.VMEM((4, 2, ru, d), BF), pltpu.VMEM((4, ru, d), BF),
+            pltpu.VMEM((3, ru, d), BF)]
+    bufs += scatter_buffers((4,), (r, d)) + scatter_buffers((), (r, d))
     for _ in range(groups):
-        bufs += scatter_buffers((3, r, GW), False)
+        bufs += scatter_buffers((), (3, r, GW))
     return pl.pallas_call(
-        back_body,
-        in_specs=[hbm] * 9 + [vm] * 2 + [hbm] * 2,
-        out_specs=[vm] * 8,
-        out_shape=[sd((rows, d), F32)] + [sd((r, d), F32)] * 4 + [sd((r, ff), F32), sd((ru, d), F32), sd((16, d), F32)],
-        scratch_shapes=[pltpu.VMEM((rows, d), BF), pltpu.VMEM((rows, d), BF), pltpu.VMEM((4, d, d), BF),
-                        act, act, act, act, pltpu.VMEM((2, maps, SEQ, SEQ), BF), one, one, one, one,
-                        pltpu.VMEM((2, SEQ, SEQ), F32), pltpu.VMEM((2, SEQ, SEQ), BF),
-                        pltpu.VMEM((n, r, d), BF), pltpu.VMEM((groups, 3, n, r, GW), BF),
+        rear_body,
+        in_specs=[hbm] * 11 + [vm] * 2,
+        out_specs=[hbm] + [vm] * 8,
+        out_shape=[sd((rows, d), BF), sd((rows, d), F32)] + [sd((r, d), F32)] * 4
+        + [sd((r, ff), F32), sd((ru, d), F32), sd((16, d), F32)],
+        scratch_shapes=[pltpu.VMEM((d, ff), BF), pltpu.VMEM((ff, d), BF), pltpu.VMEM((2, rows, ff), BF),
+                        pltpu.VMEM((rows, d), F32), flat, flat, flat, pltpu.VMEM((2, 8, ru, d), BF),
+                        pltpu.VMEM((2, n, r, d), BF), pltpu.VMEM((groups, 3, n, r, GW), BF),
                         pltpu.VMEM((4, 16, d), F32), pltpu.VMEM((6, 16, d), F32),
-                        pltpu.SemaphoreType.DMA((3 + groups, 2, 8)), pltpu.SemaphoreType.DMA((2, 2)),
-                        pltpu.SemaphoreType.DMA((2, 6)), pltpu.SemaphoreType.DMA((14,))] + bufs,
+                        pltpu.SemaphoreType.DMA((4, 2, 8)), pltpu.SemaphoreType.DMA((4, 2, 8)),
+                        pltpu.SemaphoreType.DMA((1 + groups, 2, 8)), pltpu.SemaphoreType.DMA((2, 6)),
+                        pltpu.SemaphoreType.DMA((18,)), pltpu.SemaphoreType.DMA] + bufs,
         compiler_params=pltpu.CompilerParams(collective_id=1, has_side_effects=True, vmem_limit_bytes=VMEM_MAX),
-        name="back",
-    )(x, db, dsum, wall, q, k, v, c, p, small, hm, gu, gi)
+        name="rear",
+    )(z, cot, wi, wu, x, wall, q, k, v, c, p, vecs, hm)
 
 
 def attn_fwd_body(rb, x, segr, segc, wq, wk, wv, wo, vecs, q, k, v, p, c, z, hm, bias, s_s):
@@ -707,7 +915,7 @@
 def attn_fwd(rb, x, segr, segc, wall, vecs):
     rows, d = x.shape
     groups, seqs = d // GW, rows // SEQ
-    maps = seqs * (GW // HD)
+    keys = GW // HD * SEQ
     full = lambda shape: pl.BlockSpec(shape, lambda g, *_: (0,) * len(shape))
     col = lambda i: pl.BlockSpec((None, d, GW), lambda g, *_: (i, 0, g))
     act = pl.BlockSpec((None, rows, GW), lambda g, *_: (g, 0, 0))
@@ -718,11 +926,11 @@
             num_scalar_prefetch=1, grid=(groups,),
             in_specs=[full((rows, d)), full((seqs, SEQ)), full((rows, 1)), col(0), col(1), col(2),
                       pl.BlockSpec((None, GW, d), lambda g, *_: (3, g, 0)), full((16, d))],
-            out_specs=[act, act, act, pl.BlockSpec((None, maps, SEQ, SEQ), lambda g, *_: (g, 0, 0, 0)), act,
+            out_specs=[act, act, act, pl.BlockSpec((None, rows, keys), lambda g, *_: (g, 0, 0)), act,
                        full((rows, d)), full((16, 128))],
             scratch_shapes=[pltpu.VMEM((seqs, SEQ, SEQ), F32), pltpu.VMEM((2, SEQ, SEQ), F32)]),
         out_shape=[sd((groups, rows, GW), BF)] * 3
-        + [sd((groups, maps, SEQ, SEQ), BF), sd((groups, rows, GW), BF), sd((rows, d), F32), sd((16, 128), F32)],
+        + [sd((groups, rows, keys), BF), sd((groups, rows, GW), BF), sd((rows, d), F32), sd((16, 128), F32)],
         compiler_params=pltpu.CompilerParams(vmem_limit_bytes=VMEM_MAX),
         name="attn_fwd",
     )(rb, x, segr, segc, wall, wall, wall, wall, vecs)
@@ -741,7 +949,7 @@
     dw[3, cols, :] = dot_tn(c[...], dbv).astype(dw.dtype)
 
     def one_pair(it, _):
-        pair_backward(it, q, k, v, p, dc, dq, dk, dv, dp_s, ds_s)
+        pair_backward(it, q, k, v, p, dc, dq, dk, dv, [dp_s.at[0], dp_s.at[1]], [ds_s.at[0], ds_s.at[1]])
         return 0
 
     lax.fori_loop(0, x.shape[0] // SEQ * (GW // 128), one_pair, 0)
@@ -756,7 +964,7 @@
 def attn_bwd(x, db, wall, q, k, v, p, c, dsum, gdt):
     rows, d = x.shape
     groups = d // GW
-    maps = (rows // SEQ) * (GW // HD)
+    keys = GW // HD * SEQ
     full = lambda shape: pl.BlockSpec(shape, lambda g: (0,) * len(shape), pipeline_mode=pl.Buffered(1))
     col = lambda i: pl.BlockSpec((None, d, GW), lambda g: (i, 0, g))
     vec = pl.BlockSpec((1, GW), lambda g: (0, g))
@@ -767,7 +975,7 @@
         grid=(groups,),
         in_specs=[full((rows, d)), full((rows, d)), col(0), col(1), col(2),
                   pl.BlockSpec((None, GW, d), lambda g: (3, g, 0)), act, act, act,
-                  pl.BlockSpec((None, maps, SEQ, SEQ), lambda g: (g, 0, 0, 0)), act, full((rows, d))],
+                  pl.BlockSpec((None, rows, keys), lambda g: (g, 0, 0)), act, full((rows, d))],
         out_specs=[full((4, d, d)), vec, vec, full((rows, d))],
         out_shape=[sd((4, d, d), gdt)] + [sd((1, d), F32)] * 2 + [sd((rows, d), F32)],
         scratch_shapes=[pltpu.VMEM((rows, GW), BF)] * 4
@@ -797,9 +1005,8 @@
     d, ff = tokens.shape[1], inner_weight.shape[1]
     wall, wi, wu, vecs, q, k, v, p, c, z, hm = front(rb, tokens, segr, segc, stack, vec_part, inner_weight,
                                                      outer_weight, n)
-    out, dsum, db, dwi, dwu, small = ffn(z, cot, wi.reshape(d, ff), wu.reshape(ff, d), vecs, BF)
-    dx, dwq, dwk, dwv, dwo, dwi, dwu, total = back(
-        tokens, db, dsum, wall.reshape(4, d, d), q, k, v, c, p, small, hm, dwu.reshape(n, -1, d), dwi.reshape(n, -1, ff))
+    out, dx, dwq, dwk, dwv, dwo, dwi, dwu, total = rear(
+        n, z, cot, wi.reshape(d, ff), wu.reshape(ff, d), tokens, wall.reshape(4, d, d), q, k, v, c, p, vecs, hm)
     return out, dx, dwq, dwk, dwv, dwo, dwi, dwu, total
 
 
@@ -824,7 +1031,8 @@
     stack = jnp.stack([query_weight, key_weight, value_weight, output_weight])
     names = (query_bias, value_bias, output_bias, attn_gain, attn_shift, outer_bias, final_gain, final_shift)
     part, wide = query_bias.shape[0], inner_bias.shape[0]
-    layer = near_layer if n == 32 and query_weight.shape[0] % 8 == 0 else far_layer
+    rows = tokens.shape[0]
+    layer = near_layer if n == 32 and (rows, d, ff) == (2 * SEQ, 3 * GW, 6 * SEQ) else far_layer
     out, dx, dwq, dwk, dwv, dwo, dwi, dwu, total = layer(
         n, random_blocks.reshape(-1), tokens, segment_ids.reshape(-1, SEQ), segment_ids.reshape(-1, 1), out_cotangent,
         stack, vectors_part(me, n, names, inner_bias), inner_weight, outer_weight)

time: 257 us -> 237 us (0.922)
  Pallas kernels: 233 us -> 213 us
    pallas_call x2 -> x1, Pallas kernels: 153 us -> 132 us  [rear(): pl.pallas_call(rear_body, in_specs=[hbm] * 11 + [vm] * 2, out_specs=[hbm]...]
    unnamed x20 -> x23, local copies, waits for them, and re-layouts: 8.64 us -> 9.28 us
where the time goes in v4:
time: 237 us; the launch traced here: 236 us
  Pallas kernels  213 us (90%)
  local copies, waits for them, and re-layouts  17.5 us (7%)
  other arithmetic  4.81 us (2%)
    pallas_call x1, Pallas kernels, rear(): pl.pallas_call(rear_body, in_specs=[hbm] * 11 + [vm] * 2, out_specs=[hbm]...  132 us
    pallas_call x1, Pallas kernels, front(): pl.pallas_call(front_body, in_specs=[pl.BlockSpec(memory_space=pltpu.SMEM...  80.6 us
    unnamed x23, local copies, waits for them, and re-layouts  9.28 us

profile of v4, /device:TPU:0, one launch (start us, length us, event | category | flops | bytes accessed | tf_op | source)
XLA Modules:
  0.0 236.3 jit_solution(9509754168355035010)
XLA Ops:
  0.7 0.8 stack.55
  1.5 0.1 tile.21
  1.7 0.7 tile.22
  2.3 0.1 tile.23
  2.5 0.6 pad_maximum_fusion.1.vpart
  3.1 1.7 copy.41.segc
  4.8 1.5 pad_maximum_fusion.stack
  6.3 0.8 copy.40
  7.1 0.7 reshape.74.rb
  7.8 1.3 reshape.75.segr
  9.1 80.6 %front.1 = (bf16[4,32,24,768]{3,2,1,0:T(8,128)(2,1)}, bf16[32,24,3072]{2,1,0:T(8,128)(2,1)}, bf16[32,96,768]{2,1,0:T(8,128)(2,1)}, f32[16,768]{1,0:T(8,128)}, bf...) custom-call(s32[216]{0:T(256)} %reshape.74.rb, ...), custom_call_target="tpu_custom_call" | custom-call | tf_op jit(solution)/shard_map/front/pallas_call | solution.py:403
  89.7 132.1 %rear.1 = (bf16[1024,768]{1,0:T(8,128)(2,1)}, f32[1024,768]{1,0:T(8,128)}, f32[24,768]{1,0:T(8,128)}, f32[24,768]{1,0:T(8,128)}, f32[24,768]{1,0:T(8,128)}, /*in...) custom-call(f32[1024,768]{1,0:T(8,128)} %get-tuple-element.40.z_h, ...), custom_call_target="tpu_custom_call" | custom-call | tf_op jit(solution)/shard_map/rear/pallas_call | solution.py:874
  222.4 1.2 minimum_sqrt_fusion
  223.6 0.1 broadcast_in_dim.14
  223.7 0.1 mul.24
  223.7 1.4 multiply_convert_fusion
  225.2 0.7 slice.35
  225.9 0.6 dynamic_slice.7
  226.5 0.8 constant_dynamic-slice_fusion
  227.3 0.5 slice_bitcast_fusion.1
  227.8 0.0 copy-start
  227.8 2.8 %copy.51 = bf16[1024,768]{1,0:T(8,128)(2,1)} copy(bf16[1024,768]{1,0:T(8,128)(2,1)} %get-tuple-element.94) | data formatting | bytes 3145728
  230.6 0.0 copy-done
  230.6 0.0 copy-start.6
  230.6 0.0 copy-start.5
  230.6 0.0 copy-start.4
  230.6 0.0 copy-start.3
  230.6 0.0 copy-start.2
  230.6 0.0 copy-start.1
  230.7 1.7 copy.52
  232.3 0.0 copy-done.6
  232.3 0.6 copy.53
  233.0 0.0 copy-done.5
  233.0 0.6 copy.54
  233.6 0.0 copy-done.4
  233.6 0.6 copy.55
  234.2 0.0 copy-done.3
  234.2 0.6 copy.56
  234.9 0.0 copy-done.2
  234.9 0.7 copy.57
  235.6 0.0 copy-done.1
  235.6 0.7 copy.58
  (7 shorter events, 0.1 us)
Async XLA Ops:
  227.8 2.8 %copy-start = (f32[1024,768]{1,0:T(8,128)S(1)}, f32[1024,768]{1,0:T(8,128)}, u32[]{:S(2)}) copy-start(f32[1024,768]{1,0:T(8,128)} %get-tuple-element.95) | copy-start | bytes 9437188
  230.6 1.7 copy-start.6
  230.6 2.3 copy-start.5
  230.6 3.0 %copy-start.4 = (f32[24,768]{1,0:T(8,128)S(1)}, f32[24,768]{1,0:T(8,128)}, u32[]{:S(2)}) copy-start(f32[24,768]{1,0:T(8,128)} %get-tuple-element.99) | copy-start | bytes 221188
  230.6 3.6 %copy-start.3 = (f32[24,768]{1,0:T(8,128)S(1)}, f32[24,768]{1,0:T(8,128)}, u32[]{:S(2)}) copy-start(f32[24,768]{1,0:T(8,128)} %get-tuple-element.101) | copy-start | bytes 221188
  230.6 4.2 %copy-start.2 = (f32[24,3072]{1,0:T(8,128)S(1)}, f32[24,3072]{1,0:T(8,128)}, u32[]{:S(2)}) copy-start(f32[24,3072]{1,0:T(8,128)} %get-tuple-element.105) | copy-start | bytes 884740
  230.6 4.9 %copy-start.1 = (f32[96,768]{1,0:T(8,128)S(1)}, f32[96,768]{1,0:T(8,128)}, u32[]{:S(2)}) copy-start(f32[96,768]{1,0:T(8,128)} %get-tuple-element.107) | copy-start | bytes 884740

commit v5 on v4

--- a/solution.py
+++ b/solution.py
@@ -40,12 +40,46 @@
     return lax.broadcasted_iota(jnp.int32, (1, 128), 1) < HD
 
 
-def same_document(segr, segc, bias):
-    for s in range(segr.shape[0]):
-        kseg = segr[s:s + 1, :]
+def same_document(key_ids, query_ids, bias):
+    for s in range(bias.shape[0]):
+        kseg = key_ids(s)
         for c in range(SEQ // BLOCK):
-            qseg = segc[s * SEQ + c * BLOCK:s * SEQ + (c + 1) * BLOCK, :]
-            bias[s, c * BLOCK:(c + 1) * BLOCK, :] = jnp.where((qseg == kseg) & (kseg != 0), 0.0, LOW)
+            bias[s, c * BLOCK:(c + 1) * BLOCK, :] = jnp.where((query_ids(s, c) == kseg) & (kseg != 0), 0.0, LOW)
+
+
+def same_document_flat(seg, bias):
+    ids = seg[...].astype(F32)
+    turned = jnp.transpose(ids)
+    per = SEQ // 128
+    key_ids = lambda s: jnp.concatenate([ids[s * per + i:s * per + i + 1, :] for i in range(per)], axis=1)
+
+    def query_ids(s, c):
+        i, r = s * per + c * BLOCK // 128, c * BLOCK % 128
+        return turned[r:r + BLOCK, i:i + 1]
+
+    same_document(key_ids, query_ids, bias)
+
+
+def whole_vectors(pieces, vec, wide):
+    n, d = pieces.shape[0], vec.shape[1]
+    lane = lax.broadcasted_iota(jnp.int32, (1, 128), 1)
+
+    def spread(values, width):
+        tiles = [0.0] * (d // 128)
+        for i, value in enumerate(values):
+            t, at = i * width // 128, i * width % 128
+            moved = pltpu.roll(value, at, 1) if at else value
+            tiles[t] = tiles[t] + (jnp.where(lane >= at, moved, 0.0) if at + width > 128 else moved)
+            if at + width > 128:
+                tiles[t + 1] = tiles[t + 1] + jnp.where(lane < at, moved, 0.0)
+        return jnp.concatenate(tiles, axis=1)
+
+    vec[0:8, :] = spread([pieces[u, 0:8, :] for u in range(n)], d // n)
+    per = d // wide
+    inner = [spread([pieces[j * per + i, 8:16, :] for i in range(per)], wide) for j in range(n // per)]
+    for j, v in enumerate(inner):
+        vec[8 + j:9 + j, :] = v[0:1, :]
+    vec[8 + len(inner):16, :] = jnp.zeros((8 - len(inner), d), F32)
 
 
 def pair_forward(g, it, rb, q, k, v, p, ctx, hm, bias, s_s):
@@ -63,9 +97,7 @@
         keys = pl.ds(pl.multiple_of((pair * 2 + j) * SEQ, SEQ), SEQ)
         mine = half if j == 0 else jnp.logical_not(half)
         s_s[j] = dot_nt(jnp.where(mine, qp * 0.125, 0).astype(BF), kp)
-        at = head * (6 * 3)
-        miss1 = 18 - (rb[at] + rb[at + 1] + rb[at + 2])
-        miss6 = 10 - (rb[at + 15] + rb[at + 16] + rb[at + 17])
+        miss1, miss6 = 18 - rb(head, 0), 10 - rb(head, 5)
         skip1 = jnp.where(lane_block == miss1, LOW, 0.0)
         skip6 = jnp.where(lane_block == miss6, LOW, 0.0)
         tops = None
@@ -305,7 +337,7 @@
 LATE = ((1, 0), (4, 1), (2, 2), (5, 3), (8, 4), (3, 5), (6, 6), (9, 7), (7, 8), (12, 9), (10, 10), (13, 11))
 
 
-def front_body(rb, x, segr, segc, stack, vpart, wis, wus,
+def front_body(rb, x, seg, wq, wk, wv, wo, vpart, wis, wus,
                wall_o, wi_o, wu_o, vec_o, q_o, k_o, v_o, p_o, c_o, z_o, hm_o,
                wall, vg, bias, s_s, q_s, k_s, v_s, p_s, c_s, send, recv, local, outs):
     where = place()
@@ -313,11 +345,14 @@
     rows, d = x.shape
     groups = d // GW
     steps = (rows // SEQ) * (GW // 128)
-    owns, targets = (stack, vpart, wis, wus), (wall, vg, wi_o, wu_o)
-    mine = [pltpu.make_async_copy(o, unit_of(t, me), local.at[i]) for i, (o, t) in enumerate(zip(owns, targets))]
-    for m in mine:
+    owns, targets = (wall.at[:, me], vpart, wis, wus), (wall, vg, wi_o, wu_o)
+    mine = [pltpu.make_async_copy(o, unit_of(t, me), local.at[i]) for i, (o, t) in enumerate(zip(owns[1:], targets[1:]))]
+    four = [pltpu.make_async_copy(w, wall.at[i, me], local.at[3 + i]) for i, w in enumerate((wq, wk, wv, wo))]
+    for m in four + mine:
         m.start()
     greet(*where)
+    for m in four:
+        m.wait()
     meet()
     flows = [Gather(where, o, t, send.at[i], recv.at[i]) for i, (o, t) in enumerate(zip(owns, targets))]
     early, late = flows[:2], flows[2:]
@@ -325,7 +360,7 @@
         f.begin_z()
     for f in early:
         f.begin_xy()
-    same_document(segr, segc, bias)
+    same_document_flat(seg, bias)
     for slot in Gather.ORDER:
         for f in early:
             f.step(slot)
@@ -337,11 +372,9 @@
     for f in early:
         f.finish()
     mine[0].wait()
-    mine[1].wait()
     keep = pltpu.make_async_copy(wall, wall_o, outs.at[5])
     keep.start()
-    vec = jnp.sum(vg[...].astype(F32), axis=0)
-    vec_o[...] = vec
+    whole_vectors(vg, vec_o, wus.shape[0])
     hm_o[...] = jnp.full(hm_o.shape, LOW, F32)
     z_o[...] = x[...].astype(F32) + vec_o[OB:OB + 1, :]
 
@@ -358,7 +391,8 @@
         v_s[g] = (dot(xv, weight(2)) + vec_o[VB:VB + 1, cols]).astype(BF)
 
         def one_pair(it, _):
-            pair_forward(g, it, rb, q_s.at[g], k_s.at[g], v_s.at[g], p_s.at[g], c_s.at[g], hm_o, bias, s_s)
+            pair_forward(g, it, lambda h, i: jnp.sum(rb[h].astype(F32)[i:i + 1, :], axis=1, keepdims=True).astype(jnp.int32),
+                         q_s.at[g], k_s.at[g], v_s.at[g], p_s.at[g], c_s.at[g], hm_o, bias, s_s)
             for slot, when in LATE:
                 @pl.when(g * steps + it == when)
                 def _():
@@ -382,8 +416,8 @@
                 f.step(slot)
     for f in late:
         f.finish()
+    mine[1].wait()
     mine[2].wait()
-    mine[3].wait()
     for f in flows:
         f.drain()
     keep.wait()
@@ -392,30 +426,31 @@
             put(g, i).wait()
 
 
-def front(rb, x, segr, segc, stack, vpart, wis, wus, n):
+def front(rb, x, seg, wq, wk, wv, wo, vpart, wis, wus, n):
     rows, d = x.shape
     groups = d // GW
     maps = (groups, rows, GW // HD * SEQ)
     sd = jax.ShapeDtypeStruct
     vm, hbm = pl.BlockSpec(memory_space=pltpu.VMEM), pl.BlockSpec(memory_space=pl.ANY)
-    whole = lambda a: a.shape[:-2] + (n,) + a.shape[-2:]
+    whole = lambda a: (n,) + a.shape
+    four = (4, n) + wq.shape
     act = (groups, rows, GW)
     return pl.pallas_call(
         front_body,
-        in_specs=[pl.BlockSpec(memory_space=pltpu.SMEM)] + [vm] * 7,
+        in_specs=[vm] * 3 + [hbm] * 4 + [vm] * 3,
         out_specs=[hbm] * 3 + [vm] + [hbm] * 5 + [vm] * 2,
-        out_shape=[sd(whole(stack), BF), sd(whole(wis), BF), sd(whole(wus), BF), sd((16, d), F32),
+        out_shape=[sd(four, BF), sd(whole(wis), BF), sd(whole(wus), BF), sd((16, d), F32),
                    sd(act, BF), sd(act, BF), sd(act, BF), sd(maps, BF), sd(act, BF),
                    sd((rows, d), F32), sd((16, 128), F32)],
-        scratch_shapes=[pltpu.VMEM(whole(stack), BF), pltpu.VMEM(whole(vpart), BF),
+        scratch_shapes=[pltpu.VMEM(four, BF), pltpu.VMEM(whole(vpart), F32),
                         pltpu.VMEM((rows // SEQ, SEQ, SEQ), F32), pltpu.VMEM((2, SEQ, SEQ), F32),
                         pltpu.VMEM(act, BF), pltpu.VMEM(act, BF), pltpu.VMEM(act, BF),
                         pltpu.VMEM(maps, BF), pltpu.VMEM(act, BF),
                         pltpu.SemaphoreType.DMA((4, 32)), pltpu.SemaphoreType.DMA((4, 32)),
-                        pltpu.SemaphoreType.DMA((4,)), pltpu.SemaphoreType.DMA((6,))],
+                        pltpu.SemaphoreType.DMA((7,)), pltpu.SemaphoreType.DMA((6,))],
         compiler_params=pltpu.CompilerParams(collective_id=0, has_side_effects=True, vmem_limit_bytes=VMEM_MAX),
         name="front",
-    )(rb, x, segr, segc, stack, vpart, wis, wus)
+    )(rb, x, seg, wq, wk, wv, wo, vpart, wis, wus)
 
 
 class Scatter:
@@ -894,7 +929,7 @@
 
     @pl.when(g == 0)
     def _():
-        same_document(segr, segc, bias)
+        same_document(lambda s: segr[s:s + 1, :], lambda s, c: segc[s * SEQ + c * BLOCK:s * SEQ + (c + 1) * BLOCK, :], bias)
         hm[...] = jnp.full(hm.shape, LOW, F32)
         z[...] = x[...].astype(F32) + vecs[OB:OB + 1, :]
 
@@ -905,7 +940,7 @@
     v[...] = (dot(xv, wv[...]) + vecs[VB:VB + 1, cols]).astype(BF)
 
     def one_pair(it, _):
-        pair_forward(g, it, rb, q, k, v, p, c, hm, bias, s_s)
+        pair_forward(g, it, lambda h, i: rb[h * 18 + i * 3] + rb[h * 18 + i * 3 + 1] + rb[h * 18 + i * 3 + 2], q, k, v, p, c, hm, bias, s_s)
         return 0
 
     lax.fori_loop(0, x.shape[0] // SEQ * (GW // 128), one_pair, 0)
@@ -985,12 +1020,14 @@
     )(x, db, wall, wall, wall, wall, q, k, v, p, c, dsum)
 
 
-def far_layer(n, rb, tokens, segr, segc, cot, stack, vec_part, inner_weight, outer_weight):
+def far_layer(me, n, random_blocks, tokens, segment_ids, cot, weights, vecs, inner_weight, inner_bias, outer_weight, limit):
     d, ff = tokens.shape[1], inner_weight.shape[1]
-    wall = lax.all_gather(stack, "dp", axis=1, tiled=True)
+    heads, part, wide = random_blocks.shape[0], vecs[0].shape[0], inner_bias.shape[0]
+    wall = lax.all_gather(jnp.stack(weights), "dp", axis=1, tiled=True)
     wi, wu = (lax.all_gather(a, "dp", axis=0, tiled=True) for a in (inner_weight, outer_weight))
-    vecs = lax.psum(vec_part.astype(F32), "dp")
-    q, k, v, p, c, z, hm = attn_fwd(rb, tokens, segr, segc, wall, vecs)
+    vecs = lax.psum(vectors_part(me, n, vecs, inner_bias).astype(F32), "dp")
+    q, k, v, p, c, z, hm = attn_fwd(random_blocks.reshape(-1), tokens, segment_ids.reshape(-1, SEQ),
+                                    segment_ids.reshape(-1, 1), wall, vecs)
     out, dsum, db, dwi, dwu, small = ffn(z, cot, wi, wu, vecs, F32)
     dwall, dqb, dvb, dx = attn_bwd(tokens, db, wall, q, k, v, p, c, dsum, F32)
     mine = small.at[QB:QB + 1].set(dqb).at[VB:VB + 1].set(dvb).at[TOP, :hm.shape[0]].set(hm[:, 0])
@@ -998,16 +1035,82 @@
     dwu, dwi, dwall = scatter(dwu, 0), scatter(dwi, 0), scatter(dwall, 1)
     row = lax.broadcasted_iota(jnp.int32, mine.shape, 0)
     total = jnp.where(row == TOP, lax.pmax(mine, "dp"), lax.psum(mine, "dp"))
-    return out, dx, dwall[0], dwall[1], dwall[2], dwall[3], dwi, dwu, total
-
-
-def near_layer(n, rb, tokens, segr, segc, cot, stack, vec_part, inner_weight, outer_weight):
+    vec8 = lax.dynamic_slice(total, (0, me * part), (8, part))
+    dbi = lax.dynamic_slice(total[BI:BI + ff // d].reshape(-1), (me * wide,), (wide,))
+    head_maxima = total[TOP, :heads]
+    factor = jnp.sqrt(jnp.minimum(1.0, limit[0].astype(F32) / jnp.maximum(head_maxima, 1.0)))
+    columns = jnp.repeat(factor, HD)[None, :]
+    cq, ck = ((w.astype(F32) * columns).astype(BF) for w in weights[:2])
+    return out, dx, dwall[0], dwall[1], dwall[2], dwall[3], dwi, dwu, [vec8[i] for i in range(8)], dbi, cq, ck, head_maxima
+
+
+def near_layer(me, n, random_blocks, tokens, segment_ids, cot, weights, vecs, inner_weight, inner_bias, outer_weight, limit):
     d, ff = tokens.shape[1], inner_weight.shape[1]
-    wall, wi, wu, vecs, q, k, v, p, c, z, hm = front(rb, tokens, segr, segc, stack, vec_part, inner_weight,
-                                                     outer_weight, n)
-    out, dx, dwq, dwk, dwv, dwo, dwi, dwu, total = rear(
-        n, z, cot, wi.reshape(d, ff), wu.reshape(ff, d), tokens, wall.reshape(4, d, d), q, k, v, c, p, vecs, hm)
-    return out, dx, dwq, dwk, dwv, dwo, dwi, dwu, total
+    heads, part, wide = random_blocks.shape[0], vecs[0].shape[0], inner_bias.shape[0]
+    pieces = jnp.concatenate([jnp.pad(jnp.stack(vecs), ((0, 0), (0, 128 - part))),
+                              jnp.pad(inner_bias[None, :], ((0, 7), (0, 128 - wide)))]).astype(F32)
+    wall, wi, wu, vec, q, k, v, p, c, z, hm = front(random_blocks, tokens, segment_ids.reshape(-1, 128), *weights, pieces,
+                                                    inner_weight, outer_weight, n)
+    raw = rear(n, z, cot, wi.reshape(d, ff), wu.reshape(ff, d), tokens, wall.reshape(4, d, d), q, k, v, c, p, vec, hm)
+    out, dx, dwq, dwk, dwv, dwo, dwi, dwu, cq, ck, *fins = finish(n, heads, limit, weights[0], weights[1], *raw)
+    fins = [a.reshape(-1) for a in fins]
+    return out, dx, dwq, dwk, dwv, dwo, dwi, dwu, fins[:8], fins[8], cq, ck, fins[9]
+
+
+def finish_body(n, heads, limit, wq, wk, total, *refs):
+    count = 8
+    srcs, dsts, refs = refs[:count], refs[count:2 * count], refs[2 * count:]
+    (cq, ck), fins, held, sems = refs[:2], refs[2:12], refs[12:-1], refs[-1]
+    jobs = []
+    for src, dst, tmp in zip(srcs, dsts, held):
+        cut = 4 if src.shape[0] >= 512 else 1
+        step = src.shape[0] // cut
+        for i in range(cut):
+            at = pl.ds(i * step, step)
+            slot = len(jobs)
+            jobs.append((pltpu.make_async_copy(src.at[at], tmp.at[at], sems.at[0, slot]),
+                         pltpu.make_async_copy(tmp.at[at], dst.at[at], sems.at[1, slot])))
+    for get, _ in jobs:
+        get.start()
+    me = lax.axis_index("dp")
+    d = total.shape[1]
+    part, wide = d // n, held[7].shape[0]
+    top = total[TOP:TOP + 1, 0:128]
+    head = lax.broadcasted_iota(jnp.int32, (1, d), 1) // HD
+    columns = jnp.zeros((1, d), F32)
+    for h in range(heads):
+        columns = jnp.where(head == h, top[:, h:h + 1], columns)
+    factor = jnp.sqrt(jnp.minimum(1.0, limit[0].astype(F32) / jnp.maximum(columns, 1.0)))
+    cq[...] = (wq[...].astype(F32) * factor).astype(BF)
+    ck[...] = (wk[...].astype(F32) * factor).astype(BF)
+    mine = pltpu.roll(total[0:8, :], d - me * part, 1)
+    for i in range(8):
+        fins[i][...] = mine[i:i + 1, 0:part]
+    per = d // wide
+    inner = jnp.broadcast_to(total[pl.ds(BI + me // per, 1), :], (8, d))
+    fins[8][...] = pltpu.roll(inner, d - (me % per) * wide, 1)[0:1, 0:wide]
+    fins[9][...] = top[:, 0:heads]
+    for get, put in jobs:
+        get.wait()
+        put.start()
+    for _, put in jobs:
+        put.wait()
+
+
+def finish(n, heads, limit, wq, wk, *raw):
+    mats, total = raw[:8], raw[8]
+    vm, hbm = pl.BlockSpec(memory_space=pltpu.VMEM), pl.BlockSpec(memory_space=pl.ANY)
+    sd = jax.ShapeDtypeStruct
+    return pl.pallas_call(
+        partial(finish_body, n, heads),
+        in_specs=[pl.BlockSpec(memory_space=pltpu.SMEM)] + [vm] * 3 + [hbm] * 8,
+        out_specs=[hbm] * 8 + [vm] * 12,
+        out_shape=[sd(a.shape, a.dtype) for a in mats] + [sd(wq.shape, BF)] * 2 + [sd((1, mats[2].shape[0]), F32)] * 8
+        + [sd((1, mats[7].shape[0]), F32), sd((1, heads), F32)],
+        scratch_shapes=[pltpu.VMEM(a.shape, a.dtype) for a in mats] + [pltpu.SemaphoreType.DMA((2, 16))],
+        compiler_params=pltpu.CompilerParams(vmem_limit_bytes=VMEM_MAX),
+        name="finish",
+    )(limit, wq, wk, total, *mats)
 
 
 def vectors_part(me, n, vecs, inner_bias):
@@ -1025,26 +1128,14 @@
 def per_device(n, tokens, segment_ids, random_blocks, clip_limit, query_weight, query_bias, key_weight, value_weight,
                value_bias, output_weight, output_bias, attn_gain, attn_shift, inner_weight, inner_bias,
                outer_weight, outer_bias, final_gain, final_shift, out_cotangent):
-    heads = random_blocks.shape[0]
-    d, ff = tokens.shape[1], inner_weight.shape[1]
-    me = lax.axis_index("dp")
-    stack = jnp.stack([query_weight, key_weight, value_weight, output_weight])
-    names = (query_bias, value_bias, output_bias, attn_gain, attn_shift, outer_bias, final_gain, final_shift)
-    part, wide = query_bias.shape[0], inner_bias.shape[0]
-    rows = tokens.shape[0]
-    layer = near_layer if n == 32 and (rows, d, ff) == (2 * SEQ, 3 * GW, 6 * SEQ) else far_layer
-    out, dx, dwq, dwk, dwv, dwo, dwi, dwu, total = layer(
-        n, random_blocks.reshape(-1), tokens, segment_ids.reshape(-1, SEQ), segment_ids.reshape(-1, 1), out_cotangent,
-        stack, vectors_part(me, n, names, inner_bias), inner_weight, outer_weight)
-    vec8 = lax.dynamic_slice(total, (0, me * part), (8, part))
-    dqb, dvb, dob, dag, dash, dbo, dfg, dfs = (vec8[i] for i in range(8))
-    dbi = lax.dynamic_slice(total[BI:BI + ff // d].reshape(-1), (me * wide,), (wide,))
-    head_maxima = total[TOP, :heads]
-    limit = clip_limit[0].astype(F32)
-    factor = jnp.sqrt(jnp.minimum(1.0, limit / jnp.maximum(head_maxima, 1.0)))
-    columns = jnp.repeat(factor, HD)[None, :]
-    cq = (query_weight.astype(F32) * columns).astype(BF)
-    ck = (key_weight.astype(F32) * columns).astype(BF)
+    rows, d = tokens.shape
+    near = n == 32 and (rows, d, inner_weight.shape[1]) == (2 * SEQ, 3 * GW, 6 * SEQ)
+    weights = (query_weight, key_weight, value_weight, output_weight)
+    vecs = (query_bias, value_bias, output_bias, attn_gain, attn_shift, outer_bias, final_gain, final_shift)
+    out, dx, dwq, dwk, dwv, dwo, dwi, dwu, vec8, dbi, cq, ck, head_maxima = (near_layer if near else far_layer)(
+        lax.axis_index("dp"), n, random_blocks, tokens, segment_ids, out_cotangent, weights, vecs, inner_weight, inner_bias,
+        outer_weight, clip_limit)
+    dqb, dvb, dob, dag, dash, dbo, dfg, dfs = vec8
     return (out, dx, dwq, dqb, dwk, dwv, dvb, dwo, dob, dag, dash, dwi, dbi, dwu, dbo, dfg, dfs, cq, ck, head_maxima)
 
 

time: 237 us -> 222 us (0.937)
  local copies, waits for them, and re-layouts: 17.5 us -> 2.25 us
  Pallas kernels: 213 us -> 217 us
  other arithmetic: 4.81 us -> 1.26 us
    unnamed x23 -> x1, local copies, waits for them, and re-layouts: 9.28 us -> 1.45 us
    pallas_call x1 -> x2, Pallas kernels: 80.6 us -> 85 us  [the longest x1 78.4 us: front(): pl.pallas_call(front_body, in_specs=[vm] * 3 + [hbm] * 4 + [vm] * 3, out_...]
    reshape x4 -> x0, local copies, waits for them, and re-layouts: 3.72 us -> none  [the longest x1 1.71 us: per_device(): segment_ids.reshape(-1, 1)]
where the time goes in v5:
time: 222 us
  Pallas kernels  217 us (98%)
  local copies, waits for them, and re-layouts  2.25 us (1%)
    pallas_call x1, Pallas kernels, rear(): pl.pallas_call(rear_body, in_specs=[hbm] * 11 + [vm] * 2, out_specs=[hbm]...  132 us
    pallas_call x1, Pallas kernels, front(): pl.pallas_call(front_body, in_specs=[vm] * 3 + [hbm] * 4 + [vm] * 3, out_...  78.4 us
    pallas_call x1, Pallas kernels, finish(): pl.pallas_call(partial(finish_body, n, heads), in_specs=[pl.BlockSpec(mem...  6.54 us

profile of v5, /device:TPU:0, one launch (start us, length us, event | category | flops | bytes accessed | tf_op | source)
XLA Modules:
  0.0 222.1 jit_solution(3564072028301731882)
XLA Ops:
  0.7 1.5 copy.40.rb
  2.1 0.8 stack.35
  2.9 1.3 fusion.3.vpart
  4.2 78.4 %front.1 = (bf16[4,32,24,768]{3,2,1,0:T(8,128)(2,1)}, bf16[32,24,3072]{2,1,0:T(8,128)(2,1)}, bf16[32,96,768]{2,1,0:T(8,128)(2,1)}, f32[16,768]{1,0:T(8,128)}, bf...) custom-call(s32[12,6,3]{2,1,0:T(8,128)} %copy.40.rb, ...), custom_call_target="tpu_custom_call" | custom-call | tf_op jit(solution)/shard_map/front/pallas_call | solution.py:438
  82.6 132.1 %rear.1 = (bf16[1024,768]{1,0:T(8,128)(2,1)}, f32[1024,768]{1,0:T(8,128)}, f32[24,768]{1,0:T(8,128)}, f32[24,768]{1,0:T(8,128)}, f32[24,768]{1,0:T(8,128)}, /*in...) custom-call(f32[1024,768]{1,0:T(8,128)} %get-tuple-element.60.z_h, ...), custom_call_target="tpu_custom_call" | custom-call | tf_op jit(solution)/shard_map/rear/pallas_call | solution.py:909
  215.3 6.5 %finish.1 = (bf16[1024,768]{1,0:T(8,128)(2,1)}, f32[1024,768]{1,0:T(8,128)}, f32[24,768]{1,0:T(8,128)}, f32[24,768]{1,0:T(8,128)}, f32[24,768]{1,0:T(8,128)}, /*...) custom-call(s32[1]{0:T(128)S(6)} %copy.41.limit, ...), custom_call_target="tpu_custom_call" | custom-call | tf_op jit(solution)/shard_map/finish/pallas_call | solution.py:1104

commit v6 on v5

--- a/solution.py
+++ b/solution.py
@@ -475,14 +475,14 @@
         for b in (1, 0):
             for k in range(4):
                 held = unit_of(self.grad, me + a * d1 + b * d2 + zs[k])[...]
-                self.rp[a, b, k] = (held.astype(F32) + self.rp[a, b, k].astype(F32)).astype(BF)
+                self.rp[a, b, k] = held + self.rp[a, b, k]
             if a == 1:
                 self.remote(self.rp.at[1, b], self.r1.at[b], 2 + b, d1).start()
 
     def first(self, b):
         me, fc, d1, d2, zs = self.where
         self.remote(self.rp.at[1, b], self.r1.at[b], 2 + b, d1).wait_recv()
-        self.rp[0, b] = (self.rp[0, b].astype(F32) + self.r1[b].astype(F32)).astype(BF)
+        self.rp[0, b] = self.rp[0, b] + self.r1[b]
         if b == 1:
             self.remote(self.rp.at[0, 1], self.r2, 4, d2).start()
 
@@ -490,7 +490,7 @@
         me, fc, d1, d2, zs = self.where
         self.remote(self.rp.at[0, 1], self.r2, 4, d2).wait_recv()
         for k in (1, 2, 3):
-            self.rp[0, 0, k] = (self.rp[0, 0, k].astype(F32) + self.r2[k].astype(F32)).astype(BF)
+            self.rp[0, 0, k] = self.rp[0, 0, k] + self.r2[k]
             self.remote(self.rp.at[0, 0, k], self.rz.at[k - 1], 4 + k, zs[k]).start()
 
     def near(self):
@@ -532,7 +532,7 @@
         self.remote(self.rp.at[a], self.rp.at[a], a, fc).wait_recv()
         for b in (1, 0):
             held = self.grad[lax.rem(me, 8) + a * d1 + b * d2]
-            self.rp[a, b] = (held.astype(F32) + self.rp[a, b].astype(F32)).astype(BF)
+            self.rp[a, b] = held + self.rp[a, b]
             if a == 1:
                 self.remote(self.rp.at[1, b], self.r1.at[b], 2 + b, d1).start()
 
@@ -542,7 +542,7 @@
     def second(self):
         self.remote(self.rp.at[0, 1], self.r2, 4, self.where[3]).wait_recv()
         if self.k:
-            self.rp[0, 0] = (self.rp[0, 0].astype(F32) + self.r2[...].astype(F32)).astype(BF)
+            self.rp[0, 0] = self.rp[0, 0] + self.r2[...]
             self.along().start()
 
     def near(self):
@@ -605,8 +605,8 @@
 
 
 def rear_body(z_h, cot_h, wi_h, wu_h, x_h, wall_h, q_h, k_h, v_h, c_h, p_h, vecs, hm,
-              out_h, dx, o_q, o_k, o_v, o_o, o_i, o_u, vout,
-              wi, wu, ag, z, fl, do, db, gu, gi, gg, held, got, usems, nsems, sems, vsems, isem, osem, *bufs):
+              out_h, dx_h, o_q, o_k, o_v, o_o, o_i, o_u, vout,
+              wi, wu, ag, z, dx, fl, do, db, gu, gi, gg, held, got, usems, nsems, sems, vsems, isem, osem, *bufs):
     where = place()
     zi = where[0] // 8
     rows, d = z.shape
@@ -646,6 +646,7 @@
     get_cot = pltpu.make_async_copy(cot_h, do, isem.at[9])
     get_x = pltpu.make_async_copy(x_h, do, isem.at[9])
     put_out = pltpu.make_async_copy(db, out_h, osem)
+    put_dx = pltpu.make_async_copy(dx, dx_h, osem)
     mid_cols = pl.ds(0, GW // HD * SEQ)
 
     def get_group(g, i):
@@ -673,27 +674,23 @@
 
     lax.fori_loop(0, rows // et, prep, 0)
 
-    def up(i, _):
-        j = i // (rows // rt)
-        r = pl.ds(pl.multiple_of((i % (rows // rt)) * rt, rt), rt)
+    def up(j, _):
         c = part(j)
-
-        @pl.when(i % (rows // rt) == 0)
-        def _():
-            get_up(j).wait()
-            get_down(j).wait()
-
-        u = dot(fl[r, :], wi[:, c]) + vecs[pl.ds(BI + j, 1), :]
-        u2 = u * u
-        t = jnp.tanh(u * (k0 + (k0 * k1) * u2))
-        h = 0.5 + 0.5 * t
-        a = (u * h).astype(BF)
-        act[r, c] = a
-        gp[r, c] = (h + (0.5 * u) * (1.0 - t * t) * (k0 + (3.0 * k0 * k1) * u2)).astype(BF)
-        dx[r, :] += dot(a, wu[c, :])
-        return 0
-
-    lax.fori_loop(0, (ff // d) * (rows // rt), up, 0)
+        get_up(j).wait()
+        get_down(j).wait()
+        for i in range(rows // rt):
+            r = slice(i * rt, (i + 1) * rt)
+            u = dot(fl[r, :], wi[:, c]) + vecs[pl.ds(BI + j, 1), :]
+            u2 = u * u
+            t = jnp.tanh(u * (k0 + (k0 * k1) * u2))
+            h = 0.5 + 0.5 * t
+            a = (u * h).astype(BF)
+            act[r, c] = a
+            gp[r, c] = (h + (0.5 * u) * (1.0 - t * t) * (k0 + (3.0 * k0 * k1) * u2)).astype(BF)
+            dx[r, :] += dot(a, wu[c, :])
+        return 0
+
+    lax.fori_loop(0, ff // d, up, 0)
     get_cot.wait()
 
     def mid(i, _):
@@ -794,7 +791,7 @@
 
     steps = (rows // SEQ) * (GW // 128)
     edge = GW // HD * SEQ
-    dc, dq, dk, dv = (act.at[:, pl.ds(edge + i * GW, GW)] for i in range(4))
+    dc = act.at[:, pl.ds(edge, GW)]
     dp_s = [z.at[pl.ds(j * SEQ, SEQ), pl.ds(0, SEQ)] for j in range(2)]
     ds_s = [gp.at[pl.ds(j * SEQ, SEQ), pl.ds(edge, SEQ)] for j in range(2)]
     both = lambda f: [(f.first, 1), (f.first, 0)]
@@ -828,7 +825,7 @@
         heads = [wu.at[pl.ds(i * rows, rows), cols] for i in range(3)]
 
         def one_pair(it, _):
-            pair_backward(it, *heads, ag.at[lax.rem(g, 2)], dc, dq, dk, dv, dp_s, ds_s)
+            pair_backward(it, *heads, ag.at[lax.rem(g, 2)], dc, *heads, dp_s, ds_s)
             for when, todo in events.items():
                 @pl.when(g * steps + it == when)
                 def _():
@@ -837,40 +834,50 @@
             return 0
 
         lax.fori_loop(0, steps, one_pair, 0)
-        small[QB:QB + 1, cols] = col_sum(dq[...].astype(F32))
-        small[VB:VB + 1, cols] = col_sum(dv[...].astype(F32))
 
         @pl.when(g == 0)
         def _():
             get_x.wait()
-            for i in range(3):
-                get_wall(i).wait()
 
         xv = do[...]
-        for i, grad in enumerate((dq, dk, dv)):
+        for i, grad in enumerate(heads):
             gg[g, i] = dot_tn(xv, grad[...]).reshape(n, d // n, GW).astype(BF)
         for i in range(groups):
             @pl.when(g == i)
             def _():
                 group_flow[i].begin()
-        weight = lambda i: wi[:, pl.ds(pl.multiple_of(i * d + g * GW, GW), GW)]
-        dx[...] += dot_nt(dq[...], weight(0)) + dot_nt(dk[...], weight(1)) + dot_nt(dv[...], weight(2))
+        small[QB:QB + 1, cols] = col_sum(heads[0][...].astype(F32))
+        small[VB:VB + 1, cols] = col_sum(heads[2][...].astype(F32))
         return 0
 
     lax.fori_loop(0, groups, group, 0)
     diag = lax.broadcasted_iota(jnp.int32, hm.shape, 0) == lax.broadcasted_iota(jnp.int32, hm.shape, 1)
     small[TOP:TOP + 1, 0:128] = jnp.sum(jnp.where(diag, hm[...], 0.0), axis=0, keepdims=True)
     small_flow.step(0)
+    for i in range(3):
+        get_wall(i).wait()
+    quarter = rows // 4
+
+    def inputs_part(t):
+        grads = (wu[i * rows + t * quarter:i * rows + (t + 1) * quarter, :] for i in range(3))
+        dx[t * quarter:(t + 1) * quarter, :] += sum(dot_nt(v, wi[:, i * d:(i + 1) * d]) for i, v in enumerate(grads))
+
+    inputs_part(0)
     g2.pair(1)
     g2.pair(0)
     small_flow.step(1)
+    inputs_part(1)
     g1.first(0)
+    inputs_part(2)
+    small_flow.step(2)
     g2.first(1)
-    small_flow.step(2)
     g1.second()
     g2.first(0)
+    inputs_part(3)
+    put_dx.start()
     small_flow.step(3)
     o_u[...] = up_flow(3).near() + up_flow(0).far() + up_flow(1).far() + up_flow(2).far()
+    g2.second()
     for it in range(4):
         k = (it + 1) % 4
         total = in_flow(it).near()
@@ -878,12 +885,12 @@
             total = total + in_flow(((k ^ m) - 1) % 4).far(m)
         o_i[:, part(beside(k))] = total
     o_o[...] = out_flow.last()
-    g2.second()
     for g, f in enumerate(group_flow):
         t = f.last()
         for i, o in enumerate((o_q, o_k, o_v)):
             o[:, g * GW:(g + 1) * GW] = t[i]
     vout[...] = small_flow.last()
+    put_dx.wait()
     up_flow(2).core_sent()
     up_flow(3).core_sent()
     in_flow(3).core_sent()
@@ -909,11 +916,12 @@
     return pl.pallas_call(
         rear_body,
         in_specs=[hbm] * 11 + [vm] * 2,
-        out_specs=[hbm] + [vm] * 8,
+        out_specs=[hbm] * 2 + [vm] * 7,
         out_shape=[sd((rows, d), BF), sd((rows, d), F32)] + [sd((r, d), F32)] * 4
         + [sd((r, ff), F32), sd((ru, d), F32), sd((16, d), F32)],
         scratch_shapes=[pltpu.VMEM((d, ff), BF), pltpu.VMEM((ff, d), BF), pltpu.VMEM((2, rows, ff), BF),
-                        pltpu.VMEM((rows, d), F32), flat, flat, flat, pltpu.VMEM((2, 8, ru, d), BF),
+                        pltpu.VMEM((rows, d), F32), pltpu.VMEM((rows, d), F32), flat, flat, flat,
+                        pltpu.VMEM((2, 8, ru, d), BF),
                         pltpu.VMEM((2, n, r, d), BF), pltpu.VMEM((groups, 3, n, r, GW), BF),
                         pltpu.VMEM((4, 16, d), F32), pltpu.VMEM((6, 16, d), F32),
                         pltpu.SemaphoreType.DMA((4, 2, 8)), pltpu.SemaphoreType.DMA((4, 2, 8)),

time: 222 us -> 213 us (0.959)
  Pallas kernels: 217 us -> 208 us
    pallas_call x1, Pallas kernels: 132 us -> 123 us  [rear(): pl.pallas_call(rear_body, in_specs=[hbm] * 11 + [vm] * 2, out_specs=[hbm]...]
where the time goes in v6:
time: 213 us
  Pallas kernels  208 us (98%)
  local copies, waits for them, and re-layouts  2.25 us (1%)
    pallas_call x1, Pallas kernels, rear(): pl.pallas_call(rear_body, in_specs=[hbm] * 11 + [vm] * 2, out_specs=[hbm]...  123 us
    pallas_call x1, Pallas kernels, front(): pl.pallas_call(front_body, in_specs=[vm] * 3 + [hbm] * 4 + [vm] * 3, out_...  78.4 us
    pallas_call x1, Pallas kernels, finish(): pl.pallas_call(partial(finish_body, n, heads), in_specs=[pl.BlockSpec(mem...  6.54 us

profile of v6, /device:TPU:0, one launch (start us, length us, event | category | flops | bytes accessed | tf_op | source)
XLA Modules:
  0.0 212.6 jit_solution(1981292810725627106)
XLA Ops:
  0.7 1.5 copy.40.rb
  2.1 0.8 stack.35
  2.9 1.3 fusion.3.vpart
  4.2 78.4 %front.1 = (bf16[4,32,24,768]{3,2,1,0:T(8,128)(2,1)}, bf16[32,24,3072]{2,1,0:T(8,128)(2,1)}, bf16[32,96,768]{2,1,0:T(8,128)(2,1)}, f32[16,768]{1,0:T(8,128)}, bf...) custom-call(s32[12,6,3]{2,1,0:T(8,128)} %copy.40.rb, ...), custom_call_target="tpu_custom_call" | custom-call | tf_op jit(solution)/shard_map/front/pallas_call | solution.py:438
  82.6 122.6 %rear.1 = (bf16[1024,768]{1,0:T(8,128)(2,1)}, f32[1024,768]{1,0:T(8,128)}, f32[24,768]{1,0:T(8,128)}, f32[24,768]{1,0:T(8,128)}, f32[24,768]{1,0:T(8,128)}, /*in...) custom-call(f32[1024,768]{1,0:T(8,128)} %get-tuple-element.60.z_h, ...), custom_call_target="tpu_custom_call" | custom-call | tf_op jit(solution)/shard_map/rear/pallas_call | solution.py:916
  205.9 6.5 %finish.1 = (bf16[1024,768]{1,0:T(8,128)(2,1)}, f32[1024,768]{1,0:T(8,128)}, f32[24,768]{1,0:T(8,128)}, f32[24,768]{1,0:T(8,128)}, f32[24,768]{1,0:T(8,128)}, /*...) custom-call(s32[1]{0:T(128)S(6)} %copy.41.limit, ...), custom_call_target="tpu_custom_call" | custom-call | tf_op jit(solution)/shard_map/finish/pallas_call | solution.py:1112

commit v7 on v6

--- a/solution.py
+++ b/solution.py
@@ -606,7 +606,7 @@
 
 def rear_body(z_h, cot_h, wi_h, wu_h, x_h, wall_h, q_h, k_h, v_h, c_h, p_h, vecs, hm,
               out_h, dx_h, o_q, o_k, o_v, o_o, o_i, o_u, vout,
-              wi, wu, ag, z, dx, fl, do, db, gu, gi, gg, held, got, usems, nsems, sems, vsems, isem, osem, *bufs):
+              wi, wu, ag, ds_s, dil_s, z, dx, fl, do, db, gu, gi, gg, held, got, usems, nsems, sems, vsems, isem, osem, *bufs):
     where = place()
     zi = where[0] // 8
     rows, d = z.shape
@@ -727,7 +727,7 @@
             r = slice(i * rt, (i + 1) * rt)
             di = dot_nt(do[r, :], wu[c, :]) * gp[r, c].astype(F32)
             dil = di.astype(BF)
-            act[r, c] = dil
+            dil_s[r, :] = dil
             s = col_sum(dil.astype(F32))
             sums = s if sums is None else sums + s
             dx[r, :] += dot_nt(dil, wi[:, c])
@@ -744,7 +744,7 @@
         def _():
             in_flow(it - 2).core_sent()
 
-        gi[slot] = dot_tn(fl[...], act[:, c]).reshape(gi.shape[1:]).astype(BF)
+        gi[slot] = dot_tn(fl[...], dil_s[...]).reshape(gi.shape[1:]).astype(BF)
         in_flow(it).begin()
 
         @pl.when(it >= 2)
@@ -793,7 +793,7 @@
     edge = GW // HD * SEQ
     dc = act.at[:, pl.ds(edge, GW)]
     dp_s = [z.at[pl.ds(j * SEQ, SEQ), pl.ds(0, SEQ)] for j in range(2)]
-    ds_s = [gp.at[pl.ds(j * SEQ, SEQ), pl.ds(edge, SEQ)] for j in range(2)]
+    slopes = [ds_s.at[0], ds_s.at[1]]
     both = lambda f: [(f.first, 1), (f.first, 0)]
     g0, g1, g2 = group_flow
     events = {
@@ -825,7 +825,7 @@
         heads = [wu.at[pl.ds(i * rows, rows), cols] for i in range(3)]
 
         def one_pair(it, _):
-            pair_backward(it, *heads, ag.at[lax.rem(g, 2)], dc, *heads, dp_s, ds_s)
+            pair_backward(it, *heads, ag.at[lax.rem(g, 2)], dc, *heads, dp_s, slopes)
             for when, todo in events.items():
                 @pl.when(g * steps + it == when)
                 def _():
@@ -919,7 +919,7 @@
         out_specs=[hbm] * 2 + [vm] * 7,
         out_shape=[sd((rows, d), BF), sd((rows, d), F32)] + [sd((r, d), F32)] * 4
         + [sd((r, ff), F32), sd((ru, d), F32), sd((16, d), F32)],
-        scratch_shapes=[pltpu.VMEM((d, ff), BF), pltpu.VMEM((ff, d), BF), pltpu.VMEM((2, rows, ff), BF),
+        scratch_shapes=[pltpu.VMEM((d, ff), BF), pltpu.VMEM((ff, d), BF), pltpu.VMEM((2, rows, ff), BF), pltpu.VMEM((2, SEQ, SEQ), BF), flat,
                         pltpu.VMEM((rows, d), F32), pltpu.VMEM((rows, d), F32), flat, flat, flat,
                         pltpu.VMEM((2, 8, ru, d), BF),
                         pltpu.VMEM((2, n, r, d), BF), pltpu.VMEM((groups, 3, n, r, GW), BF),

time: 213 us -> 200 us (0.939)
  Pallas kernels: 208 us -> 194 us
    pallas_call x1, Pallas kernels: 123 us -> 109 us  [rear(): pl.pallas_call(rear_body, in_specs=[hbm] * 11 + [vm] * 2, out_specs=[hbm]...]
where the time goes in v7:
time: 200 us; the launch traced here: 199 us
  Pallas kernels  194 us (97%)
  local copies, waits for them, and re-layouts  2.25 us (1%)
    pallas_call x1, Pallas kernels, rear(): pl.pallas_call(rear_body, in_specs=[hbm] * 11 + [vm] * 2, out_specs=[hbm]...  109 us
    pallas_call x1, Pallas kernels, front(): pl.pallas_call(front_body, in_specs=[vm] * 3 + [hbm] * 4 + [vm] * 3, out_...  78.4 us
    pallas_call x1, Pallas kernels, finish(): pl.pallas_call(partial(finish_body, n, heads), in_specs=[pl.BlockSpec(mem...  6.54 us

profile of v7, /device:TPU:0, one launch (start us, length us, event | category | flops | bytes accessed | tf_op | source)
XLA Modules:
  0.0 199.4 jit_solution(4862059460343155029)
XLA Ops:
  0.7 1.5 copy.40.rb
  2.1 0.8 stack.35
  2.9 1.3 fusion.3.vpart
  4.2 78.4 %front.1 = (bf16[4,32,24,768]{3,2,1,0:T(8,128)(2,1)}, bf16[32,24,3072]{2,1,0:T(8,128)(2,1)}, bf16[32,96,768]{2,1,0:T(8,128)(2,1)}, f32[16,768]{1,0:T(8,128)}, bf...) custom-call(s32[12,6,3]{2,1,0:T(8,128)} %copy.40.rb, ...), custom_call_target="tpu_custom_call" | custom-call | tf_op jit(solution)/shard_map/front/pallas_call | solution.py:438
  82.6 109.4 %rear.1 = (bf16[1024,768]{1,0:T(8,128)(2,1)}, f32[1024,768]{1,0:T(8,128)}, f32[24,768]{1,0:T(8,128)}, f32[24,768]{1,0:T(8,128)}, f32[24,768]{1,0:T(8,128)}, /*in...) custom-call(f32[1024,768]{1,0:T(8,128)} %get-tuple-element.60.z_h, ...), custom_call_target="tpu_custom_call" | custom-call | tf_op jit(solution)/shard_map/rear/pallas_call | solution.py:916
  192.6 6.5 %finish.1 = (bf16[1024,768]{1,0:T(8,128)(2,1)}, f32[1024,768]{1,0:T(8,128)}, f32[24,768]{1,0:T(8,128)}, f32[24,768]{1,0:T(8,128)}, f32[24,768]{1,0:T(8,128)}, /*...) custom-call(s32[1]{0:T(128)S(6)} %copy.41.limit, ...), custom_call_target="tpu_custom_call" | custom-call | tf_op jit(solution)/shard_map/finish/pallas_call | solution.py:1112

commit v8 on v7

--- a/solution.py
+++ b/solution.py
@@ -1071,7 +1071,7 @@
     (cq, ck), fins, held, sems = refs[:2], refs[2:12], refs[12:-1], refs[-1]
     jobs = []
     for src, dst, tmp in zip(srcs, dsts, held):
-        cut = 4 if src.shape[0] >= 512 else 1
+        cut = 8 if src.shape[0] >= 512 else 1
         step = src.shape[0] // cut
         for i in range(cut):
             at = pl.ds(i * step, step)
@@ -1115,7 +1115,7 @@
         out_specs=[hbm] * 8 + [vm] * 12,
         out_shape=[sd(a.shape, a.dtype) for a in mats] + [sd(wq.shape, BF)] * 2 + [sd((1, mats[2].shape[0]), F32)] * 8
         + [sd((1, mats[7].shape[0]), F32), sd((1, heads), F32)],
-        scratch_shapes=[pltpu.VMEM(a.shape, a.dtype) for a in mats] + [pltpu.SemaphoreType.DMA((2, 16))],
+        scratch_shapes=[pltpu.VMEM(a.shape, a.dtype) for a in mats] + [pltpu.SemaphoreType.DMA((2, 24))],
         compiler_params=pltpu.CompilerParams(vmem_limit_bytes=VMEM_MAX),
         name="finish",
     )(limit, wq, wk, total, *mats)

time: 200 us -> 200 us (level)
  no operation moved by 1% of the time
where the time goes in v8:
time: 200 us; the launch traced here: 199 us
  Pallas kernels  194 us (97%)
  local copies, waits for them, and re-layouts  2.25 us (1%)
    pallas_call x1, Pallas kernels, rear(): pl.pallas_call(rear_body, in_specs=[hbm] * 11 + [vm] * 2, out_specs=[hbm]...  109 us
    pallas_call x1, Pallas kernels, front(): pl.pallas_call(front_body, in_specs=[vm] * 3 + [hbm] * 4 + [vm] * 3, out_...  78.4 us
    pallas_call x1, Pallas kernels, finish(): pl.pallas_call(partial(finish_body, n, heads), in_specs=[pl.BlockSpec(mem...  6.66 us

profile of v8, /device:TPU:0, one launch (start us, length us, event | category | flops | bytes accessed | tf_op | source)
XLA Modules:
  0.0 199.5 jit_solution(14989944488819462643)
XLA Ops:
  0.7 1.5 copy.40.rb
  2.1 0.8 stack.35
  2.9 1.3 fusion.3.vpart
  4.2 78.4 %front.1 = (bf16[4,32,24,768]{3,2,1,0:T(8,128)(2,1)}, bf16[32,24,3072]{2,1,0:T(8,128)(2,1)}, bf16[32,96,768]{2,1,0:T(8,128)(2,1)}, f32[16,768]{1,0:T(8,128)}, bf...) custom-call(s32[12,6,3]{2,1,0:T(8,128)} %copy.40.rb, ...), custom_call_target="tpu_custom_call" | custom-call | tf_op jit(solution)/shard_map/front/pallas_call | solution.py:438
  82.6 109.4 %rear.1 = (bf16[1024,768]{1,0:T(8,128)(2,1)}, f32[1024,768]{1,0:T(8,128)}, f32[24,768]{1,0:T(8,128)}, f32[24,768]{1,0:T(8,128)}, f32[24,768]{1,0:T(8,128)}, /*in...) custom-call(f32[1024,768]{1,0:T(8,128)} %get-tuple-element.60.z_h, ...), custom_call_target="tpu_custom_call" | custom-call | tf_op jit(solution)/shard_map/rear/pallas_call | solution.py:916
  192.6 6.7 %finish.1 = (bf16[1024,768]{1,0:T(8,128)(2,1)}, f32[1024,768]{1,0:T(8,128)}, f32[24,768]{1,0:T(8,128)}, f32[24,768]{1,0:T(8,128)}, f32[24,768]{1,0:T(8,128)}, /*...) custom-call(s32[1]{0:T(128)S(6)} %copy.41.limit, ...), custom_call_target="tpu_custom_call" | custom-call | tf_op jit(solution)/shard_map/finish/pallas_call | solution.py:1112
